TPU v7x, 32 devices: a whole 2x2x4 slice. The times are simulated.
32 devices in a mesh: ctx: 32 (over z, y, x, core).
Axes of the slice: x: 2, y: 2, z: 4, core: 2. Of those that a mesh axis runs over, the one named last changes fastest.
Arguments:
- block_input: bfloat16 [64, 4, 576, 800], P('ctx'), may hold values from -6 to 6
- cotangent: bfloat16 [64, 4, 576, 800], P('ctx'), may hold values from -6 to 6
- w_in: bfloat16 [320000], P('ctx'), may hold values from -0.21875 to 0.21875
- w_conv: bfloat16 [480000], P('ctx'), may hold values from -0.1875 to 0.1875
- w_out: bfloat16 [320000], P('ctx'), may hold values from -0.4375 to 0.4375
- wide_gain: float32 [800], replicated, may hold values from 0.25 to 1.75
- wide_bias: float32 [2, 800], replicated, may hold values from -2 to 2
- narrow_gain: float32 [2, 400], replicated, may hold values from 0.25 to 1.75
- narrow_bias: float32 [4, 400], replicated, may hold values from -2 to 2
- dealing: int32 [64], replicated, may hold values from 0 to 31, as said below
Outputs:
- block_output: bfloat16 [64, 4, 576, 800], P('ctx')
- input_grad: bfloat16 [64, 4, 576, 800], P('ctx')
- grad_w_in: float32 [320000], P('ctx')
- grad_w_conv: float32 [480000], P('ctx')
- grad_w_out: float32 [320000], P('ctx')
- grad_wide_gain: float32 [800], replicated
- grad_wide_bias: float32 [2, 800], replicated
- grad_narrow_gain: float32 [2, 400], replicated
- grad_narrow_bias: float32 [4, 400], replicated
Inputs may be any that keep to these rules, and one draw needn't show every extreme that they name: `dealing`: block b and block 63 - b sit on one device, the lower in its first slot. Block b + 1 lies on the device after that of block b along ctx, cyclically, for b < 31.
All inputs are finite; a program needn't handle non-finite values.
Results may differ from a plain program's by a relative error of at most 0.0065.
Values may be sent and summed in bfloat16 or wider, within the bound.
No kernel may reach another device: no remote copies, remote signals or barrier semaphores. Data moves between devices by JAX's collectives and lax.ppermute only.
A program may use at most 192 MiB of HBM per device.

v0:
```python
import functools
import math
import jax
import jax.numpy as jnp
from jax import lax
from jax.experimental import pallas as pl
from jax.experimental.pallas import tpu as pltpu
from jax.sharding import PartitionSpec as P

EPS = 1e-05
BF = jnp.bfloat16
F32 = jnp.float32
L = 128
R = 16
SHIFT = 16
WIDE = 256


def params(mb=52):
    return pltpu.CompilerParams(dimension_semantics=("arbitrary",), vmem_limit_bytes=mb * 1024 * 1024)


def cost(flops, nbytes, trans=0):
    return pl.CostEstimate(flops=int(flops), bytes_accessed=int(nbytes), transcendentals=int(trans))


def rows_at(i):
    return pl.ds(pl.multiple_of(i * R, R), R)


def loop(n, body, init, unroll=25):
    return lax.fori_loop(0, n, body, init, unroll=min(n, unroll))


def fold(v):
    return v[:8] + v[8:]


def total8(v):
    return jnp.sum(v, axis=0, keepdims=True)


def nt(a, b):
    return lax.dot_general(a, b, (((1,), (1,)), ((), ())), preferred_element_type=F32)


def nn(a, b):
    return jnp.dot(a, b, preferred_element_type=F32)


def chunks(N, width):
    return [slice(l, min(N, l + width)) for l in range(0, N, width)]


def spread(table, rows, w):
    return jnp.concatenate([table[rows, :]] * (-(-w // L)), axis=1)[:, :w]


def fill_table(table, row):
    table[...] = jnp.broadcast_to(row, (L, row.shape[1])).T


def col_stats(read, chans, N, unroll=25):
    acc = loop(chans // R, lambda i, a: a + fold(read(i)), jnp.zeros((8, N), F32), unroll)
    mean = total8(acc) * (1.0 / chans)

    def second(i, a):
        cen = read(i) - mean
        return a + fold(cen * cen)

    acc = loop(chans // R, second, jnp.zeros((8, N), F32), unroll)
    return mean, lax.rsqrt(total8(acc) * (1.0 / chans) + EPS)


def gate(h):
    t = jnp.tanh(h)
    r = h + h * t
    return r, (1.0 + t) + (r - r * t)


def lane_sum(acc_ref, rows, v):
    N = v.shape[1]
    full = N // L * L
    tot = v[:, :L]
    for j in range(L, full, L):
        tot = tot + v[:, j:j + L]
    if full < N:
        tot = tot + jnp.concatenate([v[:, full:], jnp.zeros((v.shape[0], L - (N - full)), v.dtype)], axis=1)
    acc_ref[rows, :] += tot


def seq_spec(B, rows, N):
    return pl.BlockSpec((B, rows, N), lambda i: (i, 0, 0))


def fixed(shape):
    zero = (0,) * len(shape)
    return pl.BlockSpec(shape, lambda i: zero)


def smem():
    return pl.BlockSpec(memory_space=pltpu.SMEM)


def vmem():
    return pl.BlockSpec(memory_space=pltpu.VMEM)


def lane_total(acc):
    return jnp.sum(acc.T, axis=0, keepdims=True)


def unit_plan(n, M, C):
    size = M * C // n
    whole = math.gcd(size, C)
    q = max(d for d in range(1, WIDE + 1) if whole % d == 0)
    return q, C // q, size // q


def unit_slices(n, M, C):
    q, parts, units = unit_plan(n, M, C)
    out = []
    for p in range(n):
        for h in range(parts):
            lo = -((h - units * p) // parts)
            hi = -((h - units * (p + 1)) // parts)
            if hi > lo:
                out.append((p, h, lo, hi - lo, lo * parts + h - units * p))
    return out


def strided(start, size, step):
    return pl.ds(start, size, stride=step) if step > 1 else pl.ds(start, size)


def planes(q):
    return [(j, j * L, min(q - j * L, L)) for j in range(-(-q // L))]


def put_matrix(n, mat_ref, f32_ref, off):
    M, C = mat_ref.shape
    q, parts, _ = unit_plan(n, M, C)
    for p, h, lo, cnt, u in unit_slices(n, M, C):
        for j, at, w in planes(q):
            mat_ref[lo:lo + cnt, h * q + at:h * q + at + w] = f32_ref[p, j, strided(off + u, cnt, parts), :][:, :w]


def put_pieces(n, out_ref, mat_ref, M, C, off):
    q, parts, _ = unit_plan(n, M, C)
    for p, h, lo, cnt, u in unit_slices(n, M, C):
        for j, at, w in planes(q):
            v = mat_ref[lo:lo + cnt, h * q + at:h * q + at + w]
            if w < L:
                v = jnp.concatenate([v, jnp.zeros((cnt, L - w), v.dtype)], axis=1)
            out_ref[p, j, strided(off + u, cnt, parts), :] = v


def flipped(mat):
    C = mat.shape[1]
    eye = (lax.broadcasted_iota(jnp.int32, (C, C), 0) == lax.broadcasted_iota(jnp.int32, (C, C), 1)).astype(BF)
    return nt(eye, mat).astype(BF)


def ordered(n, slots_ref, g_ref, f32_ref):
    for p in range(n):
        f32_ref[p] = g_ref[slots_ref[p]].astype(F32)


def bias_block(row):
    v = jnp.broadcast_to(row, (L, row.shape[1])).T[:, :R]
    hi = v.astype(BF)
    rest = v - hi.astype(F32)
    mid = rest.astype(BF)
    low = (rest - mid.astype(F32)).astype(BF)
    col = lax.broadcasted_iota(jnp.int32, v.shape, 1)
    zero = jnp.zeros_like(v)
    return jnp.where(col == 0, hi.astype(F32), jnp.where(col == 1, mid.astype(F32), jnp.where(col == 2, low.astype(F32), zero))).astype(BF)


def unpack_in_kernel(n, slots_ref, g_ref, bias_ref, token_ref, w1_ref, w1t_ref, f32_ref, mat_ref):
    ordered(n, slots_ref, g_ref, f32_ref)
    put_matrix(n, mat_ref, f32_ref, 0)
    D, F = mat_ref.shape
    w1_ref[...] = mat_ref[...].astype(BF)
    w1t_ref[:, :D] = flipped(w1_ref[...])
    w1t_ref[:, D:] = bias_block(bias_ref[0:1, :])


def unpack_in(n, slots, g, bias, token, D, F):
    sd = jax.ShapeDtypeStruct
    return pl.pallas_call(
        functools.partial(unpack_in_kernel, n),
        in_specs=[smem(), vmem(), vmem(), pl.BlockSpec(memory_space=pl.ANY)], out_specs=[vmem(), vmem()],
        out_shape=[sd((D, F), BF), sd((F, D + R), BF)],
        scratch_shapes=[pltpu.VMEM(g.shape, F32), pltpu.VMEM((D, F), F32)],
        compiler_params=pltpu.CompilerParams(vmem_limit_bytes=40 * 1024 * 1024), name="unpack_in",
        cost_estimate=cost(1e9, 6e6),
    )(slots, g, bias, token)


def unpack_rest_kernel(n, slots_ref, g_ref, bias_ref, wide_ref, wc_ref, wct_ref, w3_ref, w3t_ref, f32_ref, matc_ref, mat3_ref):
    F, D = mat3_ref.shape
    ordered(n, slots_ref, g_ref, f32_ref)
    put_matrix(n, matc_ref, f32_ref, 0)
    put_matrix(n, mat3_ref, f32_ref, unit_plan(n, 3 * F, F)[2])
    for k in range(3):
        tap = matc_ref[k * F:(k + 1) * F, :].astype(BF)
        wc_ref[:, k * F:(k + 1) * F] = tap
        wct_ref[:, k * F:(k + 1) * F] = flipped(tap)
    wct_ref[:, 3 * F:] = bias_block(bias_ref[2:3, :])
    w3_ref[...] = mat3_ref[...].astype(BF)
    w3t_ref[:, :F] = flipped(w3_ref[...])
    w3t_ref[:, F:] = bias_block(wide_ref[1:2, :])


def unpack_rest(n, slots, g, bias, wide_bias, D, F):
    sd = jax.ShapeDtypeStruct
    return pl.pallas_call(
        functools.partial(unpack_rest_kernel, n),
        in_specs=[smem()] + [vmem()] * 3, out_specs=[vmem()] * 4,
        out_shape=[sd((F, 3 * F), BF), sd((F, 3 * F + R), BF), sd((F, D), BF), sd((D, F + R), BF)],
        scratch_shapes=[pltpu.VMEM(g.shape, F32), pltpu.VMEM((3 * F, F), F32), pltpu.VMEM((F, D), F32)],
        compiler_params=pltpu.CompilerParams(vmem_limit_bytes=40 * 1024 * 1024), name="unpack_rest",
        cost_estimate=cost(2e9, 14e6),
    )(slots, g, bias, wide_bias)


def rim_store(ref, i, steps, cols):
    for s in range(2 * steps):
        @pl.when(i == s)
        def _(s=s):
            w = cols[0].shape[1]
            for q, v in enumerate(cols):
                at = (s % steps * len(cols) + q) * w
                ref[s // steps, :, at:at + w] = v


def rim_load(buf, i, steps, first, second):
    w = buf.shape[1]
    for s in range(2 * steps):
        @pl.when(i == s)
        def _(s=s):
            src = first() if s < steps else second()
            buf[...] = src[:, s % steps * w:(s % steps + 1) * w]


def wide_fwd_kernel(Q, start, x_ref, gain_ref, bias_ref, *refs):
    r1_ref, n0_ref, s0_ref, rstd_ref, token_ref, gtab, btab, rbuf = refs[-8:]
    D, N = x_ref.shape[1:]
    i = pl.program_id(0)

    @pl.when(i == 0)
    def _():
        fill_table(gtab, gain_ref[...] * 0.5)
        fill_table(btab, bias_ref[0:1, :] * 0.5)
        token_ref[...] = jnp.zeros_like(token_ref)

    read = lambda j: x_ref[0, rows_at(j), :].astype(F32)
    mean, rstd = col_stats(read, D, N, 10)
    rstd_ref[0] = rstd

    def act(j, _):
        rows = rows_at(j)
        n = (read(j) - mean) * rstd
        r, d = gate(n * spread(gtab, rows, N) + spread(btab, rows, N))
        n0_ref[0, rows, :] = n.astype(BF)
        s0_ref[0, rows, :] = d.astype(BF)
        rbuf[rows, :] = r.astype(BF)
        return 0

    loop(D // R, act, 0, 10)
    for q in range(Q):
        @pl.when(lax.rem(start + i, Q) == q)
        def _(q=q):
            r1_ref[0, :D, q * N:(q + 1) * N] = rbuf[...]
            r1_ref[0, D:, q * N:(q + 1) * N] = jnp.ones((r1_ref.shape[1] - D, N), BF)


def wide_fwd(xT, gain, bias, Q, start=0, steps=None, into=None, token=None):
    S, D, N = xT.shape
    steps = S if steps is None else steps
    sd = jax.ShapeDtypeStruct
    at = lambda i: (start + i, 0, 0)
    into = tuple(into or ())
    token = () if token is None else (token,)
    one = lambda rows: pl.BlockSpec((1, rows, N), at)
    return pl.pallas_call(
        functools.partial(wide_fwd_kernel, Q, start), grid=(steps,),
        in_specs=[one(D), fixed((1, D)), fixed((2, D))] + [pl.BlockSpec(memory_space=pl.ANY)] * len(into + token),
        out_specs=[pl.BlockSpec((1, D + R, Q * N), lambda i: ((start + i) // Q, 0, 0)), one(D), one(D), one(1), fixed((8, L))],
        out_shape=[sd((S // Q, D + R, Q * N), BF), sd((S, D, N), BF), sd((S, D, N), BF), sd((S, 1, N), F32), sd((8, L), F32)],
        scratch_shapes=[pltpu.VMEM((D, L), F32)] * 2 + [pltpu.VMEM((D, N), BF)],
        input_output_aliases={3 + j: j for j in range(len(into))},
        compiler_params=params(), name="wide_fwd", cost_estimate=cost(1e9 * steps, 5.5e6 * steps),
    )(xT, gain, bias, *into, *token)


CH = 384


def front_kernel(Q, steps, r1_ref, w1t_ref, gain_ref, bias_ref, u_ref, n_ref, s_ref, rstd_ref, tail_ref, h_ref, gtab, btab):
    F, N = h_ref.shape
    T = N // Q
    i = pl.program_id(0)

    @pl.when(i == 0)
    def _():
        fill_table(gtab, gain_ref[0:1, :] * 0.5)
        fill_table(btab, bias_ref[1:2, :] * 0.5)

    h_ref[...] = nn(w1t_ref[...], r1_ref[0])
    for ls in chunks(N, CH):
        W = ls.stop - ls.start
        read = lambda j: h_ref[rows_at(j), ls]
        mean, rstd = col_stats(read, F, W)
        rstd_ref[0, :, ls] = rstd

        def act(j, _):
            rows = rows_at(j)
            n = (read(j) - mean) * rstd
            r, d = gate(n * spread(gtab, rows, W) + spread(btab, rows, W))
            u_ref[0, rows, ls] = r.astype(BF)
            n_ref[0, rows, ls] = n.astype(BF)
            s_ref[0, rows, ls] = d.astype(BF)
            return 0

        loop(F // R, act, 0)
    rim_store(tail_ref, i, steps, [u_ref[0, :, (q + 1) * T - 2 * SHIFT:(q + 1) * T] for q in range(Q)])


def front(r1, w1t, gain, bias, Q):
    G, DE, N = r1.shape
    F = w1t.shape[0]
    sd = jax.ShapeDtypeStruct
    rim = (2, F, G // 2 * Q * 2 * SHIFT)
    return pl.pallas_call(
        functools.partial(front_kernel, Q, G // 2), grid=(G,),
        in_specs=[seq_spec(1, DE, N), fixed(w1t.shape), fixed(gain.shape), fixed(bias.shape)],
        out_specs=[seq_spec(1, F, N)] * 3 + [seq_spec(1, 1, N), fixed(rim)],
        out_shape=[sd((G, F, N), BF)] * 3 + [sd((G, 1, N), F32), sd(rim, BF)],
        scratch_shapes=[pltpu.VMEM((F, N), F32)] + [pltpu.VMEM((F, L), F32)] * 2,
        compiler_params=params(), name="front", cost_estimate=cost(4e9, 19e6),
    )(r1, w1t, gain, bias)


def pull(F, W, ls, d_ref, n_at, s_at, rstd, gtab, gacc, bacc, e_ref, unroll=25):
    def first(j, carry):
        m1, m2 = carry
        rows = rows_at(j)
        ds = d_ref[rows, ls] * s_at(rows).astype(F32)
        dn = ds * n_at(rows).astype(F32)
        gain = spread(gtab, rows, W)
        t = ds * gain
        d_ref[rows, ls] = t
        lane_sum(bacc, rows, ds)
        lane_sum(gacc, rows, dn)
        return m1 + fold(t), m2 + fold(dn * gain)

    zero = jnp.zeros((8, W), F32)
    m1, m2 = loop(F // R, first, (zero, zero), unroll)
    m1, m2 = total8(m1) * (1.0 / F) * rstd, total8(m2) * (1.0 / F) * rstd

    def second(j, _):
        rows = rows_at(j)
        e_ref[0, rows, ls] = ((d_ref[rows, ls] * rstd - m1) - n_at(rows).astype(F32) * m2).astype(BF)
        return 0

    loop(F // R, second, 0, unroll)


def middle_kernel(n, Q, steps, flags_ref, u_ref, below_ref, above_ref, tail_ref, c_ref, x_ref, wct_ref, w3_ref, w3t_ref,
                  gain_ref, bias_ref, e_ref, out_ref, pieces_ref, small_ref, head_ref,
                  ubuf, cbuf, rbuf, h_ref, d_ref, n_ref, s_ref, o_ref, gacc, bacc, gwo_ref, gwc_ref, hbuf, gtab, btab):
    F, N = h_ref.shape
    T = N // Q
    D = c_ref.shape[1]
    i = pl.program_id(0)

    @pl.when(i == 0)
    def _():
        fill_table(gtab, gain_ref[1:2, :] * 0.5)
        fill_table(btab, bias_ref[3:4, :] * 0.5)
        ubuf[3 * F:, :] = jnp.ones((R, N), BF)
        rbuf[F:, :] = jnp.ones((R, N), BF)
        gwo_ref[...] = jnp.zeros_like(gwo_ref)
        gwc_ref[...] = jnp.zeros_like(gwc_ref)
        gacc[...] = jnp.zeros_like(gacc)
        bacc[...] = jnp.zeros_like(bacc)

    rim_load(hbuf, i, steps,
             lambda: jnp.where(flags_ref[0] == 1, jnp.zeros_like(below_ref[...]), below_ref[...]),
             lambda: jnp.where(flags_ref[1] == 1, tail_ref[0], above_ref[...]))
    ubuf[:F, :] = u_ref[0]
    for k in (1, 2):
        w = k * SHIFT
        parts = []
        for q in range(Q):
            parts += [hbuf[:, (q + 1) * 2 * SHIFT - w:(q + 1) * 2 * SHIFT], u_ref[0, :, q * T:(q + 1) * T - w]]
        ubuf[k * F:(k + 1) * F, :] = jnp.concatenate(parts, axis=1)
    for q in range(Q):
        cbuf[:, q * T:(q + 1) * T] = c_ref[q]
    h_ref[...] = nn(wct_ref[...], ubuf[...])
    d_ref[...] = nn(w3_ref[...], cbuf[...])
    rstds = []
    for ls in chunks(N, CH):
        W = ls.stop - ls.start
        read = lambda j: h_ref[rows_at(j), ls]
        mean, rstd = col_stats(read, F, W)
        rstds.append(rstd)

        def act(j, _):
            rows = rows_at(j)
            v = (read(j) - mean) * rstd
            r, d = gate(v * spread(gtab, rows, W) + spread(btab, rows, W))
            rbuf[rows, ls] = r.astype(BF)
            n_ref[rows, ls] = v
            s_ref[rows, ls] = d
            return 0

        loop(F // R, act, 0)
    for q in range(Q):
        o_ref[q] = nn(w3t_ref[...], rbuf[:, q * T:(q + 1) * T])
    gwo_ref[...] += nt(rbuf[...], cbuf[...])
    for ls, rstd in zip(chunks(N, CH), rstds):
        pull(F, ls.stop - ls.start, ls, d_ref, lambda rows: n_ref[rows, ls], lambda rows: s_ref[rows, ls], rstd, gtab, gacc, bacc, e_ref)
    gwc_ref[...] += nt(ubuf[...], e_ref[0])
    for q in range(Q):
        def emit(j, _):
            rows = rows_at(j)
            out_ref[q, rows, :] = (o_ref[q, rows, :] + x_ref[q, rows, :].astype(F32)).astype(BF)
            return 0

        loop(D // R, emit, 0, 25)
    rim_store(head_ref, i, steps, [e_ref[0, :, q * T:q * T + 2 * SHIFT] for q in range(Q)])

    @pl.when(i == pl.num_programs(0) - 1)
    def _():
        small_ref[...] = jnp.zeros_like(small_ref)
        small_ref[0:1, :F] = lane_total(gacc[...]) * 0.5
        small_ref[0:1, F:] = lane_total(bacc[...]) * 0.5
        small_ref[1:2, :F] = gwc_ref[3 * F:3 * F + 1, :]
        small_ref[2:3, :] = gwo_ref[F:F + 1, :]
        put_pieces(n, pieces_ref, gwc_ref, 3 * F, F, 0)
        put_pieces(n, pieces_ref, gwo_ref, F, D, unit_plan(n, 3 * F, F)[2])


def middle(n, Q, flags, uT, below, above, tails, cT, xT, wct, w3, w3t, gain, bias, rows):
    G, F, N = uT.shape
    S, D, T = cT.shape
    sd = jax.ShapeDtypeStruct
    return pl.pallas_call(
        functools.partial(middle_kernel, n, Q, G // 2), grid=(G,),
        in_specs=[smem(), seq_spec(1, F, N), fixed(below.shape), fixed(above.shape), fixed(tails.shape), seq_spec(Q, D, T), seq_spec(Q, D, T),
                  fixed(wct.shape), fixed(w3.shape), fixed(w3t.shape), fixed(gain.shape), fixed(bias.shape)],
        out_specs=[seq_spec(1, F, N), seq_spec(Q, D, T), fixed((n, WIDE // L, rows, L)), fixed((8, D)), fixed(tails.shape)],
        out_shape=[sd((G, F, N), BF), sd((S, D, T), BF), sd((n, WIDE // L, rows, L), F32), sd((8, D), F32), sd(tails.shape, BF)],
        scratch_shapes=[pltpu.VMEM((3 * F + R, N), BF), pltpu.VMEM((D, N), BF), pltpu.VMEM((F + R, N), BF), pltpu.VMEM((F, N), F32),
                        pltpu.VMEM((F, N), F32), pltpu.VMEM((F, N), F32), pltpu.VMEM((F, N), F32), pltpu.VMEM((Q, D, T), F32),
                        pltpu.VMEM((F, L), F32), pltpu.VMEM((F, L), F32), pltpu.VMEM((F + R, D), F32),
                        pltpu.VMEM((3 * F + R, F), F32), pltpu.VMEM((F, Q * 2 * SHIFT), BF), pltpu.VMEM((F, L), F32), pltpu.VMEM((F, L), F32)],
        compiler_params=params(), name="middle", cost_estimate=cost(18e9, 36e6),
    )(flags, uT, below, above, tails, cT, xT, wct, w3, w3t, gain, bias)


def back_kernel(n, Q, steps, flags_ref, e_ref, below_ref, above_ref, head_ref, n_ref, s_ref, rstd_ref, r1_ref, wc_ref, gain_ref,
                small_in, e1_ref, pieces_ref, small_ref, ebuf, d_ref, gacc, bacc, gwi_ref, hbuf, gtab, e1buf):
    F, N = d_ref.shape
    T = N // Q
    D = gwi_ref.shape[0] - R
    i = pl.program_id(0)

    @pl.when(i == 0)
    def _():
        fill_table(gtab, gain_ref[0:1, :] * 0.5)
        gwi_ref[...] = jnp.zeros_like(gwi_ref)
        gacc[...] = jnp.zeros_like(gacc)
        bacc[...] = jnp.zeros_like(bacc)

    rim_load(hbuf, i, steps,
             lambda: jnp.where(flags_ref[1] == 1, head_ref[1], above_ref[...]),
             lambda: jnp.where(flags_ref[0] == 1, jnp.zeros_like(below_ref[...]), below_ref[...]))
    ebuf[:F, :] = e_ref[0]
    for k in (1, 2):
        w = k * SHIFT
        parts = []
        for q in range(Q):
            parts += [e_ref[0, :, q * T + w:(q + 1) * T], hbuf[:, q * 2 * SHIFT:q * 2 * SHIFT + w]]
        ebuf[k * F:(k + 1) * F, :] = jnp.concatenate(parts, axis=1)
    d_ref[...] = nn(wc_ref[...], ebuf[...])
    for ls in chunks(N, CH):
        pull(F, ls.stop - ls.start, ls, d_ref, lambda rows: n_ref[0, rows, ls], lambda rows: s_ref[0, rows, ls], rstd_ref[0, :, ls],
             gtab, gacc, bacc, e1buf)
    gwi_ref[...] += nt(r1_ref[0], e1buf[0])
    for q in range(Q):
        e1_ref[q] = e1buf[0, :, q * T:(q + 1) * T]

    @pl.when(i == pl.num_programs(0) - 1)
    def _():
        small_ref[...] = small_in[...]
        small_ref[1:2, F:] = gwi_ref[D:D + 1, :]
        small_ref[3:4, :F] = lane_total(gacc[...]) * 0.5
        small_ref[3:4, F:] = lane_total(bacc[...]) * 0.5
        put_pieces(n, pieces_ref, gwi_ref, D, F, 0)


def back(n, Q, flags, eT, below, above, heads, n1, s1, rstd1, r1, wc, gain, small, rows):
    G, F, N = eT.shape
    DE = r1.shape[1]
    sd = jax.ShapeDtypeStruct
    return pl.pallas_call(
        functools.partial(back_kernel, n, Q, G // 2), grid=(G,),
        in_specs=[smem(), seq_spec(1, F, N), fixed(below.shape), fixed(above.shape), fixed(heads.shape), seq_spec(1, F, N), seq_spec(1, F, N),
                  seq_spec(1, 1, N), seq_spec(1, DE, N), fixed(wc.shape), fixed(gain.shape), fixed(small.shape)],
        out_specs=[seq_spec(Q, F, N // Q), fixed((n, WIDE // L, rows, L)), fixed(small.shape)],
        out_shape=[sd((G * Q, F, N // Q), BF), sd((n, WIDE // L, rows, L), F32), sd(small.shape, F32)],
        scratch_shapes=[pltpu.VMEM((3 * F, N), BF), pltpu.VMEM((F, N), F32), pltpu.VMEM((F, L), F32), pltpu.VMEM((F, L), F32),
                        pltpu.VMEM((DE, F), F32), pltpu.VMEM((F, Q * 2 * SHIFT), BF), pltpu.VMEM((F, L), F32),
                        pltpu.VMEM((1, F, N), BF)],
        compiler_params=params(), name="back", cost_estimate=cost(8e9, 25e6),
    )(flags, eT, below, above, heads, n1, s1, rstd1, r1, wc, gain, small)


def wide_bwd_kernel(Q, e_ref, w1_ref, n_ref, s_ref, rstd_ref, c_ref, gain_ref, small_in, *refs):
    dx_ref, small_ref, gtab, gacc, bacc = refs[-5 - Q:-Q]
    d_refs = refs[-Q:]
    D, N = d_refs[0].shape
    i = pl.program_id(0)

    @pl.when(i == 0)
    def _():
        fill_table(gtab, gain_ref[...] * 0.5)
        gacc[...] = jnp.zeros_like(gacc)
        bacc[...] = jnp.zeros_like(bacc)

    def dot(q):
        d_refs[q][...] = nn(w1_ref[...], e_ref[q])

    def pull_wide(q):
        d_ref = d_refs[q]

        def first(j, carry):
            m1, m2 = carry
            rows = rows_at(j)
            ds = d_ref[rows, :] * s_ref[q, rows, :].astype(F32)
            dn = ds * n_ref[q, rows, :].astype(F32)
            gain = spread(gtab, rows, N)
            t = ds * gain
            d_ref[rows, :] = t
            lane_sum(bacc, rows, ds)
            lane_sum(gacc, rows, dn)
            return m1 + fold(t), m2 + fold(dn * gain)

        zero = jnp.zeros((8, N), F32)
        m1, m2 = loop(D // R, first, (zero, zero), 50)
        rstd = rstd_ref[q]
        m1, m2 = total8(m1) * (1.0 / D) * rstd, total8(m2) * (1.0 / D) * rstd

        def second(j, _):
            rows = rows_at(j)
            g = (d_ref[rows, :] * rstd - m1) - n_ref[q, rows, :].astype(F32) * m2
            dx_ref[q, rows, :] = (g + c_ref[q, rows, :].astype(F32)).astype(BF)
            return 0

        loop(D // R, second, 0, 50)

    dot(0)
    for q in range(Q):
        if q + 1 < Q:
            dot(q + 1)
        pull_wide(q)

    @pl.when(i == pl.num_programs(0) - 1)
    def _():
        small_ref[...] = small_in[...]
        small_ref[4:5, :] = small_in[4:5, :] + lane_total(gacc[...]) * 0.5
        small_ref[5:6, :] = small_in[5:6, :] + lane_total(bacc[...]) * 0.5


def wide_bwd(Q, e1, w1, n0, s0, rstd0, cT, gain, small, start=0, steps=None, into=None):
    S, D, N = cT.shape
    F = e1.shape[1]
    steps = S // Q if steps is None else steps
    sd = jax.ShapeDtypeStruct
    at = lambda i: (start + i, 0, 0)
    into = () if into is None else (into,)
    part = lambda rows: pl.BlockSpec((Q, rows, N), at)
    return pl.pallas_call(
        functools.partial(wide_bwd_kernel, Q), grid=(steps,),
        in_specs=[part(F), fixed(w1.shape), part(D), part(D), part(1), part(D),
                  fixed(gain.shape), fixed(small.shape)] + [pl.BlockSpec(memory_space=pl.ANY)] * len(into),
        out_specs=[part(D), fixed(small.shape)],
        out_shape=[sd((S, D, N), BF), sd(small.shape, F32)],
        scratch_shapes=[pltpu.VMEM((D, L), F32)] * 3 + [pltpu.VMEM((D, N), F32)] * Q,
        input_output_aliases={8: 0} if into else {},
        compiler_params=params(), name="wide_bwd", cost_estimate=cost(2e9 * steps, 8.4e6 * steps),
    )(e1, w1, n0, s0, rstd0, cT, gain, small, *into)


def swap(v, bit, n):
    return lax.ppermute(v, "ctx", [(i, i ^ bit) for i in range(n)])


def bits_of(n):
    out, b = [], 1
    while b < n:
        out.append(b)
        b *= 2
    return out


def together(*values):
    return lax.optimization_barrier(values)


def slot_table(n, me):
    diff = jnp.arange(n, dtype=jnp.int32) ^ me
    return sum((jnp.where((diff & bit) != 0, n // 2 // bit, 0) for bit in bits_of(n)), jnp.zeros_like(diff))


def split_for(full, bit, me):
    pairs = full.reshape((-1, 2) + full.shape[1:])
    mine = jnp.where((me & bit) == 0, 0, 1)
    keep = lax.dynamic_index_in_dim(pairs, mine, 1, keepdims=False)
    return keep, lax.dynamic_index_in_dim(pairs, 1 - mine, 1, keepdims=False).astype(BF)


def sum_all(v, n):
    for bit in bits_of(n):
        v = v + swap(v, bit, n)
    return v


def to_units(flat, n, M, C, rows=None):
    q, parts, units = unit_plan(n, M, C)
    return jnp.pad(flat.reshape(units, q), ((0, 0), (0, WIDE - q))).reshape(units, WIDE // L, L).transpose(1, 0, 2)


def round_up(v, m=8):
    return -(-v // m) * m


def on_device(block_input, cotangent, w_in, w_conv, w_out, wide_gain, wide_bias, narrow_gain, narrow_bias, dealing):
    slots, seqs, T, D = block_input.shape
    F = narrow_gain.shape[1]
    n = lax.axis_size("ctx")
    half = dealing.shape[0] // 2
    me = lax.axis_index("ctx")
    pair = jnp.sum(jnp.where(dealing[:half] == me, jnp.arange(half, dtype=jnp.int32), 0))
    flags = jnp.stack([pair == 0, pair == half - 1]).astype(jnp.int32)
    up = [(i, (i + 1) % n) for i in range(n)]
    down = [((i + 1) % n, i) for i in range(n)]
    table = slot_table(n, me)
    units_in, units_conv, units_out = (unit_plan(n, m, c)[2] for m, c in ((D, F), (3 * F, F), (F, D)))
    rows_in, rows_rest = round_up(units_in), round_up(units_conv + units_out)

    xT = block_input.transpose(0, 1, 3, 2).reshape(slots * seqs, D, T)
    cT = cotangent.transpose(0, 1, 3, 2).reshape(slots * seqs, D, T)

    piece_in = jnp.pad(to_units(w_in, n, D, F), ((0, 0), (0, rows_in - units_in), (0, 0)))
    piece_rest = jnp.concatenate([to_units(w_conv, n, 3 * F, F), to_units(w_out, n, F, D)], axis=1)
    piece_rest = jnp.pad(piece_rest, ((0, 0), (0, rows_rest - piece_rest.shape[1]), (0, 0)))
    gain0 = wide_gain.reshape(1, D)
    bits = bits_of(n)
    Q = 2
    steps = slots * seqs // Q

    buf_in, buf_rest = piece_in[None], piece_rest[None]
    acts, gain, done, token = (), gain0, 0, None
    far = list(reversed(bits))
    for s, bit in enumerate(far):
        got_in = swap(buf_in, bit, n)
        if s < len(far) - 2:
            got_rest = swap(buf_rest, bit, n)
        count = (steps * (s + 1)) // (len(far) - 1) * Q - done if s < len(far) - 1 else 0
        if count:
            *acts, token = wide_fwd(xT, gain, wide_bias, Q, done, count, acts, token)
            done += count
        buf_in = jnp.concatenate([buf_in, got_in], axis=0)
        if s < len(far) - 2:
            buf_rest = jnp.concatenate([buf_rest, got_rest], axis=0)
        buf_in, buf_rest, token, gain = together(buf_in, buf_rest, token, gain)
    r1, n0, s0, rstd0 = acts
    got_rest = swap(buf_rest, far[-2], n)
    w1, w1t = unpack_in(n, table, buf_in, narrow_bias, token, D, F)
    uT, n1, s1, rstd1, tails = front(r1, w1t, narrow_gain, narrow_bias, Q)
    buf_rest, tails = together(jnp.concatenate([buf_rest, got_rest], axis=0), tails)
    below = lax.ppermute(tails[0], "ctx", up)
    above = lax.ppermute(tails[1], "ctx", down)
    buf_rest = jnp.concatenate([buf_rest, swap(buf_rest, far[-1], n)], axis=0)
    wc, wct, w3, w3t = unpack_rest(n, table, buf_rest, narrow_bias, wide_bias, D, F)
    eT, outT, rest, small, heads = middle(n, Q, flags, uT, below, above, tails, cT, xT, wct, w3, w3t,
                                          narrow_gain, narrow_bias, rows_rest)

    keep, send = split_for(rest, bits[0], me)
    got = swap(send, bits[0], n)
    above = lax.ppermute(heads[0], "ctx", down)
    below = lax.ppermute(heads[1], "ctx", up)
    rest = keep + got.astype(F32)
    keep, send = split_for(rest, bits[1], me)
    send, gain1 = together(send, narrow_gain)
    got = swap(send, bits[1], n)
    e1, into, small = back(n, Q, flags, eT, below, above, heads, n1, s1, rstd1, r1, wc, gain1, small, rows_in)
    rest, small = together(keep + got.astype(F32), small)

    dxT, gain, halves = None, gain0, 2
    for s in range(halves):
        keep_i, send_i = split_for(into, bits[s], me)
        keep_r, send_r = split_for(rest, bits[s + 2], me)
        send_r, send_i, gain = together(send_r, send_i, gain)
        got_r, got_i = swap(send_r, bits[s + 2], n), swap(send_i, bits[s], n)
        dxT, small = wide_bwd(Q, e1, w1, n0, s0, rstd0, cT, gain, small, s * steps // halves, steps // halves, dxT)
        rest, into, small = together(keep_r + got_r.astype(F32), keep_i + got_i.astype(F32), small)
    rest_bits, in_bits = bits[2 + halves:], bits[halves:]
    for j in range(len(bits)):
        got = swap(small, bits[j], n)
        if j < len(rest_bits):
            keep_r, send_r = split_for(rest, rest_bits[j], me)
            rest = keep_r + swap(send_r, rest_bits[j], n).astype(F32)
        if j < len(in_bits):
            keep_i, send_i = split_for(into, in_bits[j], me)
            into = keep_i + swap(send_i, in_bits[j], n).astype(F32)
        small = small + got
        if j < len(in_bits):
            small, rest, into = together(small, rest, into)
    own_rest, own_in = rest[0], into[0]

    def owned(own, at, M, C):
        q, parts, units = unit_plan(n, M, C)
        return own[:, at:at + units].transpose(1, 0, 2).reshape(units, WIDE)[:, :q].reshape(-1)

    back4 = lambda v: v.reshape(slots, seqs, D, T).transpose(0, 1, 3, 2)
    return (back4(outT), back4(dxT), owned(own_in, 0, D, F), owned(own_rest, 0, 3 * F, F), owned(own_rest, units_conv, F, D),
            small[4], jnp.stack([small[5], small[2]]), jnp.stack([small[3, :F], small[0, :F]]),
            jnp.stack([small[1, F:], small[3, F:], small[1, :F], small[0, F:]]))


def solution(mesh):
    whole, flat, copied = P("ctx", None, None, None), P("ctx"), P()
    return jax.shard_map(
        on_device, mesh=mesh,
        in_specs=(whole, whole, flat, flat, flat, copied, copied, copied, copied, copied),
        out_specs=(whole, whole, flat, flat, flat, copied, copied, copied, copied),
        check_vma=False,
    )
```

profile of v0, /device:TPU:0, one launch (start us, length us, event | category | flops | bytes accessed | tf_op | source)
XLA Modules:
  0.0 205.7 jit_solution(15419349045102290522)
XLA Ops:
  2.6 4.1 %collective-permute-start.1 = (bf16[1,2,128,128]{3,2,1,0:T(8,128)(2,1)S(1)}, bf16[1,2,128,128]{3,2,1,0:T(8,128)(2,1)S(1)}, u32[]{:S(2)}, u32[]{:S(2)}) collective-permute-start(bf16[1,2,128,128]{3,2,1,0:T(8,128)(2,1)S(1)} %fusion.10), channel_id=1, source_target_pairs={{0,16},{1,17},{2,18},{3,19},{4,20},{5,21},{6,22},{7,23},{8,24},{9,... | collective-permute-start | bytes 196616 | tf_op jit(solution)/shard_map/ppermute | solution.py:600
  9.1 7.1 %wide_fwd.4 = (bf16[4,816,1152]{2,1,0:T(8,128)(2,1)}, bf16[8,800,576]{2,1,0:T(8,128)(2,1)}, bf16[8,800,576]{2,1,0:T(8,128)(2,1)}, f32[8,1,576]{2,1,0:T(1,128)S(1)}, f32[8,128]{1,0:T(8,128)S(1)}) custom-call(bf16[8,800,576]{2,1,0:T(8,128)(2,1)} %bitcast.103, f32[1,800]{1,0:T(1,128)S(1)} %reshape.122.gain_ref, f32[2,800]{1,0:T(2,128)S(1)} %copy-done), custom_call_target="tpu_custom_call" | custom-call | flops 2000000000 | bytes 11000000 | tf_op jit(solution)/shard_map/wide_fwd/pallas_call | solution.py:287
  16.3 2.0 collective-permute-start.3
  18.4 7.1 %wide_fwd.5 = (bf16[4,816,1152]{2,1,0:T(8,128)(2,1)}, bf16[8,800,576]{2,1,0:T(8,128)(2,1)}, bf16[8,800,576]{2,1,0:T(8,128)(2,1)}, f32[8,1,576]{2,1,0:T(1,128)S(1)}, f32[8,128]{1,0:T(8,128)S(1)}) custom-call(bf16[8,800,576]{2,1,0:T(8,128)(2,1)} %bitcast.104, ...), custom_call_target="tpu_custom_call", output_to_operand_aliasing={{0}: (3, {}), {1}: (4, {}), {2}: (5, {}), {3}: (6, {})} | custom-call | flops 2000000000 | bytes 11000000 | tf_op jit(solution)/shard_map/wide_fwd/pallas_call | solution.py:287
  25.6 1.9 collective-permute-start.5
  27.7 7.1 %wide_fwd.6 = (bf16[4,816,1152]{2,1,0:T(8,128)(2,1)}, bf16[8,800,576]{2,1,0:T(8,128)(2,1)}, bf16[8,800,576]{2,1,0:T(8,128)(2,1)}, f32[8,1,576]{2,1,0:T(1,128)S(1)}, f32[8,128]{1,0:T(8,128)S(1)}) custom-call(bf16[8,800,576]{2,1,0:T(8,128)(2,1)} %bitcast.105, ...), custom_call_target="tpu_custom_call", output_to_operand_aliasing={{0}: (3, {}), {1}: (4, {}), {2}: (5, {}), {3}: (6, {})} | custom-call | flops 2000000000 | bytes 11000000 | tf_op jit(solution)/shard_map/wide_fwd/pallas_call | solution.py:287
  37.0 7.2 %wide_fwd.7 = (bf16[4,816,1152]{2,1,0:T(8,128)(2,1)}, bf16[8,800,576]{2,1,0:T(8,128)(2,1)}, bf16[8,800,576]{2,1,0:T(8,128)(2,1)}, f32[8,1,576]{2,1,0:T(1,128)S(1)}, f32[8,128]{1,0:T(8,128)S(1)}) custom-call(bf16[8,800,576]{2,1,0:T(8,128)(2,1)} %bitcast.106, ...), custom_call_target="tpu_custom_call", output_to_operand_aliasing={{0}: (3, {}), {1}: (4, {}), {2}: (5, {}), {3}: (6, {})} | custom-call | flops 2000000000 | bytes 11000000 | tf_op jit(solution)/shard_map/wide_fwd/pallas_call | solution.py:287
  44.3 1.8 collective-permute-done.7
  49.0 12.7 %front.1 = (bf16[4,400,1152]{2,1,0:T(8,128)(2,1)}, bf16[4,400,1152]{2,1,0:T(8,128)(2,1)}, bf16[4,400,1152]{2,1,0:T(8,128)(2,1)}, f32[4,1,1152]{2,1,0:T(1,128)S(1)}, bf16[2,400,128]{2,1,0:T(8,128)(2,1)S(1)}) custom-call(bf16[4,816,1152]{2,1,0:T(8,128)(2,1)} %get-tuple-element.122.r1_ref, bf16[400,816]{1,0:T(8,128)(2,1)S(1)} %get-tuple-element.131.w1t_ref, ...), custom_call_target="tpu_custom_call" | custom-call | flops 4000000000 | bytes 19000000 | tf_op jit(solution)/shard_map/front/pallas_call | solution.py:336
  63.3 5.7 %collective-permute-start.10 = (bf16[400,128]{1,0:T(8,128)(2,1)S(1)}, bf16[400,128]{1,0:T(8,128)(2,1)S(1)}, u32[]{:S(2)}, u32[]{:S(2)}) collective-permute-start(bf16[400,128]{1,0:T(8,128)(2,1)S(1)} %get-tuple-element.187), channel_id=1, source_target_pairs={{1,0},{2,1},{3,2},{4,3},{5,4},{6,5},{7,6},{8,7},{9,8},{10,9},{11,1... | collective-permute-start | bytes 307208 | tf_op jit(solution)/shard_map/ppermute | solution.py:688
  70.5 3.5 %unpack_rest.1 = (bf16[400,1200]{1,0:T(8,128)(2,1)S(1)}, bf16[400,1216]{1,0:T(8,128)(2,1)S(1)}, bf16[400,800]{1,0:T(8,128)(2,1)S(1)}, bf16[800,416]{1,0:T(8,128)(2,1)S(1)}) custom-call(s32[32]{0:T(128)S(1)} %get-tuple-element.199.slots_ref, bf16[32,2,128,128]{3,2,1,0:T(8,128)(2,1)S(1)} %pad_maximum_fusion.g_ref, f32[4,400]{1,0:T(4,128)S(1)} %copy-done.2, ...), custom_call_target="tpu_custom_call" | custom-call | flops 2000000000 | bytes 14000000 | tf_op jit(solution)/shard_map/unpack_rest/pallas_call | solution.py:218
  76.7 41.6 %middle.1 = (bf16[4,400,1152]{2,1,0:T(8,128)(2,1)}, bf16[8,800,576]{2,1,0:T(8,128)(2,1)}, f32[32,2,128,128]{3,2,1,0:T(8,128)}, f32[8,800]{1,0:T(8,128)S(1)}, bf16[2,400,128]{2,1,0:T(8,128)(2,1)S(1)}) custom-call(s32[2]{0:T(128)S(1)} %add_convert_fusion.flags_ref, bf16[4,400,1152]{2,1,0:T(8,128)(2,1)} %get-tuple-element.132.u_ref, ...), custom_call_target="tpu_custom_call" | custom-call | flops 17999998976 | bytes 36000000 | tf_op jit(solution)/shard_map/middle/pallas_call | solution.py:451
  120.8 4.9 %collective-permute-start.13 = (bf16[400,128]{1,0:T(8,128)(2,1)S(1)}, bf16[400,128]{1,0:T(8,128)(2,1)S(1)}, u32[]{:S(2)}, u32[]{:S(2)}) collective-permute-start(bf16[400,128]{1,0:T(8,128)(2,1)S(1)} %get-tuple-element.185), channel_id=1, source_target_pairs={{1,0},{2,1},{3,2},{4,3},{5,4},{6,5},{7,6},{8,7},{9,8},{10,9},{11,1... | collective-permute-start | bytes 307208 | tf_op jit(solution)/shard_map/ppermute | solution.py:696
  125.6 2.3 %bitcast_add_fusion = f32[16,2,128,128]{3,2,1,0:T(8,128)S(1)} fusion(bf16[16,2,128,128]{3,2,1,0:T(8,128)(2,1)} %collective-permute-done.14, f32[16,2,2,128,128]{4,3,2,1,0:T(8,128)} %bitcast.119, s32[]{:T(128)S(6)} %select_n.87), kind=kLoop, calls=%fused_computation.2 | loop fusion | flops 1048576 | bytes 5242884 | tf_op jit(solution)/shard_map/add | solution.py:698
  128.1 18.7 %back.1 = (bf16[8,400,576]{2,1,0:T(8,128)(2,1)}, f32[32,2,56,128]{3,2,1,0:T(8,128)}, f32[8,800]{1,0:T(8,128)S(1)}) custom-call(s32[2]{0:T(128)S(1)} %add_convert_fusion.flags_ref, bf16[4,400,1152]{2,1,0:T(8,128)(2,1)} %get-tuple-element.141.e_ref, bf16[400,128]{1,0:T(8,128)(2,1)S(1)} %collective-permute-done.12.below_ref, ...), custom_call_target="tpu_custom_call" | custom-call | flops 8000000000 | bytes 25000000 | tf_op jit(solution)/shard_map/back/pallas_call | solution.py:510
  148.4 11.7 %wide_bwd.2 = (bf16[8,800,576]{2,1,0:T(8,128)(2,1)}, f32[8,800]{1,0:T(8,128)S(1)}) custom-call(bf16[8,400,576]{2,1,0:T(8,128)(2,1)} %get-tuple-element.150.e_ref, bf16[800,400]{1,0:T(8,128)(2,1)S(1)} %get-tuple-element.151.w1_ref, bf16[8,800,576]{2,1,0:T(8,128)(2,1)} %get-tuple-element.152.n_ref, bf16[8,800,576]{2,1,0:T(8,128)(2,1)} %get-tuple-element.153.s_ref, ...), custom_call_target="tpu_custom_call" | custom-call | flops 4000000000 | bytes 16800000 | tf_op jit(solution)/shard_map/wide_bwd/pallas_call | solution.py:587
  160.4 2.1 collective-permute-start.19
  162.5 11.6 %wide_bwd.3 = (bf16[8,800,576]{2,1,0:T(8,128)(2,1)}, f32[8,800]{1,0:T(8,128)S(1)}) custom-call(bf16[8,400,576]{2,1,0:T(8,128)(2,1)} %get-tuple-element.150.e_ref, bf16[800,400]{1,0:T(8,128)(2,1)S(1)} %get-tuple-element.151.w1_ref, bf16[8,800,576]{2,1,0:T(8,128)(2,1)} %get-tuple-element.152.n_ref, ...), custom_call_target="tpu_custom_call", output_to_operand_aliasing={{0}: (8, {})} | custom-call | flops 4000000000 | bytes 16800000 | tf_op jit(solution)/shard_map/wide_bwd/pallas_call | solution.py:587
  174.2 5.1 %collective-permute-start.21 = (bf16[1,2,128,128]{3,2,1,0:T(8,128)(2,1)S(1)}, bf16[1,2,128,128]{3,2,1,0:T(8,128)(2,1)S(1)}, u32[]{:S(2)}, u32[]{:S(2)}) collective-permute-start(bf16[1,2,128,128]{3,2,1,0:T(8,128)(2,1)S(1)} %dynamic-slice_convert_fusion.5), channel_id=1, source_target_pairs={{0,16},{1,17},{2,18},{3,19},{4,20},{5,21},{6,22},{7,23},{8,24},{9,... | collective-permute-start | bytes 196616 | tf_op jit(solution)/shard_map/ppermute | solution.py:600
  182.0 3.0 %collective-permute-done.22 = bf16[4,2,56,128]{3,2,1,0:T(8,128)(2,1)S(1)} collective-permute-done((bf16[4,2,56,128]{3,2,1,0:T(8,128)(2,1)S(1)}, bf16[4,2,56,128]{3,2,1,0:T(8,128)(2,1)S(1)}, u32[]{:S(2)}, u32[]{:S(2)}) %collective-permute-start.22) | collective-permute-done | bytes 114720 | tf_op jit(solution)/shard_map/ppermute | solution.py:600
  185.3 3.8 %collective-permute-done.23 = f32[8,800]{1,0:T(8,128)S(1)} collective-permute-done((f32[8,800]{1,0:T(8,128)S(1)}, f32[8,800]{1,0:T(8,128)S(1)}, u32[]{:S(2)}, u32[]{:S(2)}) %collective-permute-start.23) | collective-permute-done | bytes 25632 | tf_op jit(solution)/shard_map/ppermute | solution.py:600
  191.0 2.4 %collective-permute-done.25 = f32[8,800]{1,0:T(8,128)S(1)} collective-permute-done((f32[8,800]{1,0:T(8,128)S(1)}, f32[8,800]{1,0:T(8,128)S(1)}, u32[]{:S(2)}, u32[]{:S(2)}) %collective-permute-start.25) | collective-permute-done | bytes 25632 | tf_op jit(solution)/shard_map/ppermute | solution.py:600
  194.2 1.8 collective-permute-start.27
  196.0 2.4 %collective-permute-done.27 = f32[8,800]{1,0:T(8,128)S(1)} collective-permute-done((f32[8,800]{1,0:T(8,128)S(1)}, f32[8,800]{1,0:T(8,128)S(1)}, u32[]{:S(2)}, u32[]{:S(2)}) %collective-permute-start.27) | collective-permute-done | bytes 25632 | tf_op jit(solution)/shard_map/ppermute | solution.py:600
  (139 shorter events, 31.5 us)
Async XLA Ops:
  2.6 13.7 %collective-permute-start.1 = (bf16[1,2,128,128]{3,2,1,0:T(8,128)(2,1)S(1)}, bf16[1,2,128,128]{3,2,1,0:T(8,128)(2,1)S(1)}, u32[]{:S(2)}, u32[]{:S(2)}) collective-permute-start(bf16[1,2,128,128]{3,2,1,0:T(8,128)(2,1)S(1)} %fusion.10), channel_id=1, source_target_pairs={{0,16},{1,17},{2,18},{3,19},{4,20},{5,21},{6,22},{7,23},{8,24},{9,... | collective-permute-start | bytes 196616 | tf_op jit(solution)/shard_map/ppermute | solution.py:600
  7.6 8.6 %collective-permute-start = (bf16[1,2,56,128]{3,2,1,0:T(8,128)(2,1)S(1)}, bf16[1,2,56,128]{3,2,1,0:T(8,128)(2,1)S(1)}, u32[]{:S(2)}, u32[]{:S(2)}) collective-permute-start(bf16[1,2,56,128]{3,2,1,0:T(8,128)(2,1)S(1)} %pad_bitcast_fusion), channel_id=1, source_target_pairs={{0,16},{1,17},{2,18},{3,19},{4,20},{5,21},{6,22},{7,23},{8,24},{9,... | collective-permute-start | bytes 86024 | tf_op jit(solution)/shard_map/ppermute | solution.py:600
  16.3 9.3 %collective-permute-start.3 = (bf16[2,2,128,128]{3,2,1,0:T(8,128)(2,1)S(1)}, bf16[2,2,128,128]{3,2,1,0:T(8,128)(2,1)S(1)}, u32[]{:S(2)}, u32[]{:S(2)}) collective-permute-start(bf16[2,2,128,128]{3,2,1,0:T(8,128)(2,1)S(1)} %pad_maximum_fusion.7), channel_id=1, source_target_pairs={{0,8},{1,9},{2,10},{3,11},{4,12},{5,13},{6,14},{7,15},{8,0},{9,1},... | collective-permute-start | bytes 393224 | tf_op jit(solution)/shard_map/ppermute | solution.py:600
  18.3 7.3 %collective-permute-start.2 = (bf16[2,2,56,128]{3,2,1,0:T(8,128)(2,1)S(1)}, bf16[2,2,56,128]{3,2,1,0:T(8,128)(2,1)S(1)}, u32[]{:S(2)}, u32[]{:S(2)}) collective-permute-start(bf16[2,2,56,128]{3,2,1,0:T(8,128)(2,1)S(1)} %pad_maximum_fusion.9), channel_id=1, source_target_pairs={{0,8},{1,9},{2,10},{3,11},{4,12},{5,13},{6,14},{7,15},{8,0},{9,1},... | collective-permute-start | bytes 172040 | tf_op jit(solution)/shard_map/ppermute | solution.py:600
  25.6 9.8 %collective-permute-start.5 = (bf16[4,2,128,128]{3,2,1,0:T(8,128)(2,1)S(1)}, bf16[4,2,128,128]{3,2,1,0:T(8,128)(2,1)S(1)}, u32[]{:S(2)}, u32[]{:S(2)}) collective-permute-start(bf16[4,2,128,128]{3,2,1,0:T(8,128)(2,1)S(1)} %pad_maximum_fusion.5), channel_id=1, source_target_pairs={{0,4},{1,5},{2,6},{3,7},{4,0},{5,1},{6,2},{7,3},{8,12},{9,13},{10,... | collective-permute-start | bytes 786440 | tf_op jit(solution)/shard_map/ppermute | solution.py:600
  27.5 7.8 %collective-permute-start.4 = (bf16[4,2,56,128]{3,2,1,0:T(8,128)(2,1)S(1)}, bf16[4,2,56,128]{3,2,1,0:T(8,128)(2,1)S(1)}, u32[]{:S(2)}, u32[]{:S(2)}) collective-permute-start(bf16[4,2,56,128]{3,2,1,0:T(8,128)(2,1)S(1)} %pad_maximum_fusion.8), channel_id=1, source_target_pairs={{0,4},{1,5},{2,6},{3,7},{4,0},{5,1},{6,2},{7,3},{8,12},{9,13},{10,... | collective-permute-start | bytes 344072 | tf_op jit(solution)/shard_map/ppermute | solution.py:600
  35.4 8.8 %collective-permute-start.6 = (bf16[8,2,56,128]{3,2,1,0:T(8,128)(2,1)S(1)}, bf16[8,2,56,128]{3,2,1,0:T(8,128)(2,1)S(1)}, u32[]{:S(2)}, u32[]{:S(2)}) collective-permute-start(bf16[8,2,56,128]{3,2,1,0:T(8,128)(2,1)S(1)} %pad_maximum_fusion.6), channel_id=1, source_target_pairs={{0,2},{1,3},{2,0},{3,1},{4,6},{5,7},{6,4},{7,5},{8,10},{9,11},{10,... | collective-permute-start | bytes 688136 | tf_op jit(solution)/shard_map/ppermute | solution.py:600
  46.2 15.5 %collective-permute-start.8 = (bf16[8,2,128,128]{3,2,1,0:T(8,128)(2,1)S(1)}, bf16[8,2,128,128]{3,2,1,0:T(8,128)(2,1)S(1)}, u32[]{:S(2)}, u32[]{:S(2)}) collective-permute-start(bf16[8,2,128,128]{3,2,1,0:T(8,128)(2,1)S(1)} %pad_maximum_fusion.3), channel_id=1, source_target_pairs={{0,2},{1,3},{2,0},{3,1},{4,6},{5,7},{6,4},{7,5},{8,10},{9,11},{10,... | collective-permute-start | bytes 1572872 | tf_op jit(solution)/shard_map/ppermute | solution.py:600
  61.9 7.2 %collective-permute-start.11 = (bf16[16,2,128,128]{3,2,1,0:T(8,128)(2,1)S(1)}, bf16[16,2,128,128]{3,2,1,0:T(8,128)(2,1)}, u32[]{:S(2)}, u32[]{:S(2)}) collective-permute-start(bf16[16,2,128,128]{3,2,1,0:T(8,128)(2,1)S(1)} %pad_maximum_fusion.1), channel_id=1, source_target_pairs={{0,1},{1,0},{2,3},{3,2},{4,5},{5,4},{6,7},{7,6},{8,9},{9,8},{10,11... | collective-permute-start | bytes 3145736 | tf_op jit(solution)/shard_map/ppermute | solution.py:600
  63.3 12.5 %collective-permute-start.10 = (bf16[400,128]{1,0:T(8,128)(2,1)S(1)}, bf16[400,128]{1,0:T(8,128)(2,1)S(1)}, u32[]{:S(2)}, u32[]{:S(2)}) collective-permute-start(bf16[400,128]{1,0:T(8,128)(2,1)S(1)} %get-tuple-element.187), channel_id=1, source_target_pairs={{1,0},{2,1},{3,2},{4,3},{5,4},{6,5},{7,6},{8,7},{9,8},{10,9},{11,1... | collective-permute-start | bytes 307208 | tf_op jit(solution)/shard_map/ppermute | solution.py:688
  69.0 7.7 %collective-permute-start.9 = (bf16[400,128]{1,0:T(8,128)(2,1)S(1)}, bf16[400,128]{1,0:T(8,128)(2,1)S(1)}, u32[]{:S(2)}, u32[]{:S(2)}) collective-permute-start(bf16[400,128]{1,0:T(8,128)(2,1)S(1)} %get-tuple-element.188), channel_id=1, source_target_pairs={{0,1},{1,2},{2,3},{3,4},{4,5},{5,6},{6,7},{7,8},{8,9},{9,10},{10,1... | collective-permute-start | bytes 307208 | tf_op jit(solution)/shard_map/ppermute | solution.py:687
  120.1 5.5 %collective-permute-start.14 = (bf16[16,2,128,128]{3,2,1,0:T(8,128)(2,1)S(1)}, bf16[16,2,128,128]{3,2,1,0:T(8,128)(2,1)}, u32[]{:S(2)}, u32[]{:S(2)}) collective-permute-start(bf16[16,2,128,128]{3,2,1,0:T(8,128)(2,1)S(1)} %fusion), channel_id=1, source_target_pairs={{0,1},{1,0},{2,3},{3,2},{4,5},{5,4},{6,7},{7,6},{8,9},{9,8},{10,11... | collective-permute-start | bytes 3145736 | tf_op jit(solution)/shard_map/ppermute | solution.py:600
  120.2 7.9 %collective-permute-start.12 = (bf16[400,128]{1,0:T(8,128)(2,1)S(1)}, bf16[400,128]{1,0:T(8,128)(2,1)S(1)}, u32[]{:S(2)}, u32[]{:S(2)}) collective-permute-start(bf16[400,128]{1,0:T(8,128)(2,1)S(1)} %get-tuple-element.186), channel_id=1, source_target_pairs={{0,1},{1,2},{2,3},{3,4},{4,5},{5,6},{6,7},{7,8},{8,9},{9,10},{10,1... | collective-permute-start | bytes 307208 | tf_op jit(solution)/shard_map/ppermute | solution.py:697
  120.8 7.3 %collective-permute-start.13 = (bf16[400,128]{1,0:T(8,128)(2,1)S(1)}, bf16[400,128]{1,0:T(8,128)(2,1)S(1)}, u32[]{:S(2)}, u32[]{:S(2)}) collective-permute-start(bf16[400,128]{1,0:T(8,128)(2,1)S(1)} %get-tuple-element.185), channel_id=1, source_target_pairs={{1,0},{2,1},{3,2},{4,3},{5,4},{6,5},{7,6},{8,7},{9,8},{10,9},{11,1... | collective-permute-start | bytes 307208 | tf_op jit(solution)/shard_map/ppermute | solution.py:696
  128.0 20.1 %collective-permute-start.15 = (bf16[8,2,128,128]{3,2,1,0:T(8,128)(2,1)S(1)}, bf16[8,2,128,128]{3,2,1,0:T(8,128)(2,1)S(1)}, u32[]{:S(2)}, u32[]{:S(2)}) collective-permute-start(bf16[8,2,128,128]{3,2,1,0:T(8,128)(2,1)S(1)} %fusion.1), channel_id=1, source_target_pairs={{0,2},{1,3},{2,0},{3,1},{4,6},{5,7},{6,4},{7,5},{8,10},{9,11},{10,... | collective-permute-start | bytes 1572872 | tf_op jit(solution)/shard_map/ppermute | solution.py:600
  148.2 12.0 %collective-permute-start.17 = (bf16[16,2,56,128]{3,2,1,0:T(8,128)(2,1)S(1)}, bf16[16,2,56,128]{3,2,1,0:T(8,128)(2,1)S(1)}, u32[]{:S(2)}, u32[]{:S(2)}) collective-permute-start(bf16[16,2,56,128]{3,2,1,0:T(8,128)(2,1)S(1)} %fusion.2), channel_id=1, source_target_pairs={{0,1},{1,0},{2,3},{3,2},{4,5},{5,4},{6,7},{7,6},{8,9},{9,8},{10,11... | collective-permute-start | bytes 1376264 | tf_op jit(solution)/shard_map/ppermute | solution.py:600
  148.3 11.8 %collective-permute-start.16 = (bf16[4,2,128,128]{3,2,1,0:T(8,128)(2,1)S(1)}, bf16[4,2,128,128]{3,2,1,0:T(8,128)(2,1)S(1)}, u32[]{:S(2)}, u32[]{:S(2)}) collective-permute-start(bf16[4,2,128,128]{3,2,1,0:T(8,128)(2,1)S(1)} %fusion.3), channel_id=1, source_target_pairs={{0,4},{1,5},{2,6},{3,7},{4,0},{5,1},{6,2},{7,3},{8,12},{9,13},{10,... | collective-permute-start | bytes 786440 | tf_op jit(solution)/shard_map/ppermute | solution.py:600
  160.4 13.7 %collective-permute-start.19 = (bf16[8,2,56,128]{3,2,1,0:T(8,128)(2,1)S(1)}, bf16[8,2,56,128]{3,2,1,0:T(8,128)(2,1)S(1)}, u32[]{:S(2)}, u32[]{:S(2)}) collective-permute-start(bf16[8,2,56,128]{3,2,1,0:T(8,128)(2,1)S(1)} %fusion.4), channel_id=1, source_target_pairs={{0,2},{1,3},{2,0},{3,1},{4,6},{5,7},{6,4},{7,5},{8,10},{9,11},{10,... | collective-permute-start | bytes 688136 | tf_op jit(solution)/shard_map/ppermute | solution.py:600
  162.5 11.6 %collective-permute-start.18 = (bf16[2,2,128,128]{3,2,1,0:T(8,128)(2,1)S(1)}, bf16[2,2,128,128]{3,2,1,0:T(8,128)(2,1)S(1)}, u32[]{:S(2)}, u32[]{:S(2)}) collective-permute-start(bf16[2,2,128,128]{3,2,1,0:T(8,128)(2,1)S(1)} %fusion.5), channel_id=1, source_target_pairs={{0,8},{1,9},{2,10},{3,11},{4,12},{5,13},{6,14},{7,15},{8,0},{9,1},... | collective-permute-start | bytes 393224 | tf_op jit(solution)/shard_map/ppermute | solution.py:600
  174.2 7.7 %collective-permute-start.21 = (bf16[1,2,128,128]{3,2,1,0:T(8,128)(2,1)S(1)}, bf16[1,2,128,128]{3,2,1,0:T(8,128)(2,1)S(1)}, u32[]{:S(2)}, u32[]{:S(2)}) collective-permute-start(bf16[1,2,128,128]{3,2,1,0:T(8,128)(2,1)S(1)} %dynamic-slice_convert_fusion.5), channel_id=1, source_target_pairs={{0,16},{1,17},{2,18},{3,19},{4,20},{5,21},{6,22},{7,23},{8,24},{9,... | collective-permute-start | bytes 196616 | tf_op jit(solution)/shard_map/ppermute | solution.py:600
  179.4 5.6 %collective-permute-start.22 = (bf16[4,2,56,128]{3,2,1,0:T(8,128)(2,1)S(1)}, bf16[4,2,56,128]{3,2,1,0:T(8,128)(2,1)S(1)}, u32[]{:S(2)}, u32[]{:S(2)}) collective-permute-start(bf16[4,2,56,128]{3,2,1,0:T(8,128)(2,1)S(1)} %fusion.8), channel_id=1, source_target_pairs={{0,4},{1,5},{2,6},{3,7},{4,0},{5,1},{6,2},{7,3},{8,12},{9,13},{10,... | collective-permute-start | bytes 344072 | tf_op jit(solution)/shard_map/ppermute | solution.py:600
  189.3 4.8 %collective-permute-start.26 = (bf16[1,2,56,128]{3,2,1,0:T(8,128)(2,1)S(1)}, bf16[1,2,56,128]{3,2,1,0:T(8,128)(2,1)S(1)}, u32[]{:S(2)}, u32[]{:S(2)}) collective-permute-start(bf16[1,2,56,128]{3,2,1,0:T(8,128)(2,1)S(1)} %dynamic-slice_convert_fusion.7), channel_id=1, source_target_pairs={{0,16},{1,17},{2,18},{3,19},{4,20},{5,21},{6,22},{7,23},{8,24},{9,... | collective-permute-start | bytes 86024 | tf_op jit(solution)/shard_map/ppermute | solution.py:600
  194.2 4.2 %collective-permute-start.27 = (f32[8,800]{1,0:T(8,128)S(1)}, f32[8,800]{1,0:T(8,128)S(1)}, u32[]{:S(2)}, u32[]{:S(2)}) collective-permute-start(f32[8,800]{1,0:T(8,128)S(1)} %add.132), channel_id=1, source_target_pairs={{0,8},{1,9},{2,10},{3,11},{4,12},{5,13},{6,14},{7,15},{8,0},{9,1},... | collective-permute-start | bytes 76808 | tf_op jit(solution)/shard_map/ppermute | solution.py:600
  198.4 4.8 %collective-permute-start.28 = (f32[8,800]{1,0:T(8,128)S(1)}, f32[8,800]{1,0:T(8,128)S(1)}, u32[]{:S(2)}, u32[]{:S(2)}) collective-permute-start(f32[8,800]{1,0:T(8,128)S(1)} %add.134), channel_id=1, source_target_pairs={{0,16},{1,17},{2,18},{3,19},{4,20},{5,21},{6,22},{7,23},{8,24},{9,... | collective-permute-start | bytes 76808 | tf_op jit(solution)/shard_map/ppermute | solution.py:600
  (15 other events, 86.8 us)
where the time goes:
time: 206 us
  Pallas kernels  130 us (63%)
  starting transfers between devices  34.7 us (17%)
  waiting for transfers between devices  18.9 us (9%)
  local copies, waits for them, and re-layouts  12.5 us (6%)
  other arithmetic  7 us (3%)
  between operations  2.57 us (1%)
    pallas_call x1, Pallas kernels, middle(): pl.pallas_call(functools.partial(middle_kernel, n, Q, G // 2), grid=(G,),...  41.6 us
    pallas_call x4, Pallas kernels, wide_fwd(): pl.pallas_call(functools.partial(wide_fwd_kernel, Q, start), grid=(steps,...  28.6 us
    ppermute x25, starting transfers between devices, swap(): return lax.ppermute(v, 'ctx', [(i, i ^ bit) for i in range(n)])  23.6 us
    pallas_call x2, Pallas kernels, wide_bwd(): pl.pallas_call(functools.partial(wide_bwd_kernel, Q), grid=(steps,), in_s...  23.4 us
    pallas_call x1, Pallas kernels, back(): pl.pallas_call(functools.partial(back_kernel, n, Q, G // 2), grid=(G,), i...  18.7 us
    ppermute x25, waiting for transfers between devices, swap(): return lax.ppermute(v, 'ctx', [(i, i ^ bit) for i in range(n)])  18 us
    pallas_call x1, Pallas kernels, front(): pl.pallas_call(functools.partial(front_kernel, Q, G // 2), grid=(G,), in_...  12.7 us
    ppermute x1, starting transfers between devices, on_device(): above = lax.ppermute(tails[1], 'ctx', down)  5.68 us
  transfers between devices with their start and end apart: 29, of which 12 were waited for; matrix products, arithmetic and copies ran while one was open for 5% of the time, Pallas kernels for 43%

commit v1 on v0

--- a/solution.py
+++ b/solution.py
@@ -161,9 +161,12 @@
     return nt(eye, mat).astype(BF)
 
 
-def ordered(n, slots_ref, g_ref, f32_ref):
+def ordered(n, slots_ref, a_ref, b_ref, f32_ref):
+    odd = slots_ref[n]
     for p in range(n):
-        f32_ref[p] = g_ref[slots_ref[p]].astype(F32)
+        slot = slots_ref[p]
+        piece = jnp.where(odd == p % 2, a_ref[slot].astype(F32), b_ref[slot].astype(F32))
+        f32_ref[p] = piece
 
 
 def bias_block(row):
@@ -177,8 +180,8 @@
     return jnp.where(col == 0, hi.astype(F32), jnp.where(col == 1, mid.astype(F32), jnp.where(col == 2, low.astype(F32), zero))).astype(BF)
 
 
-def unpack_in_kernel(n, slots_ref, g_ref, bias_ref, token_ref, w1_ref, w1t_ref, f32_ref, mat_ref):
-    ordered(n, slots_ref, g_ref, f32_ref)
+def unpack_in_kernel(n, slots_ref, a_ref, b_ref, bias_ref, token_ref, w1_ref, w1t_ref, f32_ref, mat_ref):
+    ordered(n, slots_ref, a_ref, b_ref, f32_ref)
     put_matrix(n, mat_ref, f32_ref, 0)
     D, F = mat_ref.shape
     w1_ref[...] = mat_ref[...].astype(BF)
@@ -186,21 +189,21 @@
     w1t_ref[:, D:] = bias_block(bias_ref[0:1, :])
 
 
-def unpack_in(n, slots, g, bias, token, D, F):
+def unpack_in(n, slots, a, b, bias, token, D, F):
     sd = jax.ShapeDtypeStruct
     return pl.pallas_call(
         functools.partial(unpack_in_kernel, n),
-        in_specs=[smem(), vmem(), vmem(), pl.BlockSpec(memory_space=pl.ANY)], out_specs=[vmem(), vmem()],
+        in_specs=[smem()] + [vmem()] * 3 + [pl.BlockSpec(memory_space=pl.ANY)], out_specs=[vmem(), vmem()],
         out_shape=[sd((D, F), BF), sd((F, D + R), BF)],
-        scratch_shapes=[pltpu.VMEM(g.shape, F32), pltpu.VMEM((D, F), F32)],
+        scratch_shapes=[pltpu.VMEM((n,) + a.shape[1:], F32), pltpu.VMEM((D, F), F32)],
         compiler_params=pltpu.CompilerParams(vmem_limit_bytes=40 * 1024 * 1024), name="unpack_in",
         cost_estimate=cost(1e9, 6e6),
-    )(slots, g, bias, token)
-
-
-def unpack_rest_kernel(n, slots_ref, g_ref, bias_ref, wide_ref, wc_ref, wct_ref, w3_ref, w3t_ref, f32_ref, matc_ref, mat3_ref):
+    )(slots, a, b, bias, token)
+
+
+def unpack_rest_kernel(n, slots_ref, a_ref, b_ref, bias_ref, wide_ref, wc_ref, wct_ref, w3_ref, w3t_ref, f32_ref, matc_ref, mat3_ref):
     F, D = mat3_ref.shape
-    ordered(n, slots_ref, g_ref, f32_ref)
+    ordered(n, slots_ref, a_ref, b_ref, f32_ref)
     put_matrix(n, matc_ref, f32_ref, 0)
     put_matrix(n, mat3_ref, f32_ref, unit_plan(n, 3 * F, F)[2])
     for k in range(3):
@@ -213,16 +216,16 @@
     w3t_ref[:, F:] = bias_block(wide_ref[1:2, :])
 
 
-def unpack_rest(n, slots, g, bias, wide_bias, D, F):
+def unpack_rest(n, slots, a, b, bias, wide_bias, D, F):
     sd = jax.ShapeDtypeStruct
     return pl.pallas_call(
         functools.partial(unpack_rest_kernel, n),
-        in_specs=[smem()] + [vmem()] * 3, out_specs=[vmem()] * 4,
+        in_specs=[smem()] + [vmem()] * 4, out_specs=[vmem()] * 4,
         out_shape=[sd((F, 3 * F), BF), sd((F, 3 * F + R), BF), sd((F, D), BF), sd((D, F + R), BF)],
-        scratch_shapes=[pltpu.VMEM(g.shape, F32), pltpu.VMEM((3 * F, F), F32), pltpu.VMEM((F, D), F32)],
+        scratch_shapes=[pltpu.VMEM((n,) + a.shape[1:], F32), pltpu.VMEM((3 * F, F), F32), pltpu.VMEM((F, D), F32)],
         compiler_params=pltpu.CompilerParams(vmem_limit_bytes=40 * 1024 * 1024), name="unpack_rest",
         cost_estimate=cost(2e9, 14e6),
-    )(slots, g, bias, wide_bias)
+    )(slots, a, b, bias, wide_bias)
 
 
 def rim_store(ref, i, steps, cols):
@@ -418,8 +421,7 @@
             return 0
 
         loop(F // R, act, 0)
-    for q in range(Q):
-        o_ref[q] = nn(w3t_ref[...], rbuf[:, q * T:(q + 1) * T])
+    o_ref[...] = nn(w3t_ref[...], rbuf[...])
     gwo_ref[...] += nt(rbuf[...], cbuf[...])
     for ls, rstd in zip(chunks(N, CH), rstds):
         pull(F, ls.stop - ls.start, ls, d_ref, lambda rows: n_ref[rows, ls], lambda rows: s_ref[rows, ls], rstd, gtab, gacc, bacc, e_ref)
@@ -427,10 +429,10 @@
     for q in range(Q):
         def emit(j, _):
             rows = rows_at(j)
-            out_ref[q, rows, :] = (o_ref[q, rows, :] + x_ref[q, rows, :].astype(F32)).astype(BF)
+            out_ref[q, rows, :] = (o_ref[rows, q * T:(q + 1) * T] + x_ref[q, rows, :].astype(F32)).astype(BF)
             return 0
 
-        loop(D // R, emit, 0, 25)
+        loop(D // R, emit, 0, 50)
     rim_store(head_ref, i, steps, [e_ref[0, :, q * T:q * T + 2 * SHIFT] for q in range(Q)])
 
     @pl.when(i == pl.num_programs(0) - 1)
@@ -455,7 +457,7 @@
         out_specs=[seq_spec(1, F, N), seq_spec(Q, D, T), fixed((n, WIDE // L, rows, L)), fixed((8, D)), fixed(tails.shape)],
         out_shape=[sd((G, F, N), BF), sd((S, D, T), BF), sd((n, WIDE // L, rows, L), F32), sd((8, D), F32), sd(tails.shape, BF)],
         scratch_shapes=[pltpu.VMEM((3 * F + R, N), BF), pltpu.VMEM((D, N), BF), pltpu.VMEM((F + R, N), BF), pltpu.VMEM((F, N), F32),
-                        pltpu.VMEM((F, N), F32), pltpu.VMEM((F, N), F32), pltpu.VMEM((F, N), F32), pltpu.VMEM((Q, D, T), F32),
+                        pltpu.VMEM((F, N), F32), pltpu.VMEM((F, N), F32), pltpu.VMEM((F, N), F32), pltpu.VMEM((D, N), F32),
                         pltpu.VMEM((F, L), F32), pltpu.VMEM((F, L), F32), pltpu.VMEM((F + R, D), F32),
                         pltpu.VMEM((3 * F + R, F), F32), pltpu.VMEM((F, Q * 2 * SHIFT), BF), pltpu.VMEM((F, L), F32), pltpu.VMEM((F, L), F32)],
         compiler_params=params(), name="middle", cost_estimate=cost(18e9, 36e6),
@@ -614,7 +616,8 @@
 
 def slot_table(n, me):
     diff = jnp.arange(n, dtype=jnp.int32) ^ me
-    return sum((jnp.where((diff & bit) != 0, n // 2 // bit, 0) for bit in bits_of(n)), jnp.zeros_like(diff))
+    slots = sum((jnp.where((diff & bit) != 0, n // 2 // bit, 0) for bit in bits_of(n)[1:]), jnp.zeros_like(diff))
+    return jnp.concatenate([slots, (me & 1)[None].astype(jnp.int32)])
 
 
 def split_for(full, bit, me):
@@ -675,19 +678,20 @@
         if count:
             *acts, token = wide_fwd(xT, gain, wide_bias, Q, done, count, acts, token)
             done += count
-        buf_in = jnp.concatenate([buf_in, got_in], axis=0)
+        if s < len(far) - 1:
+            buf_in = jnp.concatenate([buf_in, got_in], axis=0)
         if s < len(far) - 2:
             buf_rest = jnp.concatenate([buf_rest, got_rest], axis=0)
         buf_in, buf_rest, token, gain = together(buf_in, buf_rest, token, gain)
     r1, n0, s0, rstd0 = acts
     got_rest = swap(buf_rest, far[-2], n)
-    w1, w1t = unpack_in(n, table, buf_in, narrow_bias, token, D, F)
+    w1, w1t = unpack_in(n, table, buf_in, got_in, narrow_bias, token, D, F)
     uT, n1, s1, rstd1, tails = front(r1, w1t, narrow_gain, narrow_bias, Q)
     buf_rest, tails = together(jnp.concatenate([buf_rest, got_rest], axis=0), tails)
     below = lax.ppermute(tails[0], "ctx", up)
     above = lax.ppermute(tails[1], "ctx", down)
-    buf_rest = jnp.concatenate([buf_rest, swap(buf_rest, far[-1], n)], axis=0)
-    wc, wct, w3, w3t = unpack_rest(n, table, buf_rest, narrow_bias, wide_bias, D, F)
+    got_rest = swap(buf_rest, far[-1], n)
+    wc, wct, w3, w3t = unpack_rest(n, table, buf_rest, got_rest, narrow_bias, wide_bias, D, F)
     eT, outT, rest, small, heads = middle(n, Q, flags, uT, below, above, tails, cT, xT, wct, w3, w3t,
                                           narrow_gain, narrow_bias, rows_rest)
 

time: 206 us -> 202 us (0.981)
  Pallas kernels: 130 us -> 127 us
    pallas_call x1, Pallas kernels: 41.6 us -> 37.5 us  [middle(): pl.pallas_call(functools.partial(middle_kernel, n, Q, G // 2), grid=(G,),...]
  transfers between devices with their start and end apart: 29 -> 29, of which waited for: 12 -> 12; matrix products, arithmetic and copies ran while one was open for 5% -> 4% of each run, Pallas kernels for 43% -> 44%
where the time goes in v1:
time: 202 us; the launch traced here: 201 us
  Pallas kernels  127 us (63%)
  starting transfers between devices  33.7 us (17%)
  waiting for transfers between devices  18.7 us (9%)
  local copies, waits for them, and re-layouts  13.6 us (7%)
  other arithmetic  5.59 us (3%)
  between operations  2.56 us (1%)
    pallas_call x1, Pallas kernels, middle(): pl.pallas_call(functools.partial(middle_kernel, n, Q, G // 2), grid=(G,),...  37.5 us
    pallas_call x4, Pallas kernels, wide_fwd(): pl.pallas_call(functools.partial(wide_fwd_kernel, Q, start), grid=(steps,...  28.6 us
    ppermute x25, starting transfers between devices, swap(): return lax.ppermute(v, 'ctx', [(i, i ^ bit) for i in range(n)])  23.8 us
    pallas_call x2, Pallas kernels, wide_bwd(): pl.pallas_call(functools.partial(wide_bwd_kernel, Q), grid=(steps,), in_s...  23.4 us
    pallas_call x1, Pallas kernels, back(): pl.pallas_call(functools.partial(back_kernel, n, Q, G // 2), grid=(G,), i...  19.2 us
    ppermute x25, waiting for transfers between devices, swap(): return lax.ppermute(v, 'ctx', [(i, i ^ bit) for i in range(n)])  17.6 us
    pallas_call x1, Pallas kernels, front(): pl.pallas_call(functools.partial(front_kernel, Q, G // 2), grid=(G,), in_...  12.7 us
    ppermute x1, starting transfers between devices, on_device(): above = lax.ppermute(heads[0], 'ctx', down)  4.87 us
  transfers between devices with their start and end apart: 29, of which 12 were waited for; matrix products, arithmetic and copies ran while one was open for 4% of the time, Pallas kernels for 44%

profile of v1, /device:TPU:0, one launch (start us, length us, event | category | flops | bytes accessed | tf_op | source)
XLA Modules:
  0.0 200.8 jit_solution(4616859743170845799)
XLA Ops:
  2.6 4.1 %collective-permute-start.1 = (bf16[1,2,128,128]{3,2,1,0:T(8,128)(2,1)S(1)}, bf16[1,2,128,128]{3,2,1,0:T(8,128)(2,1)S(1)}, u32[]{:S(2)}, u32[]{:S(2)}) collective-permute-start(bf16[1,2,128,128]{3,2,1,0:T(8,128)(2,1)S(1)} %fusion.10), channel_id=1, source_target_pairs={{0,16},{1,17},{2,18},{3,19},{4,20},{5,21},{6,22},{7,23},{8,24},{9,... | collective-permute-start | bytes 196616 | tf_op jit(solution)/shard_map/ppermute | solution.py:602
  9.1 7.1 %wide_fwd.4 = (bf16[4,816,1152]{2,1,0:T(8,128)(2,1)}, bf16[8,800,576]{2,1,0:T(8,128)(2,1)}, bf16[8,800,576]{2,1,0:T(8,128)(2,1)}, f32[8,1,576]{2,1,0:T(1,128)S(1)}, f32[8,128]{1,0:T(8,128)S(1)}) custom-call(bf16[8,800,576]{2,1,0:T(8,128)(2,1)} %bitcast.104, f32[1,800]{1,0:T(1,128)S(1)} %reshape.122.gain_ref, f32[2,800]{1,0:T(2,128)S(1)} %copy-done), custom_call_target="tpu_custom_call" | custom-call | flops 2000000000 | bytes 11000000 | tf_op jit(solution)/shard_map/wide_fwd/pallas_call | solution.py:290
  16.3 2.0 collective-permute-start.3
  18.4 7.1 %wide_fwd.5 = (bf16[4,816,1152]{2,1,0:T(8,128)(2,1)}, bf16[8,800,576]{2,1,0:T(8,128)(2,1)}, bf16[8,800,576]{2,1,0:T(8,128)(2,1)}, f32[8,1,576]{2,1,0:T(1,128)S(1)}, f32[8,128]{1,0:T(8,128)S(1)}) custom-call(bf16[8,800,576]{2,1,0:T(8,128)(2,1)} %bitcast.105, ...), custom_call_target="tpu_custom_call", output_to_operand_aliasing={{0}: (3, {}), {1}: (4, {}), {2}: (5, {}), {3}: (6, {})} | custom-call | flops 2000000000 | bytes 11000000 | tf_op jit(solution)/shard_map/wide_fwd/pallas_call | solution.py:290
  25.6 1.9 collective-permute-start.5
  27.7 7.1 %wide_fwd.6 = (bf16[4,816,1152]{2,1,0:T(8,128)(2,1)}, bf16[8,800,576]{2,1,0:T(8,128)(2,1)}, bf16[8,800,576]{2,1,0:T(8,128)(2,1)}, f32[8,1,576]{2,1,0:T(1,128)S(1)}, f32[8,128]{1,0:T(8,128)S(1)}) custom-call(bf16[8,800,576]{2,1,0:T(8,128)(2,1)} %bitcast.106, ...), custom_call_target="tpu_custom_call", output_to_operand_aliasing={{0}: (3, {}), {1}: (4, {}), {2}: (5, {}), {3}: (6, {})} | custom-call | flops 2000000000 | bytes 11000000 | tf_op jit(solution)/shard_map/wide_fwd/pallas_call | solution.py:290
  37.0 7.2 %wide_fwd.7 = (bf16[4,816,1152]{2,1,0:T(8,128)(2,1)}, bf16[8,800,576]{2,1,0:T(8,128)(2,1)}, bf16[8,800,576]{2,1,0:T(8,128)(2,1)}, f32[8,1,576]{2,1,0:T(1,128)S(1)}, f32[8,128]{1,0:T(8,128)S(1)}) custom-call(bf16[8,800,576]{2,1,0:T(8,128)(2,1)} %bitcast.107, ...), custom_call_target="tpu_custom_call", output_to_operand_aliasing={{0}: (3, {}), {1}: (4, {}), {2}: (5, {}), {3}: (6, {})} | custom-call | flops 2000000000 | bytes 11000000 | tf_op jit(solution)/shard_map/wide_fwd/pallas_call | solution.py:290
  47.9 12.7 %front.1 = (bf16[4,400,1152]{2,1,0:T(8,128)(2,1)}, bf16[4,400,1152]{2,1,0:T(8,128)(2,1)}, bf16[4,400,1152]{2,1,0:T(8,128)(2,1)}, f32[4,1,1152]{2,1,0:T(1,128)S(1)}, bf16[2,400,128]{2,1,0:T(8,128)(2,1)S(1)}) custom-call(bf16[4,816,1152]{2,1,0:T(8,128)(2,1)} %get-tuple-element.125.r1_ref, bf16[400,816]{1,0:T(8,128)(2,1)S(1)} %get-tuple-element.134.w1t_ref, ...), custom_call_target="tpu_custom_call" | custom-call | flops 4000000000 | bytes 19000000 | tf_op jit(solution)/shard_map/front/pallas_call | solution.py:339
  62.9 4.5 %collective-permute-start.10 = (bf16[400,128]{1,0:T(8,128)(2,1)S(1)}, bf16[400,128]{1,0:T(8,128)(2,1)S(1)}, u32[]{:S(2)}, u32[]{:S(2)}) collective-permute-start(bf16[400,128]{1,0:T(8,128)(2,1)S(1)} %get-tuple-element.190), channel_id=1, source_target_pairs={{1,0},{2,1},{3,2},{4,3},{5,4},{6,5},{7,6},{8,7},{9,8},{10,9},{11,1... | collective-permute-start | bytes 307208 | tf_op jit(solution)/shard_map/ppermute | solution.py:692
  67.5 3.7 %unpack_rest.1 = (bf16[400,1200]{1,0:T(8,128)(2,1)S(1)}, bf16[400,1216]{1,0:T(8,128)(2,1)S(1)}, bf16[400,800]{1,0:T(8,128)(2,1)S(1)}, bf16[800,416]{1,0:T(8,128)(2,1)S(1)}) custom-call(s32[33]{0:T(128)S(1)} %pad_add_fusion.slots_ref, bf16[16,2,128,128]{3,2,1,0:T(8,128)(2,1)S(1)} %pad_maximum_fusion.a_ref, ...), custom_call_target="tpu_custom_call" | custom-call | flops 2000000000 | bytes 14000000 | tf_op jit(solution)/shard_map/unpack_rest/pallas_call | solution.py:221
  75.1 37.5 %middle.1 = (bf16[4,400,1152]{2,1,0:T(8,128)(2,1)}, bf16[8,800,576]{2,1,0:T(8,128)(2,1)}, f32[32,2,128,128]{3,2,1,0:T(8,128)}, f32[8,800]{1,0:T(8,128)S(1)}, bf16[2,400,128]{2,1,0:T(8,128)(2,1)S(1)}) custom-call(s32[2]{0:T(128)S(1)} %add_convert_fusion.flags_ref, bf16[4,400,1152]{2,1,0:T(8,128)(2,1)} %get-tuple-element.135.u_ref, ...), custom_call_target="tpu_custom_call" | custom-call | flops 17999998976 | bytes 36000000 | tf_op jit(solution)/shard_map/middle/pallas_call | solution.py:453
  112.7 1.8 fusion
  115.2 4.9 %collective-permute-start.13 = (bf16[400,128]{1,0:T(8,128)(2,1)S(1)}, bf16[400,128]{1,0:T(8,128)(2,1)S(1)}, u32[]{:S(2)}, u32[]{:S(2)}) collective-permute-start(bf16[400,128]{1,0:T(8,128)(2,1)S(1)} %get-tuple-element.188), channel_id=1, source_target_pairs={{1,0},{2,1},{3,2},{4,3},{5,4},{6,5},{7,6},{8,7},{9,8},{10,9},{11,1... | collective-permute-start | bytes 307208 | tf_op jit(solution)/shard_map/ppermute | solution.py:700
  120.1 2.3 %bitcast_add_fusion = f32[16,2,128,128]{3,2,1,0:T(8,128)S(1)} fusion(bf16[16,2,128,128]{3,2,1,0:T(8,128)(2,1)} %collective-permute-done.14, f32[16,2,2,128,128]{4,3,2,1,0:T(8,128)} %bitcast.120, s32[]{:T(128)S(6)} %select_n.83), kind=kLoop, calls=%fused_computation.1 | loop fusion | flops 1048576 | bytes 5242884 | tf_op jit(solution)/shard_map/add | solution.py:702
  122.6 19.2 %back.1 = (bf16[8,400,576]{2,1,0:T(8,128)(2,1)}, f32[32,2,56,128]{3,2,1,0:T(8,128)}, f32[8,800]{1,0:T(8,128)S(1)}) custom-call(s32[2]{0:T(128)S(1)} %add_convert_fusion.flags_ref, bf16[4,400,1152]{2,1,0:T(8,128)(2,1)} %get-tuple-element.144.e_ref, bf16[400,128]{1,0:T(8,128)(2,1)S(1)} %collective-permute-done.12.below_ref, ...), custom_call_target="tpu_custom_call" | custom-call | flops 8000000000 | bytes 25000000 | tf_op jit(solution)/shard_map/back/pallas_call | solution.py:512
  143.3 11.7 %wide_bwd.2 = (bf16[8,800,576]{2,1,0:T(8,128)(2,1)}, f32[8,800]{1,0:T(8,128)S(1)}) custom-call(bf16[8,400,576]{2,1,0:T(8,128)(2,1)} %get-tuple-element.153.e_ref, bf16[800,400]{1,0:T(8,128)(2,1)S(1)} %get-tuple-element.154.w1_ref, bf16[8,800,576]{2,1,0:T(8,128)(2,1)} %get-tuple-element.155.n_ref, bf16[8,800,576]{2,1,0:T(8,128)(2,1)} %get-tuple-element.156.s_ref, ...), custom_call_target="tpu_custom_call" | custom-call | flops 4000000000 | bytes 16800000 | tf_op jit(solution)/shard_map/wide_bwd/pallas_call | solution.py:589
  155.3 2.1 %collective-permute-start.19 = (bf16[8,2,56,128]{3,2,1,0:T(8,128)(2,1)S(1)}, bf16[8,2,56,128]{3,2,1,0:T(8,128)(2,1)S(1)}, u32[]{:S(2)}, u32[]{:S(2)}) collective-permute-start(bf16[8,2,56,128]{3,2,1,0:T(8,128)(2,1)S(1)} %fusion.4), channel_id=1, source_target_pairs={{0,2},{1,3},{2,0},{3,1},{4,6},{5,7},{6,4},{7,5},{8,10},{9,11},{10,... | collective-permute-start | bytes 688136 | tf_op jit(solution)/shard_map/ppermute | solution.py:602
  157.4 11.6 %wide_bwd.3 = (bf16[8,800,576]{2,1,0:T(8,128)(2,1)}, f32[8,800]{1,0:T(8,128)S(1)}) custom-call(bf16[8,400,576]{2,1,0:T(8,128)(2,1)} %get-tuple-element.153.e_ref, bf16[800,400]{1,0:T(8,128)(2,1)S(1)} %get-tuple-element.154.w1_ref, bf16[8,800,576]{2,1,0:T(8,128)(2,1)} %get-tuple-element.155.n_ref, ...), custom_call_target="tpu_custom_call", output_to_operand_aliasing={{0}: (8, {})} | custom-call | flops 4000000000 | bytes 16800000 | tf_op jit(solution)/shard_map/wide_bwd/pallas_call | solution.py:589
  169.1 5.3 %collective-permute-start.21 = (bf16[1,2,128,128]{3,2,1,0:T(8,128)(2,1)S(1)}, bf16[1,2,128,128]{3,2,1,0:T(8,128)(2,1)S(1)}, u32[]{:S(2)}, u32[]{:S(2)}) collective-permute-start(bf16[1,2,128,128]{3,2,1,0:T(8,128)(2,1)S(1)} %dynamic-slice_convert_fusion.5), channel_id=1, source_target_pairs={{0,16},{1,17},{2,18},{3,19},{4,20},{5,21},{6,22},{7,23},{8,24},{9,... | collective-permute-start | bytes 196616 | tf_op jit(solution)/shard_map/ppermute | solution.py:602
  177.1 3.0 %collective-permute-done.22 = bf16[4,2,56,128]{3,2,1,0:T(8,128)(2,1)S(1)} collective-permute-done((bf16[4,2,56,128]{3,2,1,0:T(8,128)(2,1)S(1)}, bf16[4,2,56,128]{3,2,1,0:T(8,128)(2,1)S(1)}, u32[]{:S(2)}, u32[]{:S(2)}) %collective-permute-start.22) | collective-permute-done | bytes 114720 | tf_op jit(solution)/shard_map/ppermute | solution.py:602
  180.4 3.8 %collective-permute-done.23 = f32[8,800]{1,0:T(8,128)S(1)} collective-permute-done((f32[8,800]{1,0:T(8,128)S(1)}, f32[8,800]{1,0:T(8,128)S(1)}, u32[]{:S(2)}, u32[]{:S(2)}) %collective-permute-start.23) | collective-permute-done | bytes 25632 | tf_op jit(solution)/shard_map/ppermute | solution.py:602
  185.9 2.6 %collective-permute-done.25 = f32[8,800]{1,0:T(8,128)S(1)} collective-permute-done((f32[8,800]{1,0:T(8,128)S(1)}, f32[8,800]{1,0:T(8,128)S(1)}, u32[]{:S(2)}, u32[]{:S(2)}) %collective-permute-start.25) | collective-permute-done | bytes 25632 | tf_op jit(solution)/shard_map/ppermute | solution.py:602
  189.3 1.8 collective-permute-start.27
  191.1 2.4 %collective-permute-done.27 = f32[8,800]{1,0:T(8,128)S(1)} collective-permute-done((f32[8,800]{1,0:T(8,128)S(1)}, f32[8,800]{1,0:T(8,128)S(1)}, u32[]{:S(2)}, u32[]{:S(2)}) %collective-permute-start.27) | collective-permute-done | bytes 25632 | tf_op jit(solution)/shard_map/ppermute | solution.py:602
  (139 shorter events, 30.8 us)
Async XLA Ops:
  2.6 13.7 %collective-permute-start.1 = (bf16[1,2,128,128]{3,2,1,0:T(8,128)(2,1)S(1)}, bf16[1,2,128,128]{3,2,1,0:T(8,128)(2,1)S(1)}, u32[]{:S(2)}, u32[]{:S(2)}) collective-permute-start(bf16[1,2,128,128]{3,2,1,0:T(8,128)(2,1)S(1)} %fusion.10), channel_id=1, source_target_pairs={{0,16},{1,17},{2,18},{3,19},{4,20},{5,21},{6,22},{7,23},{8,24},{9,... | collective-permute-start | bytes 196616 | tf_op jit(solution)/shard_map/ppermute | solution.py:602
  7.6 8.6 %collective-permute-start = (bf16[1,2,56,128]{3,2,1,0:T(8,128)(2,1)S(1)}, bf16[1,2,56,128]{3,2,1,0:T(8,128)(2,1)S(1)}, u32[]{:S(2)}, u32[]{:S(2)}) collective-permute-start(bf16[1,2,56,128]{3,2,1,0:T(8,128)(2,1)S(1)} %pad_bitcast_fusion), channel_id=1, source_target_pairs={{0,16},{1,17},{2,18},{3,19},{4,20},{5,21},{6,22},{7,23},{8,24},{9,... | collective-permute-start | bytes 86024 | tf_op jit(solution)/shard_map/ppermute | solution.py:602
  16.3 9.3 %collective-permute-start.3 = (bf16[2,2,128,128]{3,2,1,0:T(8,128)(2,1)S(1)}, bf16[2,2,128,128]{3,2,1,0:T(8,128)(2,1)S(1)}, u32[]{:S(2)}, u32[]{:S(2)}) collective-permute-start(bf16[2,2,128,128]{3,2,1,0:T(8,128)(2,1)S(1)} %pad_maximum_fusion.5), channel_id=1, source_target_pairs={{0,8},{1,9},{2,10},{3,11},{4,12},{5,13},{6,14},{7,15},{8,0},{9,1},... | collective-permute-start | bytes 393224 | tf_op jit(solution)/shard_map/ppermute | solution.py:602
  18.3 7.3 %collective-permute-start.2 = (bf16[2,2,56,128]{3,2,1,0:T(8,128)(2,1)S(1)}, bf16[2,2,56,128]{3,2,1,0:T(8,128)(2,1)S(1)}, u32[]{:S(2)}, u32[]{:S(2)}) collective-permute-start(bf16[2,2,56,128]{3,2,1,0:T(8,128)(2,1)S(1)} %pad_maximum_fusion.7), channel_id=1, source_target_pairs={{0,8},{1,9},{2,10},{3,11},{4,12},{5,13},{6,14},{7,15},{8,0},{9,1},... | collective-permute-start | bytes 172040 | tf_op jit(solution)/shard_map/ppermute | solution.py:602
  25.6 9.8 %collective-permute-start.5 = (bf16[4,2,128,128]{3,2,1,0:T(8,128)(2,1)S(1)}, bf16[4,2,128,128]{3,2,1,0:T(8,128)(2,1)S(1)}, u32[]{:S(2)}, u32[]{:S(2)}) collective-permute-start(bf16[4,2,128,128]{3,2,1,0:T(8,128)(2,1)S(1)} %pad_maximum_fusion.3), channel_id=1, source_target_pairs={{0,4},{1,5},{2,6},{3,7},{4,0},{5,1},{6,2},{7,3},{8,12},{9,13},{10,... | collective-permute-start | bytes 786440 | tf_op jit(solution)/shard_map/ppermute | solution.py:602
  27.5 7.8 %collective-permute-start.4 = (bf16[4,2,56,128]{3,2,1,0:T(8,128)(2,1)S(1)}, bf16[4,2,56,128]{3,2,1,0:T(8,128)(2,1)S(1)}, u32[]{:S(2)}, u32[]{:S(2)}) collective-permute-start(bf16[4,2,56,128]{3,2,1,0:T(8,128)(2,1)S(1)} %pad_maximum_fusion.6), channel_id=1, source_target_pairs={{0,4},{1,5},{2,6},{3,7},{4,0},{5,1},{6,2},{7,3},{8,12},{9,13},{10,... | collective-permute-start | bytes 344072 | tf_op jit(solution)/shard_map/ppermute | solution.py:602
  35.4 8.8 %collective-permute-start.6 = (bf16[8,2,56,128]{3,2,1,0:T(8,128)(2,1)S(1)}, bf16[8,2,56,128]{3,2,1,0:T(8,128)(2,1)S(1)}, u32[]{:S(2)}, u32[]{:S(2)}) collective-permute-start(bf16[8,2,56,128]{3,2,1,0:T(8,128)(2,1)S(1)} %pad_maximum_fusion.4), channel_id=1, source_target_pairs={{0,2},{1,3},{2,0},{3,1},{4,6},{5,7},{6,4},{7,5},{8,10},{9,11},{10,... | collective-permute-start | bytes 688136 | tf_op jit(solution)/shard_map/ppermute | solution.py:602
  44.3 16.2 %collective-permute-start.8 = (bf16[8,2,128,128]{3,2,1,0:T(8,128)(2,1)S(1)}, bf16[8,2,128,128]{3,2,1,0:T(8,128)(2,1)S(1)}, u32[]{:S(2)}, u32[]{:S(2)}) collective-permute-start(bf16[8,2,128,128]{3,2,1,0:T(8,128)(2,1)S(1)} %pad_maximum_fusion.1), channel_id=1, source_target_pairs={{0,2},{1,3},{2,0},{3,1},{4,6},{5,7},{6,4},{7,5},{8,10},{9,11},{10,... | collective-permute-start | bytes 1572872 | tf_op jit(solution)/shard_map/ppermute | solution.py:602
  60.7 6.8 %collective-permute-start.11 = (bf16[16,2,128,128]{3,2,1,0:T(8,128)(2,1)S(1)}, bf16[16,2,128,128]{3,2,1,0:T(8,128)(2,1)S(1)}, u32[]{:S(2)}, u32[]{:S(2)}) collective-permute-start(bf16[16,2,128,128]{3,2,1,0:T(8,128)(2,1)S(1)} %pad_maximum_fusion.a_ref), channel_id=1, source_target_pairs={{0,1},{1,0},{2,3},{3,2},{4,5},{5,4},{6,7},{7,6},{8,9},{9,8},{10,11... | collective-permute-start | bytes 3145736 | tf_op jit(solution)/shard_map/ppermute | solution.py:602
  62.9 11.2 %collective-permute-start.10 = (bf16[400,128]{1,0:T(8,128)(2,1)S(1)}, bf16[400,128]{1,0:T(8,128)(2,1)S(1)}, u32[]{:S(2)}, u32[]{:S(2)}) collective-permute-start(bf16[400,128]{1,0:T(8,128)(2,1)S(1)} %get-tuple-element.190), channel_id=1, source_target_pairs={{1,0},{2,1},{3,2},{4,3},{5,4},{6,5},{7,6},{8,7},{9,8},{10,9},{11,1... | collective-permute-start | bytes 307208 | tf_op jit(solution)/shard_map/ppermute | solution.py:692
  67.4 7.7 %collective-permute-start.9 = (bf16[400,128]{1,0:T(8,128)(2,1)S(1)}, bf16[400,128]{1,0:T(8,128)(2,1)S(1)}, u32[]{:S(2)}, u32[]{:S(2)}) collective-permute-start(bf16[400,128]{1,0:T(8,128)(2,1)S(1)} %get-tuple-element.191), channel_id=1, source_target_pairs={{0,1},{1,2},{2,3},{3,4},{4,5},{5,6},{6,7},{7,8},{8,9},{9,10},{10,1... | collective-permute-start | bytes 307208 | tf_op jit(solution)/shard_map/ppermute | solution.py:691
  114.5 5.5 %collective-permute-start.14 = (bf16[16,2,128,128]{3,2,1,0:T(8,128)(2,1)S(1)}, bf16[16,2,128,128]{3,2,1,0:T(8,128)(2,1)}, u32[]{:S(2)}, u32[]{:S(2)}) collective-permute-start(bf16[16,2,128,128]{3,2,1,0:T(8,128)(2,1)S(1)} %fusion), channel_id=1, source_target_pairs={{0,1},{1,0},{2,3},{3,2},{4,5},{5,4},{6,7},{7,6},{8,9},{9,8},{10,11... | collective-permute-start | bytes 3145736 | tf_op jit(solution)/shard_map/ppermute | solution.py:602
  114.7 7.9 %collective-permute-start.12 = (bf16[400,128]{1,0:T(8,128)(2,1)S(1)}, bf16[400,128]{1,0:T(8,128)(2,1)S(1)}, u32[]{:S(2)}, u32[]{:S(2)}) collective-permute-start(bf16[400,128]{1,0:T(8,128)(2,1)S(1)} %get-tuple-element.189), channel_id=1, source_target_pairs={{0,1},{1,2},{2,3},{3,4},{4,5},{5,6},{6,7},{7,8},{8,9},{9,10},{10,1... | collective-permute-start | bytes 307208 | tf_op jit(solution)/shard_map/ppermute | solution.py:701
  115.2 7.3 %collective-permute-start.13 = (bf16[400,128]{1,0:T(8,128)(2,1)S(1)}, bf16[400,128]{1,0:T(8,128)(2,1)S(1)}, u32[]{:S(2)}, u32[]{:S(2)}) collective-permute-start(bf16[400,128]{1,0:T(8,128)(2,1)S(1)} %get-tuple-element.188), channel_id=1, source_target_pairs={{1,0},{2,1},{3,2},{4,3},{5,4},{6,5},{7,6},{8,7},{9,8},{10,9},{11,1... | collective-permute-start | bytes 307208 | tf_op jit(solution)/shard_map/ppermute | solution.py:700
  122.4 20.5 %collective-permute-start.15 = (bf16[8,2,128,128]{3,2,1,0:T(8,128)(2,1)S(1)}, bf16[8,2,128,128]{3,2,1,0:T(8,128)(2,1)S(1)}, u32[]{:S(2)}, u32[]{:S(2)}) collective-permute-start(bf16[8,2,128,128]{3,2,1,0:T(8,128)(2,1)S(1)} %fusion.1), channel_id=1, source_target_pairs={{0,2},{1,3},{2,0},{3,1},{4,6},{5,7},{6,4},{7,5},{8,10},{9,11},{10,... | collective-permute-start | bytes 1572872 | tf_op jit(solution)/shard_map/ppermute | solution.py:602
  143.1 12.0 %collective-permute-start.17 = (bf16[16,2,56,128]{3,2,1,0:T(8,128)(2,1)S(1)}, bf16[16,2,56,128]{3,2,1,0:T(8,128)(2,1)S(1)}, u32[]{:S(2)}, u32[]{:S(2)}) collective-permute-start(bf16[16,2,56,128]{3,2,1,0:T(8,128)(2,1)S(1)} %fusion.2), channel_id=1, source_target_pairs={{0,1},{1,0},{2,3},{3,2},{4,5},{5,4},{6,7},{7,6},{8,9},{9,8},{10,11... | collective-permute-start | bytes 1376264 | tf_op jit(solution)/shard_map/ppermute | solution.py:602
  143.2 11.8 %collective-permute-start.16 = (bf16[4,2,128,128]{3,2,1,0:T(8,128)(2,1)S(1)}, bf16[4,2,128,128]{3,2,1,0:T(8,128)(2,1)S(1)}, u32[]{:S(2)}, u32[]{:S(2)}) collective-permute-start(bf16[4,2,128,128]{3,2,1,0:T(8,128)(2,1)S(1)} %fusion.3), channel_id=1, source_target_pairs={{0,4},{1,5},{2,6},{3,7},{4,0},{5,1},{6,2},{7,3},{8,12},{9,13},{10,... | collective-permute-start | bytes 786440 | tf_op jit(solution)/shard_map/ppermute | solution.py:602
  155.3 13.7 %collective-permute-start.19 = (bf16[8,2,56,128]{3,2,1,0:T(8,128)(2,1)S(1)}, bf16[8,2,56,128]{3,2,1,0:T(8,128)(2,1)S(1)}, u32[]{:S(2)}, u32[]{:S(2)}) collective-permute-start(bf16[8,2,56,128]{3,2,1,0:T(8,128)(2,1)S(1)} %fusion.4), channel_id=1, source_target_pairs={{0,2},{1,3},{2,0},{3,1},{4,6},{5,7},{6,4},{7,5},{8,10},{9,11},{10,... | collective-permute-start | bytes 688136 | tf_op jit(solution)/shard_map/ppermute | solution.py:602
  157.4 11.6 %collective-permute-start.18 = (bf16[2,2,128,128]{3,2,1,0:T(8,128)(2,1)S(1)}, bf16[2,2,128,128]{3,2,1,0:T(8,128)(2,1)S(1)}, u32[]{:S(2)}, u32[]{:S(2)}) collective-permute-start(bf16[2,2,128,128]{3,2,1,0:T(8,128)(2,1)S(1)} %fusion.5), channel_id=1, source_target_pairs={{0,8},{1,9},{2,10},{3,11},{4,12},{5,13},{6,14},{7,15},{8,0},{9,1},... | collective-permute-start | bytes 393224 | tf_op jit(solution)/shard_map/ppermute | solution.py:602
  169.1 7.9 %collective-permute-start.21 = (bf16[1,2,128,128]{3,2,1,0:T(8,128)(2,1)S(1)}, bf16[1,2,128,128]{3,2,1,0:T(8,128)(2,1)S(1)}, u32[]{:S(2)}, u32[]{:S(2)}) collective-permute-start(bf16[1,2,128,128]{3,2,1,0:T(8,128)(2,1)S(1)} %dynamic-slice_convert_fusion.5), channel_id=1, source_target_pairs={{0,16},{1,17},{2,18},{3,19},{4,20},{5,21},{6,22},{7,23},{8,24},{9,... | collective-permute-start | bytes 196616 | tf_op jit(solution)/shard_map/ppermute | solution.py:602
  174.5 5.6 %collective-permute-start.22 = (bf16[4,2,56,128]{3,2,1,0:T(8,128)(2,1)S(1)}, bf16[4,2,56,128]{3,2,1,0:T(8,128)(2,1)S(1)}, u32[]{:S(2)}, u32[]{:S(2)}) collective-permute-start(bf16[4,2,56,128]{3,2,1,0:T(8,128)(2,1)S(1)} %fusion.8), channel_id=1, source_target_pairs={{0,4},{1,5},{2,6},{3,7},{4,0},{5,1},{6,2},{7,3},{8,12},{9,13},{10,... | collective-permute-start | bytes 344072 | tf_op jit(solution)/shard_map/ppermute | solution.py:602
  180.2 4.2 %collective-permute-start.24 = (bf16[2,2,56,128]{3,2,1,0:T(8,128)(2,1)S(1)}, bf16[2,2,56,128]{3,2,1,0:T(8,128)(2,1)S(1)}, u32[]{:S(2)}, u32[]{:S(2)}) collective-permute-start(bf16[2,2,56,128]{3,2,1,0:T(8,128)(2,1)S(1)} %fusion.11), channel_id=1, source_target_pairs={{0,8},{1,9},{2,10},{3,11},{4,12},{5,13},{6,14},{7,15},{8,0},{9,1},... | collective-permute-start | bytes 172040 | tf_op jit(solution)/shard_map/ppermute | solution.py:602
  184.5 4.8 %collective-permute-start.26 = (bf16[1,2,56,128]{3,2,1,0:T(8,128)(2,1)S(1)}, bf16[1,2,56,128]{3,2,1,0:T(8,128)(2,1)S(1)}, u32[]{:S(2)}, u32[]{:S(2)}) collective-permute-start(bf16[1,2,56,128]{3,2,1,0:T(8,128)(2,1)S(1)} %dynamic-slice_convert_fusion.7), channel_id=1, source_target_pairs={{0,16},{1,17},{2,18},{3,19},{4,20},{5,21},{6,22},{7,23},{8,24},{9,... | collective-permute-start | bytes 86024 | tf_op jit(solution)/shard_map/ppermute | solution.py:602
  193.5 4.8 %collective-permute-start.28 = (f32[8,800]{1,0:T(8,128)S(1)}, f32[8,800]{1,0:T(8,128)S(1)}, u32[]{:S(2)}, u32[]{:S(2)}) collective-permute-start(f32[8,800]{1,0:T(8,128)S(1)} %add.130), channel_id=1, source_target_pairs={{0,16},{1,17},{2,18},{3,19},{4,20},{5,21},{6,22},{7,23},{8,24},{9,... | collective-permute-start | bytes 76808 | tf_op jit(solution)/shard_map/ppermute | solution.py:602
  (15 other events, 93.0 us)

commit v2 on v1

--- a/solution.py
+++ b/solution.py
@@ -95,7 +95,7 @@
 
 def fixed(shape):
     zero = (0,) * len(shape)
-    return pl.BlockSpec(shape, lambda i: zero)
+    return pl.BlockSpec(shape, lambda i: zero, pipeline_mode=pl.Buffered(1))
 
 
 def smem():
@@ -294,7 +294,7 @@
         out_shape=[sd((S // Q, D + R, Q * N), BF), sd((S, D, N), BF), sd((S, D, N), BF), sd((S, 1, N), F32), sd((8, L), F32)],
         scratch_shapes=[pltpu.VMEM((D, L), F32)] * 2 + [pltpu.VMEM((D, N), BF)],
         input_output_aliases={3 + j: j for j in range(len(into))},
-        compiler_params=params(), name="wide_fwd", cost_estimate=cost(1e9 * steps, 5.5e6 * steps),
+        compiler_params=params(52), name="wide_fwd", cost_estimate=cost(1e9 * steps, 5.5e6 * steps),
     )(xT, gain, bias, *into, *token)
 
 
@@ -342,7 +342,7 @@
         out_specs=[seq_spec(1, F, N)] * 3 + [seq_spec(1, 1, N), fixed(rim)],
         out_shape=[sd((G, F, N), BF)] * 3 + [sd((G, 1, N), F32), sd(rim, BF)],
         scratch_shapes=[pltpu.VMEM((F, N), F32)] + [pltpu.VMEM((F, L), F32)] * 2,
-        compiler_params=params(), name="front", cost_estimate=cost(4e9, 19e6),
+        compiler_params=params(52), name="front", cost_estimate=cost(4e9, 19e6),
     )(r1, w1t, gain, bias)
 
 
@@ -373,7 +373,7 @@
 
 def middle_kernel(n, Q, steps, flags_ref, u_ref, below_ref, above_ref, tail_ref, c_ref, x_ref, wct_ref, w3_ref, w3t_ref,
                   gain_ref, bias_ref, e_ref, out_ref, pieces_ref, small_ref, head_ref,
-                  ubuf, cbuf, rbuf, h_ref, d_ref, n_ref, s_ref, o_ref, gacc, bacc, gwo_ref, gwc_ref, hbuf, gtab, btab):
+                  ubuf, cbuf, rbuf, h_ref, d_ref, n_ref, s_ref, o_ref, gacc, bacc, gwo_ref, gwc_ref, hbuf, gtab, btab, pieces32):
     F, N = h_ref.shape
     T = N // Q
     D = c_ref.shape[1]
@@ -442,8 +442,9 @@
         small_ref[0:1, F:] = lane_total(bacc[...]) * 0.5
         small_ref[1:2, :F] = gwc_ref[3 * F:3 * F + 1, :]
         small_ref[2:3, :] = gwo_ref[F:F + 1, :]
-        put_pieces(n, pieces_ref, gwc_ref, 3 * F, F, 0)
-        put_pieces(n, pieces_ref, gwo_ref, F, D, unit_plan(n, 3 * F, F)[2])
+        put_pieces(n, pieces32, gwc_ref, 3 * F, F, 0)
+        put_pieces(n, pieces32, gwo_ref, F, D, unit_plan(n, 3 * F, F)[2])
+        pieces_ref[...] = pieces32[...].astype(BF)
 
 
 def middle(n, Q, flags, uT, below, above, tails, cT, xT, wct, w3, w3t, gain, bias, rows):
@@ -455,17 +456,18 @@
         in_specs=[smem(), seq_spec(1, F, N), fixed(below.shape), fixed(above.shape), fixed(tails.shape), seq_spec(Q, D, T), seq_spec(Q, D, T),
                   fixed(wct.shape), fixed(w3.shape), fixed(w3t.shape), fixed(gain.shape), fixed(bias.shape)],
         out_specs=[seq_spec(1, F, N), seq_spec(Q, D, T), fixed((n, WIDE // L, rows, L)), fixed((8, D)), fixed(tails.shape)],
-        out_shape=[sd((G, F, N), BF), sd((S, D, T), BF), sd((n, WIDE // L, rows, L), F32), sd((8, D), F32), sd(tails.shape, BF)],
+        out_shape=[sd((G, F, N), BF), sd((S, D, T), BF), sd((n, WIDE // L, rows, L), BF), sd((8, D), F32), sd(tails.shape, BF)],
         scratch_shapes=[pltpu.VMEM((3 * F + R, N), BF), pltpu.VMEM((D, N), BF), pltpu.VMEM((F + R, N), BF), pltpu.VMEM((F, N), F32),
                         pltpu.VMEM((F, N), F32), pltpu.VMEM((F, N), F32), pltpu.VMEM((F, N), F32), pltpu.VMEM((D, N), F32),
                         pltpu.VMEM((F, L), F32), pltpu.VMEM((F, L), F32), pltpu.VMEM((F + R, D), F32),
-                        pltpu.VMEM((3 * F + R, F), F32), pltpu.VMEM((F, Q * 2 * SHIFT), BF), pltpu.VMEM((F, L), F32), pltpu.VMEM((F, L), F32)],
-        compiler_params=params(), name="middle", cost_estimate=cost(18e9, 36e6),
+                        pltpu.VMEM((3 * F + R, F), F32), pltpu.VMEM((F, Q * 2 * SHIFT), BF), pltpu.VMEM((F, L), F32), pltpu.VMEM((F, L), F32),
+                        pltpu.VMEM((n, WIDE // L, rows, L), F32)],
+        compiler_params=params(46 if n <= 32 else 60), name="middle", cost_estimate=cost(18e9, 36e6),
     )(flags, uT, below, above, tails, cT, xT, wct, w3, w3t, gain, bias)
 
 
 def back_kernel(n, Q, steps, flags_ref, e_ref, below_ref, above_ref, head_ref, n_ref, s_ref, rstd_ref, r1_ref, wc_ref, gain_ref,
-                small_in, e1_ref, pieces_ref, small_ref, ebuf, d_ref, gacc, bacc, gwi_ref, hbuf, gtab, e1buf):
+                small_in, e1_ref, pieces_ref, small_ref, ebuf, d_ref, gacc, bacc, gwi_ref, hbuf, gtab, e1buf, pieces32):
     F, N = d_ref.shape
     T = N // Q
     D = gwi_ref.shape[0] - R
@@ -502,7 +504,8 @@
         small_ref[1:2, F:] = gwi_ref[D:D + 1, :]
         small_ref[3:4, :F] = lane_total(gacc[...]) * 0.5
         small_ref[3:4, F:] = lane_total(bacc[...]) * 0.5
-        put_pieces(n, pieces_ref, gwi_ref, D, F, 0)
+        put_pieces(n, pieces32, gwi_ref, D, F, 0)
+        pieces_ref[...] = pieces32[...].astype(BF)
 
 
 def back(n, Q, flags, eT, below, above, heads, n1, s1, rstd1, r1, wc, gain, small, rows):
@@ -514,11 +517,11 @@
         in_specs=[smem(), seq_spec(1, F, N), fixed(below.shape), fixed(above.shape), fixed(heads.shape), seq_spec(1, F, N), seq_spec(1, F, N),
                   seq_spec(1, 1, N), seq_spec(1, DE, N), fixed(wc.shape), fixed(gain.shape), fixed(small.shape)],
         out_specs=[seq_spec(Q, F, N // Q), fixed((n, WIDE // L, rows, L)), fixed(small.shape)],
-        out_shape=[sd((G * Q, F, N // Q), BF), sd((n, WIDE // L, rows, L), F32), sd(small.shape, F32)],
+        out_shape=[sd((G * Q, F, N // Q), BF), sd((n, WIDE // L, rows, L), BF), sd(small.shape, F32)],
         scratch_shapes=[pltpu.VMEM((3 * F, N), BF), pltpu.VMEM((F, N), F32), pltpu.VMEM((F, L), F32), pltpu.VMEM((F, L), F32),
                         pltpu.VMEM((DE, F), F32), pltpu.VMEM((F, Q * 2 * SHIFT), BF), pltpu.VMEM((F, L), F32),
-                        pltpu.VMEM((1, F, N), BF)],
-        compiler_params=params(), name="back", cost_estimate=cost(8e9, 25e6),
+                        pltpu.VMEM((1, F, N), BF), pltpu.VMEM((n, WIDE // L, rows, L), F32)],
+        compiler_params=params(52), name="back", cost_estimate=cost(8e9, 25e6),
     )(flags, eT, below, above, heads, n1, s1, rstd1, r1, wc, gain, small)
 
 
@@ -594,7 +597,7 @@
         out_shape=[sd((S, D, N), BF), sd(small.shape, F32)],
         scratch_shapes=[pltpu.VMEM((D, L), F32)] * 3 + [pltpu.VMEM((D, N), F32)] * Q,
         input_output_aliases={8: 0} if into else {},
-        compiler_params=params(), name="wide_bwd", cost_estimate=cost(2e9 * steps, 8.4e6 * steps),
+        compiler_params=params(52), name="wide_bwd", cost_estimate=cost(2e9 * steps, 8.4e6 * steps),
     )(e1, w1, n0, s0, rstd0, cT, gain, small, *into)
 
 

time: 202 us -> 197 us (0.975)
  local copies, waits for them, and re-layouts: 13.6 us -> 9.66 us
  waiting for transfers between devices: 18.7 us -> 22.1 us
  Pallas kernels: 127 us -> 124 us
    convert_element_type x10 -> x8, local copies, waits for them, and re-layouts: 3.37 us -> 0.29 us  [split_for(): lax.dynamic_index_in_dim(pairs, 1 - mine, 1, keepdims=False).astype(BF)]
  transfers between devices with their start and end apart: 29 -> 29, of which waited for: 12 -> 13; matrix products, arithmetic and copies ran while one was open for 4% -> 3% of each run, Pallas kernels for 44% -> 45%
where the time goes in v2:
time: 197 us; the launch traced here: 196 us
  Pallas kernels  124 us (63%)
  starting transfers between devices  33.2 us (17%)
  waiting for transfers between devices  22.1 us (11%)
  local copies, waits for them, and re-layouts  9.66 us (5%)
  other arithmetic  4.9 us (2%)
  between operations  2.47 us (1%)
    pallas_call x1, Pallas kernels, middle(): pl.pallas_call(functools.partial(middle_kernel, n, Q, G // 2), grid=(G,),...  36.3 us
    pallas_call x4, Pallas kernels, wide_fwd(): pl.pallas_call(functools.partial(wide_fwd_kernel, Q, start), grid=(steps,...  28.6 us
    pallas_call x2, Pallas kernels, wide_bwd(): pl.pallas_call(functools.partial(wide_bwd_kernel, Q), grid=(steps,), in_s...  23.2 us
    ppermute x25, starting transfers between devices, swap(): return lax.ppermute(v, 'ctx', [(i, i ^ bit) for i in range(n)])  23 us
    ppermute x25, waiting for transfers between devices, swap(): return lax.ppermute(v, 'ctx', [(i, i ^ bit) for i in range(n)])  18.3 us
    pallas_call x1, Pallas kernels, back(): pl.pallas_call(functools.partial(back_kernel, n, Q, G // 2), grid=(G,), i...  18 us
    pallas_call x1, Pallas kernels, front(): pl.pallas_call(functools.partial(front_kernel, Q, G // 2), grid=(G,), in_...  12.6 us
    ppermute x1, starting transfers between devices, on_device(): above = lax.ppermute(heads[0], 'ctx', down)  4.83 us
  transfers between devices with their start and end apart: 29, of which 13 were waited for; matrix products, arithmetic and copies ran while one was open for 3% of the time, Pallas kernels for 45%

profile of v2, /device:TPU:0, one launch (start us, length us, event | category | flops | bytes accessed | tf_op | source)
XLA Modules:
  0.0 196.3 jit_solution(9038368317780159747)
XLA Ops:
  2.6 4.1 %collective-permute-start.1 = (bf16[1,2,128,128]{3,2,1,0:T(8,128)(2,1)S(1)}, bf16[1,2,128,128]{3,2,1,0:T(8,128)(2,1)S(1)}, u32[]{:S(2)}, u32[]{:S(2)}) collective-permute-start(bf16[1,2,128,128]{3,2,1,0:T(8,128)(2,1)S(1)} %fusion.8), channel_id=1, source_target_pairs={{0,16},{1,17},{2,18},{3,19},{4,20},{5,21},{6,22},{7,23},{8,24},{9,... | collective-permute-start | bytes 196616 | tf_op jit(solution)/shard_map/ppermute | solution.py:605
  9.1 7.1 %wide_fwd.4 = (bf16[4,816,1152]{2,1,0:T(8,128)(2,1)}, bf16[8,800,576]{2,1,0:T(8,128)(2,1)}, bf16[8,800,576]{2,1,0:T(8,128)(2,1)}, f32[8,1,576]{2,1,0:T(1,128)S(1)}, f32[8,128]{1,0:T(8,128)S(1)}) custom-call(bf16[8,800,576]{2,1,0:T(8,128)(2,1)} %bitcast.106, f32[1,800]{1,0:T(1,128)S(1)} %reshape.124.gain_ref, f32[2,800]{1,0:T(2,128)S(1)} %copy-done), custom_call_target="tpu_custom_call" | custom-call | flops 2000000000 | bytes 11000000 | tf_op jit(solution)/shard_map/wide_fwd/pallas_call | solution.py:290
  16.3 2.0 collective-permute-start.3
  18.4 7.1 %wide_fwd.5 = (bf16[4,816,1152]{2,1,0:T(8,128)(2,1)}, bf16[8,800,576]{2,1,0:T(8,128)(2,1)}, bf16[8,800,576]{2,1,0:T(8,128)(2,1)}, f32[8,1,576]{2,1,0:T(1,128)S(1)}, f32[8,128]{1,0:T(8,128)S(1)}) custom-call(bf16[8,800,576]{2,1,0:T(8,128)(2,1)} %bitcast.107, ...), custom_call_target="tpu_custom_call", output_to_operand_aliasing={{0}: (3, {}), {1}: (4, {}), {2}: (5, {}), {3}: (6, {})} | custom-call | flops 2000000000 | bytes 11000000 | tf_op jit(solution)/shard_map/wide_fwd/pallas_call | solution.py:290
  25.6 1.9 collective-permute-start.5
  27.7 7.1 %wide_fwd.6 = (bf16[4,816,1152]{2,1,0:T(8,128)(2,1)}, bf16[8,800,576]{2,1,0:T(8,128)(2,1)}, bf16[8,800,576]{2,1,0:T(8,128)(2,1)}, f32[8,1,576]{2,1,0:T(1,128)S(1)}, f32[8,128]{1,0:T(8,128)S(1)}) custom-call(bf16[8,800,576]{2,1,0:T(8,128)(2,1)} %bitcast.108, ...), custom_call_target="tpu_custom_call", output_to_operand_aliasing={{0}: (3, {}), {1}: (4, {}), {2}: (5, {}), {3}: (6, {})} | custom-call | flops 2000000000 | bytes 11000000 | tf_op jit(solution)/shard_map/wide_fwd/pallas_call | solution.py:290
  37.0 7.2 %wide_fwd.7 = (bf16[4,816,1152]{2,1,0:T(8,128)(2,1)}, bf16[8,800,576]{2,1,0:T(8,128)(2,1)}, bf16[8,800,576]{2,1,0:T(8,128)(2,1)}, f32[8,1,576]{2,1,0:T(1,128)S(1)}, f32[8,128]{1,0:T(8,128)S(1)}) custom-call(bf16[8,800,576]{2,1,0:T(8,128)(2,1)} %bitcast.109, ...), custom_call_target="tpu_custom_call", output_to_operand_aliasing={{0}: (3, {}), {1}: (4, {}), {2}: (5, {}), {3}: (6, {})} | custom-call | flops 2000000000 | bytes 11000000 | tf_op jit(solution)/shard_map/wide_fwd/pallas_call | solution.py:290
  46.1 1.7 unpack_in.1
  47.8 12.6 %front.1 = (bf16[4,400,1152]{2,1,0:T(8,128)(2,1)}, bf16[4,400,1152]{2,1,0:T(8,128)(2,1)}, bf16[4,400,1152]{2,1,0:T(8,128)(2,1)}, f32[4,1,1152]{2,1,0:T(1,128)S(1)}, bf16[2,400,128]{2,1,0:T(8,128)(2,1)S(1)}) custom-call(bf16[4,816,1152]{2,1,0:T(8,128)(2,1)} %get-tuple-element.125.r1_ref, bf16[400,816]{1,0:T(8,128)(2,1)S(1)} %get-tuple-element.134.w1t_ref, ...), custom_call_target="tpu_custom_call" | custom-call | flops 4000000000 | bytes 19000000 | tf_op jit(solution)/shard_map/front/pallas_call | solution.py:339
  62.8 4.5 %collective-permute-start.10 = (bf16[400,128]{1,0:T(8,128)(2,1)S(1)}, bf16[400,128]{1,0:T(8,128)(2,1)S(1)}, u32[]{:S(2)}, u32[]{:S(2)}) collective-permute-start(bf16[400,128]{1,0:T(8,128)(2,1)S(1)} %get-tuple-element.190), channel_id=1, source_target_pairs={{1,0},{2,1},{3,2},{4,3},{5,4},{6,5},{7,6},{8,7},{9,8},{10,9},{11,1... | collective-permute-start | bytes 307208 | tf_op jit(solution)/shard_map/ppermute | solution.py:695
  67.3 3.6 %unpack_rest.1 = (bf16[400,1200]{1,0:T(8,128)(2,1)S(1)}, bf16[400,1216]{1,0:T(8,128)(2,1)S(1)}, bf16[400,800]{1,0:T(8,128)(2,1)S(1)}, bf16[800,416]{1,0:T(8,128)(2,1)S(1)}) custom-call(s32[33]{0:T(128)S(1)} %pad_add_fusion.slots_ref, bf16[16,2,128,128]{3,2,1,0:T(8,128)(2,1)S(1)} %pad_maximum_fusion.a_ref, ...), custom_call_target="tpu_custom_call" | custom-call | flops 2000000000 | bytes 14000000 | tf_op jit(solution)/shard_map/unpack_rest/pallas_call | solution.py:221
  71.9 3.1 %collective-permute-done.9.below_ref = bf16[400,128]{1,0:T(8,128)(2,1)S(1)} collective-permute-done((bf16[400,128]{1,0:T(8,128)(2,1)S(1)}, bf16[400,128]{1,0:T(8,128)(2,1)S(1)}, u32[]{:S(2)}, u32[]{:S(2)}) %collective-permute-start.9) | collective-permute-done | bytes 102432 | tf_op jit(solution)/shard_map/ppermute | solution.py:694
  75.0 36.3 %middle.1 = (bf16[4,400,1152]{2,1,0:T(8,128)(2,1)}, bf16[8,800,576]{2,1,0:T(8,128)(2,1)}, bf16[32,2,128,128]{3,2,1,0:T(8,128)(2,1)S(1)}, f32[8,800]{1,0:T(8,128)S(1)}, bf16[2,400,128]{2,1,0:T(8,128)(2,1)S(1)}) custom-call(s32[2]{0:T(128)S(1)} %add_convert_fusion.flags_ref, bf16[4,400,1152]{2,1,0:T(8,128)(2,1)} %get-tuple-element.135.u_ref, ...), custom_call_target="tpu_custom_call" | custom-call | flops 17999998976 | bytes 36000000 | tf_op jit(solution)/shard_map/middle/pallas_call | solution.py:454
  113.2 4.8 %collective-permute-start.13 = (bf16[400,128]{1,0:T(8,128)(2,1)S(1)}, bf16[400,128]{1,0:T(8,128)(2,1)S(1)}, u32[]{:S(2)}, u32[]{:S(2)}) collective-permute-start(bf16[400,128]{1,0:T(8,128)(2,1)S(1)} %get-tuple-element.188), channel_id=1, source_target_pairs={{1,0},{2,1},{3,2},{4,3},{5,4},{6,5},{7,6},{8,7},{9,8},{10,9},{11,1... | collective-permute-start | bytes 307208 | tf_op jit(solution)/shard_map/ppermute | solution.py:703
  120.5 18.0 %back.1 = (bf16[8,400,576]{2,1,0:T(8,128)(2,1)}, bf16[32,2,56,128]{3,2,1,0:T(8,128)(2,1)S(1)}, f32[8,800]{1,0:T(8,128)S(1)}) custom-call(s32[2]{0:T(128)S(1)} %add_convert_fusion.flags_ref, bf16[4,400,1152]{2,1,0:T(8,128)(2,1)} %get-tuple-element.144.e_ref, bf16[400,128]{1,0:T(8,128)(2,1)S(1)} %collective-permute-done.12.below_ref, ...), custom_call_target="tpu_custom_call" | custom-call | flops 8000000000 | bytes 25000000 | tf_op jit(solution)/shard_map/back/pallas_call | solution.py:515
  138.9 11.6 %wide_bwd.2 = (bf16[8,800,576]{2,1,0:T(8,128)(2,1)}, f32[8,800]{1,0:T(8,128)S(1)}) custom-call(bf16[8,400,576]{2,1,0:T(8,128)(2,1)} %get-tuple-element.153.e_ref, bf16[800,400]{1,0:T(8,128)(2,1)S(1)} %get-tuple-element.154.w1_ref, bf16[8,800,576]{2,1,0:T(8,128)(2,1)} %get-tuple-element.155.n_ref, bf16[8,800,576]{2,1,0:T(8,128)(2,1)} %get-tuple-element.156.s_ref, ...), custom_call_target="tpu_custom_call" | custom-call | flops 4000000000 | bytes 16800000 | tf_op jit(solution)/shard_map/wide_bwd/pallas_call | solution.py:592
  152.1 11.6 %wide_bwd.3 = (bf16[8,800,576]{2,1,0:T(8,128)(2,1)}, f32[8,800]{1,0:T(8,128)S(1)}) custom-call(bf16[8,400,576]{2,1,0:T(8,128)(2,1)} %get-tuple-element.153.e_ref, bf16[800,400]{1,0:T(8,128)(2,1)S(1)} %get-tuple-element.154.w1_ref, bf16[8,800,576]{2,1,0:T(8,128)(2,1)} %get-tuple-element.155.n_ref, ...), custom_call_target="tpu_custom_call", output_to_operand_aliasing={{0}: (8, {})} | custom-call | flops 4000000000 | bytes 16800000 | tf_op jit(solution)/shard_map/wide_bwd/pallas_call | solution.py:592
  163.9 6.0 %collective-permute-start.21 = (bf16[1,2,128,128]{3,2,1,0:T(8,128)(2,1)S(1)}, bf16[1,2,128,128]{3,2,1,0:T(8,128)(2,1)S(1)}, u32[]{:S(2)}, u32[]{:S(2)}) collective-permute-start(bf16[1,2,128,128]{3,2,1,0:T(8,128)(2,1)S(1)} %dynamic-slice_convert_fusion.5), channel_id=1, source_target_pairs={{0,16},{1,17},{2,18},{3,19},{4,20},{5,21},{6,22},{7,23},{8,24},{9,... | collective-permute-start | bytes 196616 | tf_op jit(solution)/shard_map/ppermute | solution.py:605
  172.5 3.0 %collective-permute-done.22 = bf16[4,2,56,128]{3,2,1,0:T(8,128)(2,1)S(1)} collective-permute-done((bf16[4,2,56,128]{3,2,1,0:T(8,128)(2,1)S(1)}, bf16[4,2,56,128]{3,2,1,0:T(8,128)(2,1)S(1)}, u32[]{:S(2)}, u32[]{:S(2)}) %collective-permute-start.22) | collective-permute-done | bytes 114720 | tf_op jit(solution)/shard_map/ppermute | solution.py:605
  175.8 3.8 %collective-permute-done.23 = f32[8,800]{1,0:T(8,128)S(1)} collective-permute-done((f32[8,800]{1,0:T(8,128)S(1)}, f32[8,800]{1,0:T(8,128)S(1)}, u32[]{:S(2)}, u32[]{:S(2)}) %collective-permute-start.23) | collective-permute-done | bytes 25632 | tf_op jit(solution)/shard_map/ppermute | solution.py:605
  180.6 3.3 %collective-permute-done.25 = f32[8,800]{1,0:T(8,128)S(1)} collective-permute-done((f32[8,800]{1,0:T(8,128)S(1)}, f32[8,800]{1,0:T(8,128)S(1)}, u32[]{:S(2)}, u32[]{:S(2)}) %collective-permute-start.25) | collective-permute-done | bytes 25632 | tf_op jit(solution)/shard_map/ppermute | solution.py:605
  184.7 1.8 collective-permute-start.27
  186.6 2.4 %collective-permute-done.27 = f32[8,800]{1,0:T(8,128)S(1)} collective-permute-done((f32[8,800]{1,0:T(8,128)S(1)}, f32[8,800]{1,0:T(8,128)S(1)}, u32[]{:S(2)}, u32[]{:S(2)}) %collective-permute-start.27) | collective-permute-done | bytes 25632 | tf_op jit(solution)/shard_map/ppermute | solution.py:605
  189.0 1.7 collective-permute-start.28
  (131 shorter events, 27.3 us)
Async XLA Ops:
  2.6 13.7 %collective-permute-start.1 = (bf16[1,2,128,128]{3,2,1,0:T(8,128)(2,1)S(1)}, bf16[1,2,128,128]{3,2,1,0:T(8,128)(2,1)S(1)}, u32[]{:S(2)}, u32[]{:S(2)}) collective-permute-start(bf16[1,2,128,128]{3,2,1,0:T(8,128)(2,1)S(1)} %fusion.8), channel_id=1, source_target_pairs={{0,16},{1,17},{2,18},{3,19},{4,20},{5,21},{6,22},{7,23},{8,24},{9,... | collective-permute-start | bytes 196616 | tf_op jit(solution)/shard_map/ppermute | solution.py:605
  7.6 8.6 %collective-permute-start = (bf16[1,2,56,128]{3,2,1,0:T(8,128)(2,1)S(1)}, bf16[1,2,56,128]{3,2,1,0:T(8,128)(2,1)S(1)}, u32[]{:S(2)}, u32[]{:S(2)}) collective-permute-start(bf16[1,2,56,128]{3,2,1,0:T(8,128)(2,1)S(1)} %pad_bitcast_fusion), channel_id=1, source_target_pairs={{0,16},{1,17},{2,18},{3,19},{4,20},{5,21},{6,22},{7,23},{8,24},{9,... | collective-permute-start | bytes 86024 | tf_op jit(solution)/shard_map/ppermute | solution.py:605
  16.3 9.3 %collective-permute-start.3 = (bf16[2,2,128,128]{3,2,1,0:T(8,128)(2,1)S(1)}, bf16[2,2,128,128]{3,2,1,0:T(8,128)(2,1)S(1)}, u32[]{:S(2)}, u32[]{:S(2)}) collective-permute-start(bf16[2,2,128,128]{3,2,1,0:T(8,128)(2,1)S(1)} %pad_maximum_fusion.5), channel_id=1, source_target_pairs={{0,8},{1,9},{2,10},{3,11},{4,12},{5,13},{6,14},{7,15},{8,0},{9,1},... | collective-permute-start | bytes 393224 | tf_op jit(solution)/shard_map/ppermute | solution.py:605
  18.3 7.3 %collective-permute-start.2 = (bf16[2,2,56,128]{3,2,1,0:T(8,128)(2,1)S(1)}, bf16[2,2,56,128]{3,2,1,0:T(8,128)(2,1)S(1)}, u32[]{:S(2)}, u32[]{:S(2)}) collective-permute-start(bf16[2,2,56,128]{3,2,1,0:T(8,128)(2,1)S(1)} %pad_maximum_fusion.7), channel_id=1, source_target_pairs={{0,8},{1,9},{2,10},{3,11},{4,12},{5,13},{6,14},{7,15},{8,0},{9,1},... | collective-permute-start | bytes 172040 | tf_op jit(solution)/shard_map/ppermute | solution.py:605
  25.6 9.8 %collective-permute-start.5 = (bf16[4,2,128,128]{3,2,1,0:T(8,128)(2,1)S(1)}, bf16[4,2,128,128]{3,2,1,0:T(8,128)(2,1)S(1)}, u32[]{:S(2)}, u32[]{:S(2)}) collective-permute-start(bf16[4,2,128,128]{3,2,1,0:T(8,128)(2,1)S(1)} %pad_maximum_fusion.3), channel_id=1, source_target_pairs={{0,4},{1,5},{2,6},{3,7},{4,0},{5,1},{6,2},{7,3},{8,12},{9,13},{10,... | collective-permute-start | bytes 786440 | tf_op jit(solution)/shard_map/ppermute | solution.py:605
  27.5 7.8 %collective-permute-start.4 = (bf16[4,2,56,128]{3,2,1,0:T(8,128)(2,1)S(1)}, bf16[4,2,56,128]{3,2,1,0:T(8,128)(2,1)S(1)}, u32[]{:S(2)}, u32[]{:S(2)}) collective-permute-start(bf16[4,2,56,128]{3,2,1,0:T(8,128)(2,1)S(1)} %pad_maximum_fusion.6), channel_id=1, source_target_pairs={{0,4},{1,5},{2,6},{3,7},{4,0},{5,1},{6,2},{7,3},{8,12},{9,13},{10,... | collective-permute-start | bytes 344072 | tf_op jit(solution)/shard_map/ppermute | solution.py:605
  35.4 8.8 %collective-permute-start.6 = (bf16[8,2,56,128]{3,2,1,0:T(8,128)(2,1)S(1)}, bf16[8,2,56,128]{3,2,1,0:T(8,128)(2,1)S(1)}, u32[]{:S(2)}, u32[]{:S(2)}) collective-permute-start(bf16[8,2,56,128]{3,2,1,0:T(8,128)(2,1)S(1)} %pad_maximum_fusion.4), channel_id=1, source_target_pairs={{0,2},{1,3},{2,0},{3,1},{4,6},{5,7},{6,4},{7,5},{8,10},{9,11},{10,... | collective-permute-start | bytes 688136 | tf_op jit(solution)/shard_map/ppermute | solution.py:605
  44.3 16.1 %collective-permute-start.8 = (bf16[8,2,128,128]{3,2,1,0:T(8,128)(2,1)S(1)}, bf16[8,2,128,128]{3,2,1,0:T(8,128)(2,1)S(1)}, u32[]{:S(2)}, u32[]{:S(2)}) collective-permute-start(bf16[8,2,128,128]{3,2,1,0:T(8,128)(2,1)S(1)} %pad_maximum_fusion.1), channel_id=1, source_target_pairs={{0,2},{1,3},{2,0},{3,1},{4,6},{5,7},{6,4},{7,5},{8,10},{9,11},{10,... | collective-permute-start | bytes 1572872 | tf_op jit(solution)/shard_map/ppermute | solution.py:605
  60.5 6.8 %collective-permute-start.11 = (bf16[16,2,128,128]{3,2,1,0:T(8,128)(2,1)S(1)}, bf16[16,2,128,128]{3,2,1,0:T(8,128)(2,1)S(1)}, u32[]{:S(2)}, u32[]{:S(2)}) collective-permute-start(bf16[16,2,128,128]{3,2,1,0:T(8,128)(2,1)S(1)} %pad_maximum_fusion.a_ref), channel_id=1, source_target_pairs={{0,1},{1,0},{2,3},{3,2},{4,5},{5,4},{6,7},{7,6},{8,9},{9,8},{10,11... | collective-permute-start | bytes 3145736 | tf_op jit(solution)/shard_map/ppermute | solution.py:605
  62.8 9.2 %collective-permute-start.10 = (bf16[400,128]{1,0:T(8,128)(2,1)S(1)}, bf16[400,128]{1,0:T(8,128)(2,1)S(1)}, u32[]{:S(2)}, u32[]{:S(2)}) collective-permute-start(bf16[400,128]{1,0:T(8,128)(2,1)S(1)} %get-tuple-element.190), channel_id=1, source_target_pairs={{1,0},{2,1},{3,2},{4,3},{5,4},{6,5},{7,6},{8,7},{9,8},{10,9},{11,1... | collective-permute-start | bytes 307208 | tf_op jit(solution)/shard_map/ppermute | solution.py:695
  67.3 7.7 %collective-permute-start.9 = (bf16[400,128]{1,0:T(8,128)(2,1)S(1)}, bf16[400,128]{1,0:T(8,128)(2,1)S(1)}, u32[]{:S(2)}, u32[]{:S(2)}) collective-permute-start(bf16[400,128]{1,0:T(8,128)(2,1)S(1)} %get-tuple-element.191), channel_id=1, source_target_pairs={{0,1},{1,2},{2,3},{3,4},{4,5},{5,6},{6,7},{7,8},{8,9},{9,10},{10,1... | collective-permute-start | bytes 307208 | tf_op jit(solution)/shard_map/ppermute | solution.py:694
  112.4 5.6 %collective-permute-start.14 = (bf16[16,2,128,128]{3,2,1,0:T(8,128)(2,1)}, bf16[16,2,128,128]{3,2,1,0:T(8,128)(2,1)}, u32[]{:S(2)}, u32[]{:S(2)}) collective-permute-start(bf16[16,2,128,128]{3,2,1,0:T(8,128)(2,1)} %dynamic-slice_bitcast_fusion), channel_id=1, source_target_pairs={{0,1},{1,0},{2,3},{3,2},{4,5},{5,4},{6,7},{7,6},{8,9},{9,8},{10,11... | collective-permute-start | bytes 3145736 | tf_op jit(solution)/shard_map/ppermute | solution.py:605
  112.4 8.1 %collective-permute-start.12 = (bf16[400,128]{1,0:T(8,128)(2,1)S(1)}, bf16[400,128]{1,0:T(8,128)(2,1)S(1)}, u32[]{:S(2)}, u32[]{:S(2)}) collective-permute-start(bf16[400,128]{1,0:T(8,128)(2,1)S(1)} %get-tuple-element.189), channel_id=1, source_target_pairs={{0,1},{1,2},{2,3},{3,4},{4,5},{5,6},{6,7},{7,8},{8,9},{9,10},{10,1... | collective-permute-start | bytes 307208 | tf_op jit(solution)/shard_map/ppermute | solution.py:704
  113.2 7.3 %collective-permute-start.13 = (bf16[400,128]{1,0:T(8,128)(2,1)S(1)}, bf16[400,128]{1,0:T(8,128)(2,1)S(1)}, u32[]{:S(2)}, u32[]{:S(2)}) collective-permute-start(bf16[400,128]{1,0:T(8,128)(2,1)S(1)} %get-tuple-element.188), channel_id=1, source_target_pairs={{1,0},{2,1},{3,2},{4,3},{5,4},{6,5},{7,6},{8,7},{9,8},{10,9},{11,1... | collective-permute-start | bytes 307208 | tf_op jit(solution)/shard_map/ppermute | solution.py:703
  119.7 18.8 %collective-permute-start.15 = (bf16[8,2,128,128]{3,2,1,0:T(8,128)(2,1)S(1)}, bf16[8,2,128,128]{3,2,1,0:T(8,128)(2,1)S(1)}, u32[]{:S(2)}, u32[]{:S(2)}) collective-permute-start(bf16[8,2,128,128]{3,2,1,0:T(8,128)(2,1)S(1)} %fusion), channel_id=1, source_target_pairs={{0,2},{1,3},{2,0},{3,1},{4,6},{5,7},{6,4},{7,5},{8,10},{9,11},{10,... | collective-permute-start | bytes 1572872 | tf_op jit(solution)/shard_map/ppermute | solution.py:605
  138.7 11.8 %collective-permute-start.17 = (bf16[16,2,56,128]{3,2,1,0:T(8,128)(2,1)S(1)}, bf16[16,2,56,128]{3,2,1,0:T(8,128)(2,1)S(1)}, u32[]{:S(2)}, u32[]{:S(2)}) collective-permute-start(bf16[16,2,56,128]{3,2,1,0:T(8,128)(2,1)S(1)} %dynamic-slice_bitcast_fusion.1), channel_id=1, source_target_pairs={{0,1},{1,0},{2,3},{3,2},{4,5},{5,4},{6,7},{7,6},{8,9},{9,8},{10,11... | collective-permute-start | bytes 1376264 | tf_op jit(solution)/shard_map/ppermute | solution.py:605
  138.8 11.7 %collective-permute-start.16 = (bf16[4,2,128,128]{3,2,1,0:T(8,128)(2,1)S(1)}, bf16[4,2,128,128]{3,2,1,0:T(8,128)(2,1)S(1)}, u32[]{:S(2)}, u32[]{:S(2)}) collective-permute-start(bf16[4,2,128,128]{3,2,1,0:T(8,128)(2,1)S(1)} %fusion.1), channel_id=1, source_target_pairs={{0,4},{1,5},{2,6},{3,7},{4,0},{5,1},{6,2},{7,3},{8,12},{9,13},{10,... | collective-permute-start | bytes 786440 | tf_op jit(solution)/shard_map/ppermute | solution.py:605
  150.8 13.0 %collective-permute-start.19 = (bf16[8,2,56,128]{3,2,1,0:T(8,128)(2,1)S(1)}, bf16[8,2,56,128]{3,2,1,0:T(8,128)(2,1)S(1)}, u32[]{:S(2)}, u32[]{:S(2)}) collective-permute-start(bf16[8,2,56,128]{3,2,1,0:T(8,128)(2,1)S(1)} %fusion.2), channel_id=1, source_target_pairs={{0,2},{1,3},{2,0},{3,1},{4,6},{5,7},{6,4},{7,5},{8,10},{9,11},{10,... | collective-permute-start | bytes 688136 | tf_op jit(solution)/shard_map/ppermute | solution.py:605
  152.1 11.6 %collective-permute-start.18 = (bf16[2,2,128,128]{3,2,1,0:T(8,128)(2,1)S(1)}, bf16[2,2,128,128]{3,2,1,0:T(8,128)(2,1)S(1)}, u32[]{:S(2)}, u32[]{:S(2)}) collective-permute-start(bf16[2,2,128,128]{3,2,1,0:T(8,128)(2,1)S(1)} %fusion.3), channel_id=1, source_target_pairs={{0,8},{1,9},{2,10},{3,11},{4,12},{5,13},{6,14},{7,15},{8,0},{9,1},... | collective-permute-start | bytes 393224 | tf_op jit(solution)/shard_map/ppermute | solution.py:605
  163.9 8.7 %collective-permute-start.21 = (bf16[1,2,128,128]{3,2,1,0:T(8,128)(2,1)S(1)}, bf16[1,2,128,128]{3,2,1,0:T(8,128)(2,1)S(1)}, u32[]{:S(2)}, u32[]{:S(2)}) collective-permute-start(bf16[1,2,128,128]{3,2,1,0:T(8,128)(2,1)S(1)} %dynamic-slice_convert_fusion.5), channel_id=1, source_target_pairs={{0,16},{1,17},{2,18},{3,19},{4,20},{5,21},{6,22},{7,23},{8,24},{9,... | collective-permute-start | bytes 196616 | tf_op jit(solution)/shard_map/ppermute | solution.py:605
  169.9 5.6 %collective-permute-start.22 = (bf16[4,2,56,128]{3,2,1,0:T(8,128)(2,1)S(1)}, bf16[4,2,56,128]{3,2,1,0:T(8,128)(2,1)S(1)}, u32[]{:S(2)}, u32[]{:S(2)}) collective-permute-start(bf16[4,2,56,128]{3,2,1,0:T(8,128)(2,1)S(1)} %fusion.6), channel_id=1, source_target_pairs={{0,4},{1,5},{2,6},{3,7},{4,0},{5,1},{6,2},{7,3},{8,12},{9,13},{10,... | collective-permute-start | bytes 344072 | tf_op jit(solution)/shard_map/ppermute | solution.py:605
  179.9 4.8 %collective-permute-start.26 = (bf16[1,2,56,128]{3,2,1,0:T(8,128)(2,1)S(1)}, bf16[1,2,56,128]{3,2,1,0:T(8,128)(2,1)S(1)}, u32[]{:S(2)}, u32[]{:S(2)}) collective-permute-start(bf16[1,2,56,128]{3,2,1,0:T(8,128)(2,1)S(1)} %dynamic-slice_convert_fusion.7), channel_id=1, source_target_pairs={{0,16},{1,17},{2,18},{3,19},{4,20},{5,21},{6,22},{7,23},{8,24},{9,... | collective-permute-start | bytes 86024 | tf_op jit(solution)/shard_map/ppermute | solution.py:605
  184.7 4.2 %collective-permute-start.27 = (f32[8,800]{1,0:T(8,128)S(1)}, f32[8,800]{1,0:T(8,128)S(1)}, u32[]{:S(2)}, u32[]{:S(2)}) collective-permute-start(f32[8,800]{1,0:T(8,128)S(1)} %add.128), channel_id=1, source_target_pairs={{0,8},{1,9},{2,10},{3,11},{4,12},{5,13},{6,14},{7,15},{8,0},{9,1},... | collective-permute-start | bytes 76808 | tf_op jit(solution)/shard_map/ppermute | solution.py:605
  189.0 4.8 %collective-permute-start.28 = (f32[8,800]{1,0:T(8,128)S(1)}, f32[8,800]{1,0:T(8,128)S(1)}, u32[]{:S(2)}, u32[]{:S(2)}) collective-permute-start(f32[8,800]{1,0:T(8,128)S(1)} %add.130), channel_id=1, source_target_pairs={{0,16},{1,17},{2,18},{3,19},{4,20},{5,21},{6,22},{7,23},{8,24},{9,... | collective-permute-start | bytes 76808 | tf_op jit(solution)/shard_map/ppermute | solution.py:605
  (11 other events, 69.1 us)

commit v3 on v2

--- a/solution.py
+++ b/solution.py
@@ -254,7 +254,7 @@
 
     @pl.when(i == 0)
     def _():
-        fill_table(gtab, gain_ref[...] * 0.5)
+        fill_table(gtab, gain_ref[...].reshape(1, D) * 0.5)
         fill_table(btab, bias_ref[0:1, :] * 0.5)
         token_ref[...] = jnp.zeros_like(token_ref)
 
@@ -289,7 +289,7 @@
     one = lambda rows: pl.BlockSpec((1, rows, N), at)
     return pl.pallas_call(
         functools.partial(wide_fwd_kernel, Q, start), grid=(steps,),
-        in_specs=[one(D), fixed((1, D)), fixed((2, D))] + [pl.BlockSpec(memory_space=pl.ANY)] * len(into + token),
+        in_specs=[one(D), fixed((D,)), fixed((2, D))] + [pl.BlockSpec(memory_space=pl.ANY)] * len(into + token),
         out_specs=[pl.BlockSpec((1, D + R, Q * N), lambda i: ((start + i) // Q, 0, 0)), one(D), one(D), one(1), fixed((8, L))],
         out_shape=[sd((S // Q, D + R, Q * N), BF), sd((S, D, N), BF), sd((S, D, N), BF), sd((S, 1, N), F32), sd((8, L), F32)],
         scratch_shapes=[pltpu.VMEM((D, L), F32)] * 2 + [pltpu.VMEM((D, N), BF)],
@@ -533,7 +533,7 @@
 
     @pl.when(i == 0)
     def _():
-        fill_table(gtab, gain_ref[...] * 0.5)
+        fill_table(gtab, gain_ref[...].reshape(1, D) * 0.5)
         gacc[...] = jnp.zeros_like(gacc)
         bacc[...] = jnp.zeros_like(bacc)
 
@@ -665,7 +665,7 @@
     piece_in = jnp.pad(to_units(w_in, n, D, F), ((0, 0), (0, rows_in - units_in), (0, 0)))
     piece_rest = jnp.concatenate([to_units(w_conv, n, 3 * F, F), to_units(w_out, n, F, D)], axis=1)
     piece_rest = jnp.pad(piece_rest, ((0, 0), (0, rows_rest - piece_rest.shape[1]), (0, 0)))
-    gain0 = wide_gain.reshape(1, D)
+    gain0 = wide_gain
     bits = bits_of(n)
     Q = 2
     steps = slots * seqs // Q
@@ -717,8 +717,16 @@
         got_r, got_i = swap(send_r, bits[s + 2], n), swap(send_i, bits[s], n)
         dxT, small = wide_bwd(Q, e1, w1, n0, s0, rstd0, cT, gain, small, s * steps // halves, steps // halves, dxT)
         rest, into, small = together(keep_r + got_r.astype(F32), keep_i + got_i.astype(F32), small)
+    def owned(own, at, M, C):
+        q, parts, units = unit_plan(n, M, C)
+        return own[:, at:at + units].transpose(1, 0, 2).reshape(units, WIDE)[:, :q].reshape(-1)
+
+
     rest_bits, in_bits = bits[2 + halves:], bits[halves:]
+    flat = {}
     for j in range(len(bits)):
+        if j == len(in_bits) + 1:
+            small, flat["in"], flat["conv"] = together(small, owned(into[0], 0, D, F), owned(rest[0], 0, 3 * F, F))
         got = swap(small, bits[j], n)
         if j < len(rest_bits):
             keep_r, send_r = split_for(rest, rest_bits[j], me)
@@ -729,14 +737,9 @@
         small = small + got
         if j < len(in_bits):
             small, rest, into = together(small, rest, into)
-    own_rest, own_in = rest[0], into[0]
-
-    def owned(own, at, M, C):
-        q, parts, units = unit_plan(n, M, C)
-        return own[:, at:at + units].transpose(1, 0, 2).reshape(units, WIDE)[:, :q].reshape(-1)
 
     back4 = lambda v: v.reshape(slots, seqs, D, T).transpose(0, 1, 3, 2)
-    return (back4(outT), back4(dxT), owned(own_in, 0, D, F), owned(own_rest, 0, 3 * F, F), owned(own_rest, units_conv, F, D),
+    return (back4(outT), back4(dxT), flat["in"], flat["conv"], owned(rest[0], units_conv, F, D),
             small[4], jnp.stack([small[5], small[2]]), jnp.stack([small[3, :F], small[0, :F]]),
             jnp.stack([small[1, F:], small[3, F:], small[1, :F], small[0, F:]]))
 

time: 197 us -> 197 us (level)
  no operation moved by 1% of the time
where the time goes in v3:
time: 197 us; the launch traced here: 196 us
  Pallas kernels  124 us (63%)
  starting transfers between devices  33.5 us (17%)
  waiting for transfers between devices  21.5 us (11%)
  local copies, waits for them, and re-layouts  9.67 us (5%)
  other arithmetic  4.91 us (2%)
  between operations  2.48 us (1%)
    pallas_call x1, Pallas kernels, middle(): pl.pallas_call(functools.partial(middle_kernel, n, Q, G // 2), grid=(G,),...  36.3 us
    pallas_call x4, Pallas kernels, wide_fwd(): pl.pallas_call(functools.partial(wide_fwd_kernel, Q, start), grid=(steps,...  28.6 us
    ppermute x25, starting transfers between devices, swap(): return lax.ppermute(v, 'ctx', [(i, i ^ bit) for i in range(n)])  23.3 us
    pallas_call x2, Pallas kernels, wide_bwd(): pl.pallas_call(functools.partial(wide_bwd_kernel, Q), grid=(steps,), in_s...  23.2 us
    pallas_call x1, Pallas kernels, back(): pl.pallas_call(functools.partial(back_kernel, n, Q, G // 2), grid=(G,), i...  18.1 us
    ppermute x25, waiting for transfers between devices, swap(): return lax.ppermute(v, 'ctx', [(i, i ^ bit) for i in range(n)])  17.7 us
    pallas_call x1, Pallas kernels, front(): pl.pallas_call(functools.partial(front_kernel, Q, G // 2), grid=(G,), in_...  12.6 us
    ppermute x1, starting transfers between devices, on_device(): above = lax.ppermute(heads[0], 'ctx', down)  4.83 us
  transfers between devices with their start and end apart: 29, of which 13 were waited for; matrix products, arithmetic and copies ran while one was open for 3% of the time, Pallas kernels for 45%

profile of v3, /device:TPU:0, one launch (start us, length us, event | category | flops | bytes accessed | tf_op | source)
XLA Modules:
  0.0 196.0 jit_solution(12162667259592073943)
XLA Ops:
  2.6 4.1 %collective-permute-start.1 = (bf16[1,2,128,128]{3,2,1,0:T(8,128)(2,1)S(1)}, bf16[1,2,128,128]{3,2,1,0:T(8,128)(2,1)S(1)}, u32[]{:S(2)}, u32[]{:S(2)}) collective-permute-start(bf16[1,2,128,128]{3,2,1,0:T(8,128)(2,1)S(1)} %fusion.8), channel_id=1, source_target_pairs={{0,16},{1,17},{2,18},{3,19},{4,20},{5,21},{6,22},{7,23},{8,24},{9,... | collective-permute-start | bytes 196616 | tf_op jit(solution)/shard_map/ppermute | solution.py:605
  9.1 7.1 %wide_fwd.4 = (bf16[4,816,1152]{2,1,0:T(8,128)(2,1)}, bf16[8,800,576]{2,1,0:T(8,128)(2,1)}, bf16[8,800,576]{2,1,0:T(8,128)(2,1)}, f32[8,1,576]{2,1,0:T(1,128)S(1)}, f32[8,128]{1,0:T(8,128)S(1)}) custom-call(bf16[8,800,576]{2,1,0:T(8,128)(2,1)} %bitcast.106, f32[800]{0:T(1024)S(1)} %copy-done, f32[2,800]{1,0:T(2,128)S(1)} %copy-done.2), custom_call_target="tpu_custom_call" | custom-call | flops 2000000000 | bytes 11000000 | tf_op jit(solution)/shard_map/wide_fwd/pallas_call | solution.py:290
  16.3 2.0 %collective-permute-start.3 = (bf16[2,2,128,128]{3,2,1,0:T(8,128)(2,1)S(1)}, bf16[2,2,128,128]{3,2,1,0:T(8,128)(2,1)S(1)}, u32[]{:S(2)}, u32[]{:S(2)}) collective-permute-start(bf16[2,2,128,128]{3,2,1,0:T(8,128)(2,1)S(1)} %pad_maximum_fusion.5), channel_id=1, source_target_pairs={{0,8},{1,9},{2,10},{3,11},{4,12},{5,13},{6,14},{7,15},{8,0},{9,1},... | collective-permute-start | bytes 393224 | tf_op jit(solution)/shard_map/ppermute | solution.py:605
  18.4 7.1 %wide_fwd.5 = (bf16[4,816,1152]{2,1,0:T(8,128)(2,1)}, bf16[8,800,576]{2,1,0:T(8,128)(2,1)}, bf16[8,800,576]{2,1,0:T(8,128)(2,1)}, f32[8,1,576]{2,1,0:T(1,128)S(1)}, f32[8,128]{1,0:T(8,128)S(1)}) custom-call(bf16[8,800,576]{2,1,0:T(8,128)(2,1)} %bitcast.107, ...), custom_call_target="tpu_custom_call", output_to_operand_aliasing={{0}: (3, {}), {1}: (4, {}), {2}: (5, {}), {3}: (6, {})} | custom-call | flops 2000000000 | bytes 11000000 | tf_op jit(solution)/shard_map/wide_fwd/pallas_call | solution.py:290
  25.6 1.9 collective-permute-start.5
  27.7 7.1 %wide_fwd.6 = (bf16[4,816,1152]{2,1,0:T(8,128)(2,1)}, bf16[8,800,576]{2,1,0:T(8,128)(2,1)}, bf16[8,800,576]{2,1,0:T(8,128)(2,1)}, f32[8,1,576]{2,1,0:T(1,128)S(1)}, f32[8,128]{1,0:T(8,128)S(1)}) custom-call(bf16[8,800,576]{2,1,0:T(8,128)(2,1)} %bitcast.108, ...), custom_call_target="tpu_custom_call", output_to_operand_aliasing={{0}: (3, {}), {1}: (4, {}), {2}: (5, {}), {3}: (6, {})} | custom-call | flops 2000000000 | bytes 11000000 | tf_op jit(solution)/shard_map/wide_fwd/pallas_call | solution.py:290
  37.0 7.2 %wide_fwd.7 = (bf16[4,816,1152]{2,1,0:T(8,128)(2,1)}, bf16[8,800,576]{2,1,0:T(8,128)(2,1)}, bf16[8,800,576]{2,1,0:T(8,128)(2,1)}, f32[8,1,576]{2,1,0:T(1,128)S(1)}, f32[8,128]{1,0:T(8,128)S(1)}) custom-call(bf16[8,800,576]{2,1,0:T(8,128)(2,1)} %bitcast.109, ...), custom_call_target="tpu_custom_call", output_to_operand_aliasing={{0}: (3, {}), {1}: (4, {}), {2}: (5, {}), {3}: (6, {})} | custom-call | flops 2000000000 | bytes 11000000 | tf_op jit(solution)/shard_map/wide_fwd/pallas_call | solution.py:290
  46.1 1.7 unpack_in.1
  47.8 12.6 %front.1 = (bf16[4,400,1152]{2,1,0:T(8,128)(2,1)}, bf16[4,400,1152]{2,1,0:T(8,128)(2,1)}, bf16[4,400,1152]{2,1,0:T(8,128)(2,1)}, f32[4,1,1152]{2,1,0:T(1,128)S(1)}, bf16[2,400,128]{2,1,0:T(8,128)(2,1)S(1)}) custom-call(bf16[4,816,1152]{2,1,0:T(8,128)(2,1)} %get-tuple-element.128.r1_ref, bf16[400,816]{1,0:T(8,128)(2,1)S(1)} %get-tuple-element.137.w1t_ref, ...), custom_call_target="tpu_custom_call" | custom-call | flops 4000000000 | bytes 19000000 | tf_op jit(solution)/shard_map/front/pallas_call | solution.py:339
  62.7 4.5 %collective-permute-start.10 = (bf16[400,128]{1,0:T(8,128)(2,1)S(1)}, bf16[400,128]{1,0:T(8,128)(2,1)S(1)}, u32[]{:S(2)}, u32[]{:S(2)}) collective-permute-start(bf16[400,128]{1,0:T(8,128)(2,1)S(1)} %get-tuple-element.196), channel_id=1, source_target_pairs={{1,0},{2,1},{3,2},{4,3},{5,4},{6,5},{7,6},{8,7},{9,8},{10,9},{11,1... | collective-permute-start | bytes 307208 | tf_op jit(solution)/shard_map/ppermute | solution.py:695
  67.3 3.6 %unpack_rest.1 = (bf16[400,1200]{1,0:T(8,128)(2,1)S(1)}, bf16[400,1216]{1,0:T(8,128)(2,1)S(1)}, bf16[400,800]{1,0:T(8,128)(2,1)S(1)}, bf16[800,416]{1,0:T(8,128)(2,1)S(1)}) custom-call(s32[33]{0:T(128)S(1)} %pad_add_fusion.slots_ref, bf16[16,2,128,128]{3,2,1,0:T(8,128)(2,1)S(1)} %pad_maximum_fusion.a_ref, ...), custom_call_target="tpu_custom_call" | custom-call | flops 2000000000 | bytes 14000000 | tf_op jit(solution)/shard_map/unpack_rest/pallas_call | solution.py:221
  71.9 3.1 %collective-permute-done.9.below_ref = bf16[400,128]{1,0:T(8,128)(2,1)S(1)} collective-permute-done((bf16[400,128]{1,0:T(8,128)(2,1)S(1)}, bf16[400,128]{1,0:T(8,128)(2,1)S(1)}, u32[]{:S(2)}, u32[]{:S(2)}) %collective-permute-start.9) | collective-permute-done | bytes 102432 | tf_op jit(solution)/shard_map/ppermute | solution.py:694
  75.0 36.3 %middle.1 = (bf16[4,400,1152]{2,1,0:T(8,128)(2,1)}, bf16[8,800,576]{2,1,0:T(8,128)(2,1)}, bf16[32,2,128,128]{3,2,1,0:T(8,128)(2,1)S(1)}, f32[8,800]{1,0:T(8,128)S(1)}, bf16[2,400,128]{2,1,0:T(8,128)(2,1)S(1)}) custom-call(s32[2]{0:T(128)S(1)} %add_convert_fusion.flags_ref, bf16[4,400,1152]{2,1,0:T(8,128)(2,1)} %get-tuple-element.138.u_ref, ...), custom_call_target="tpu_custom_call" | custom-call | flops 17999998976 | bytes 36000000 | tf_op jit(solution)/shard_map/middle/pallas_call | solution.py:454
  113.2 4.8 %collective-permute-start.13 = (bf16[400,128]{1,0:T(8,128)(2,1)S(1)}, bf16[400,128]{1,0:T(8,128)(2,1)S(1)}, u32[]{:S(2)}, u32[]{:S(2)}) collective-permute-start(bf16[400,128]{1,0:T(8,128)(2,1)S(1)} %get-tuple-element.194), channel_id=1, source_target_pairs={{1,0},{2,1},{3,2},{4,3},{5,4},{6,5},{7,6},{8,7},{9,8},{10,9},{11,1... | collective-permute-start | bytes 307208 | tf_op jit(solution)/shard_map/ppermute | solution.py:703
  120.4 18.1 %back.1 = (bf16[8,400,576]{2,1,0:T(8,128)(2,1)}, bf16[32,2,56,128]{3,2,1,0:T(8,128)(2,1)S(1)}, f32[8,800]{1,0:T(8,128)S(1)}) custom-call(s32[2]{0:T(128)S(1)} %add_convert_fusion.flags_ref, bf16[4,400,1152]{2,1,0:T(8,128)(2,1)} %get-tuple-element.147.e_ref, bf16[400,128]{1,0:T(8,128)(2,1)S(1)} %collective-permute-done.12.below_ref, ...), custom_call_target="tpu_custom_call" | custom-call | flops 8000000000 | bytes 25000000 | tf_op jit(solution)/shard_map/back/pallas_call | solution.py:515
  138.9 11.6 %wide_bwd.2 = (bf16[8,800,576]{2,1,0:T(8,128)(2,1)}, f32[8,800]{1,0:T(8,128)S(1)}) custom-call(bf16[8,400,576]{2,1,0:T(8,128)(2,1)} %get-tuple-element.156.e_ref, bf16[800,400]{1,0:T(8,128)(2,1)S(1)} %get-tuple-element.157.w1_ref, bf16[8,800,576]{2,1,0:T(8,128)(2,1)} %get-tuple-element.158.n_ref, bf16[8,800,576]{2,1,0:T(8,128)(2,1)} %get-tuple-element.159.s_ref, ...), custom_call_target="tpu_custom_call" | custom-call | flops 4000000000 | bytes 16800000 | tf_op jit(solution)/shard_map/wide_bwd/pallas_call | solution.py:592
  152.2 11.6 %wide_bwd.3 = (bf16[8,800,576]{2,1,0:T(8,128)(2,1)}, f32[8,800]{1,0:T(8,128)S(1)}) custom-call(bf16[8,400,576]{2,1,0:T(8,128)(2,1)} %get-tuple-element.156.e_ref, bf16[800,400]{1,0:T(8,128)(2,1)S(1)} %get-tuple-element.157.w1_ref, bf16[8,800,576]{2,1,0:T(8,128)(2,1)} %get-tuple-element.158.n_ref, ...), custom_call_target="tpu_custom_call", output_to_operand_aliasing={{0}: (8, {})} | custom-call | flops 4000000000 | bytes 16800000 | tf_op jit(solution)/shard_map/wide_bwd/pallas_call | solution.py:592
  163.9 6.0 %collective-permute-start.21 = (bf16[1,2,128,128]{3,2,1,0:T(8,128)(2,1)S(1)}, bf16[1,2,128,128]{3,2,1,0:T(8,128)(2,1)S(1)}, u32[]{:S(2)}, u32[]{:S(2)}) collective-permute-start(bf16[1,2,128,128]{3,2,1,0:T(8,128)(2,1)S(1)} %dynamic-slice_convert_fusion.5), channel_id=1, source_target_pairs={{0,16},{1,17},{2,18},{3,19},{4,20},{5,21},{6,22},{7,23},{8,24},{9,... | collective-permute-start | bytes 196616 | tf_op jit(solution)/shard_map/ppermute | solution.py:605
  172.5 3.0 %collective-permute-done.22 = bf16[4,2,56,128]{3,2,1,0:T(8,128)(2,1)S(1)} collective-permute-done((bf16[4,2,56,128]{3,2,1,0:T(8,128)(2,1)S(1)}, bf16[4,2,56,128]{3,2,1,0:T(8,128)(2,1)S(1)}, u32[]{:S(2)}, u32[]{:S(2)}) %collective-permute-start.22) | collective-permute-done | bytes 114720 | tf_op jit(solution)/shard_map/ppermute | solution.py:605
  175.8 3.8 %collective-permute-done.23 = f32[8,800]{1,0:T(8,128)S(1)} collective-permute-done((f32[8,800]{1,0:T(8,128)S(1)}, f32[8,800]{1,0:T(8,128)S(1)}, u32[]{:S(2)}, u32[]{:S(2)}) %collective-permute-start.23) | collective-permute-done | bytes 25632 | tf_op jit(solution)/shard_map/ppermute | solution.py:605
  180.7 3.3 %collective-permute-done.25 = f32[8,800]{1,0:T(8,128)S(1)} collective-permute-done((f32[8,800]{1,0:T(8,128)S(1)}, f32[8,800]{1,0:T(8,128)S(1)}, u32[]{:S(2)}, u32[]{:S(2)}) %collective-permute-start.25) | collective-permute-done | bytes 25632 | tf_op jit(solution)/shard_map/ppermute | solution.py:605
  184.8 1.8 collective-permute-start.27
  188.7 2.0 %collective-permute-start.28 = (f32[8,800]{1,0:T(8,128)S(1)}, f32[8,800]{1,0:T(8,128)S(1)}, u32[]{:S(2)}, u32[]{:S(2)}) collective-permute-start(f32[8,800]{1,0:T(8,128)S(1)} %add.130), channel_id=1, source_target_pairs={{0,16},{1,17},{2,18},{3,19},{4,20},{5,21},{6,22},{7,23},{8,24},{9,... | collective-permute-start | bytes 76808 | tf_op jit(solution)/shard_map/ppermute | solution.py:605
  191.6 1.9 collective-permute-done.28
  (134 shorter events, 27.2 us)
Async XLA Ops:
  2.6 13.7 %collective-permute-start.1 = (bf16[1,2,128,128]{3,2,1,0:T(8,128)(2,1)S(1)}, bf16[1,2,128,128]{3,2,1,0:T(8,128)(2,1)S(1)}, u32[]{:S(2)}, u32[]{:S(2)}) collective-permute-start(bf16[1,2,128,128]{3,2,1,0:T(8,128)(2,1)S(1)} %fusion.8), channel_id=1, source_target_pairs={{0,16},{1,17},{2,18},{3,19},{4,20},{5,21},{6,22},{7,23},{8,24},{9,... | collective-permute-start | bytes 196616 | tf_op jit(solution)/shard_map/ppermute | solution.py:605
  7.6 8.6 %collective-permute-start = (bf16[1,2,56,128]{3,2,1,0:T(8,128)(2,1)S(1)}, bf16[1,2,56,128]{3,2,1,0:T(8,128)(2,1)S(1)}, u32[]{:S(2)}, u32[]{:S(2)}) collective-permute-start(bf16[1,2,56,128]{3,2,1,0:T(8,128)(2,1)S(1)} %pad_bitcast_fusion), channel_id=1, source_target_pairs={{0,16},{1,17},{2,18},{3,19},{4,20},{5,21},{6,22},{7,23},{8,24},{9,... | collective-permute-start | bytes 86024 | tf_op jit(solution)/shard_map/ppermute | solution.py:605
  16.3 9.3 %collective-permute-start.3 = (bf16[2,2,128,128]{3,2,1,0:T(8,128)(2,1)S(1)}, bf16[2,2,128,128]{3,2,1,0:T(8,128)(2,1)S(1)}, u32[]{:S(2)}, u32[]{:S(2)}) collective-permute-start(bf16[2,2,128,128]{3,2,1,0:T(8,128)(2,1)S(1)} %pad_maximum_fusion.5), channel_id=1, source_target_pairs={{0,8},{1,9},{2,10},{3,11},{4,12},{5,13},{6,14},{7,15},{8,0},{9,1},... | collective-permute-start | bytes 393224 | tf_op jit(solution)/shard_map/ppermute | solution.py:605
  18.3 7.3 %collective-permute-start.2 = (bf16[2,2,56,128]{3,2,1,0:T(8,128)(2,1)S(1)}, bf16[2,2,56,128]{3,2,1,0:T(8,128)(2,1)S(1)}, u32[]{:S(2)}, u32[]{:S(2)}) collective-permute-start(bf16[2,2,56,128]{3,2,1,0:T(8,128)(2,1)S(1)} %pad_maximum_fusion.7), channel_id=1, source_target_pairs={{0,8},{1,9},{2,10},{3,11},{4,12},{5,13},{6,14},{7,15},{8,0},{9,1},... | collective-permute-start | bytes 172040 | tf_op jit(solution)/shard_map/ppermute | solution.py:605
  25.6 9.8 %collective-permute-start.5 = (bf16[4,2,128,128]{3,2,1,0:T(8,128)(2,1)S(1)}, bf16[4,2,128,128]{3,2,1,0:T(8,128)(2,1)S(1)}, u32[]{:S(2)}, u32[]{:S(2)}) collective-permute-start(bf16[4,2,128,128]{3,2,1,0:T(8,128)(2,1)S(1)} %pad_maximum_fusion.3), channel_id=1, source_target_pairs={{0,4},{1,5},{2,6},{3,7},{4,0},{5,1},{6,2},{7,3},{8,12},{9,13},{10,... | collective-permute-start | bytes 786440 | tf_op jit(solution)/shard_map/ppermute | solution.py:605
  27.5 7.8 %collective-permute-start.4 = (bf16[4,2,56,128]{3,2,1,0:T(8,128)(2,1)S(1)}, bf16[4,2,56,128]{3,2,1,0:T(8,128)(2,1)S(1)}, u32[]{:S(2)}, u32[]{:S(2)}) collective-permute-start(bf16[4,2,56,128]{3,2,1,0:T(8,128)(2,1)S(1)} %pad_maximum_fusion.6), channel_id=1, source_target_pairs={{0,4},{1,5},{2,6},{3,7},{4,0},{5,1},{6,2},{7,3},{8,12},{9,13},{10,... | collective-permute-start | bytes 344072 | tf_op jit(solution)/shard_map/ppermute | solution.py:605
  35.4 8.8 %collective-permute-start.6 = (bf16[8,2,56,128]{3,2,1,0:T(8,128)(2,1)S(1)}, bf16[8,2,56,128]{3,2,1,0:T(8,128)(2,1)S(1)}, u32[]{:S(2)}, u32[]{:S(2)}) collective-permute-start(bf16[8,2,56,128]{3,2,1,0:T(8,128)(2,1)S(1)} %pad_maximum_fusion.4), channel_id=1, source_target_pairs={{0,2},{1,3},{2,0},{3,1},{4,6},{5,7},{6,4},{7,5},{8,10},{9,11},{10,... | collective-permute-start | bytes 688136 | tf_op jit(solution)/shard_map/ppermute | solution.py:605
  44.3 16.1 %collective-permute-start.8 = (bf16[8,2,128,128]{3,2,1,0:T(8,128)(2,1)S(1)}, bf16[8,2,128,128]{3,2,1,0:T(8,128)(2,1)S(1)}, u32[]{:S(2)}, u32[]{:S(2)}) collective-permute-start(bf16[8,2,128,128]{3,2,1,0:T(8,128)(2,1)S(1)} %pad_maximum_fusion.1), channel_id=1, source_target_pairs={{0,2},{1,3},{2,0},{3,1},{4,6},{5,7},{6,4},{7,5},{8,10},{9,11},{10,... | collective-permute-start | bytes 1572872 | tf_op jit(solution)/shard_map/ppermute | solution.py:605
  60.5 6.8 %collective-permute-start.11 = (bf16[16,2,128,128]{3,2,1,0:T(8,128)(2,1)S(1)}, bf16[16,2,128,128]{3,2,1,0:T(8,128)(2,1)S(1)}, u32[]{:S(2)}, u32[]{:S(2)}) collective-permute-start(bf16[16,2,128,128]{3,2,1,0:T(8,128)(2,1)S(1)} %pad_maximum_fusion.a_ref), channel_id=1, source_target_pairs={{0,1},{1,0},{2,3},{3,2},{4,5},{5,4},{6,7},{7,6},{8,9},{9,8},{10,11... | collective-permute-start | bytes 3145736 | tf_op jit(solution)/shard_map/ppermute | solution.py:605
  62.7 9.2 %collective-permute-start.10 = (bf16[400,128]{1,0:T(8,128)(2,1)S(1)}, bf16[400,128]{1,0:T(8,128)(2,1)S(1)}, u32[]{:S(2)}, u32[]{:S(2)}) collective-permute-start(bf16[400,128]{1,0:T(8,128)(2,1)S(1)} %get-tuple-element.196), channel_id=1, source_target_pairs={{1,0},{2,1},{3,2},{4,3},{5,4},{6,5},{7,6},{8,7},{9,8},{10,9},{11,1... | collective-permute-start | bytes 307208 | tf_op jit(solution)/shard_map/ppermute | solution.py:695
  67.3 7.7 %collective-permute-start.9 = (bf16[400,128]{1,0:T(8,128)(2,1)S(1)}, bf16[400,128]{1,0:T(8,128)(2,1)S(1)}, u32[]{:S(2)}, u32[]{:S(2)}) collective-permute-start(bf16[400,128]{1,0:T(8,128)(2,1)S(1)} %get-tuple-element.197), channel_id=1, source_target_pairs={{0,1},{1,2},{2,3},{3,4},{4,5},{5,6},{6,7},{7,8},{8,9},{9,10},{10,1... | collective-permute-start | bytes 307208 | tf_op jit(solution)/shard_map/ppermute | solution.py:694
  112.4 5.6 %collective-permute-start.14 = (bf16[16,2,128,128]{3,2,1,0:T(8,128)(2,1)}, bf16[16,2,128,128]{3,2,1,0:T(8,128)(2,1)}, u32[]{:S(2)}, u32[]{:S(2)}) collective-permute-start(bf16[16,2,128,128]{3,2,1,0:T(8,128)(2,1)} %dynamic-slice_bitcast_fusion), channel_id=1, source_target_pairs={{0,1},{1,0},{2,3},{3,2},{4,5},{5,4},{6,7},{7,6},{8,9},{9,8},{10,11... | collective-permute-start | bytes 3145736 | tf_op jit(solution)/shard_map/ppermute | solution.py:605
  112.4 8.1 %collective-permute-start.12 = (bf16[400,128]{1,0:T(8,128)(2,1)S(1)}, bf16[400,128]{1,0:T(8,128)(2,1)S(1)}, u32[]{:S(2)}, u32[]{:S(2)}) collective-permute-start(bf16[400,128]{1,0:T(8,128)(2,1)S(1)} %get-tuple-element.195), channel_id=1, source_target_pairs={{0,1},{1,2},{2,3},{3,4},{4,5},{5,6},{6,7},{7,8},{8,9},{9,10},{10,1... | collective-permute-start | bytes 307208 | tf_op jit(solution)/shard_map/ppermute | solution.py:704
  113.2 7.3 %collective-permute-start.13 = (bf16[400,128]{1,0:T(8,128)(2,1)S(1)}, bf16[400,128]{1,0:T(8,128)(2,1)S(1)}, u32[]{:S(2)}, u32[]{:S(2)}) collective-permute-start(bf16[400,128]{1,0:T(8,128)(2,1)S(1)} %get-tuple-element.194), channel_id=1, source_target_pairs={{1,0},{2,1},{3,2},{4,3},{5,4},{6,5},{7,6},{8,7},{9,8},{10,9},{11,1... | collective-permute-start | bytes 307208 | tf_op jit(solution)/shard_map/ppermute | solution.py:703
  119.7 18.9 %collective-permute-start.15 = (bf16[8,2,128,128]{3,2,1,0:T(8,128)(2,1)S(1)}, bf16[8,2,128,128]{3,2,1,0:T(8,128)(2,1)S(1)}, u32[]{:S(2)}, u32[]{:S(2)}) collective-permute-start(bf16[8,2,128,128]{3,2,1,0:T(8,128)(2,1)S(1)} %fusion), channel_id=1, source_target_pairs={{0,2},{1,3},{2,0},{3,1},{4,6},{5,7},{6,4},{7,5},{8,10},{9,11},{10,... | collective-permute-start | bytes 1572872 | tf_op jit(solution)/shard_map/ppermute | solution.py:605
  138.7 11.8 %collective-permute-start.17 = (bf16[16,2,56,128]{3,2,1,0:T(8,128)(2,1)S(1)}, bf16[16,2,56,128]{3,2,1,0:T(8,128)(2,1)S(1)}, u32[]{:S(2)}, u32[]{:S(2)}) collective-permute-start(bf16[16,2,56,128]{3,2,1,0:T(8,128)(2,1)S(1)} %dynamic-slice_bitcast_fusion.1), channel_id=1, source_target_pairs={{0,1},{1,0},{2,3},{3,2},{4,5},{5,4},{6,7},{7,6},{8,9},{9,8},{10,11... | collective-permute-start | bytes 1376264 | tf_op jit(solution)/shard_map/ppermute | solution.py:605
  138.8 11.7 %collective-permute-start.16 = (bf16[4,2,128,128]{3,2,1,0:T(8,128)(2,1)S(1)}, bf16[4,2,128,128]{3,2,1,0:T(8,128)(2,1)S(1)}, u32[]{:S(2)}, u32[]{:S(2)}) collective-permute-start(bf16[4,2,128,128]{3,2,1,0:T(8,128)(2,1)S(1)} %fusion.1), channel_id=1, source_target_pairs={{0,4},{1,5},{2,6},{3,7},{4,0},{5,1},{6,2},{7,3},{8,12},{9,13},{10,... | collective-permute-start | bytes 786440 | tf_op jit(solution)/shard_map/ppermute | solution.py:605
  150.8 13.0 %collective-permute-start.19 = (bf16[8,2,56,128]{3,2,1,0:T(8,128)(2,1)S(1)}, bf16[8,2,56,128]{3,2,1,0:T(8,128)(2,1)S(1)}, u32[]{:S(2)}, u32[]{:S(2)}) collective-permute-start(bf16[8,2,56,128]{3,2,1,0:T(8,128)(2,1)S(1)} %fusion.2), channel_id=1, source_target_pairs={{0,2},{1,3},{2,0},{3,1},{4,6},{5,7},{6,4},{7,5},{8,10},{9,11},{10,... | collective-permute-start | bytes 688136 | tf_op jit(solution)/shard_map/ppermute | solution.py:605
  152.2 11.6 %collective-permute-start.18 = (bf16[2,2,128,128]{3,2,1,0:T(8,128)(2,1)S(1)}, bf16[2,2,128,128]{3,2,1,0:T(8,128)(2,1)S(1)}, u32[]{:S(2)}, u32[]{:S(2)}) collective-permute-start(bf16[2,2,128,128]{3,2,1,0:T(8,128)(2,1)S(1)} %fusion.3), channel_id=1, source_target_pairs={{0,8},{1,9},{2,10},{3,11},{4,12},{5,13},{6,14},{7,15},{8,0},{9,1},... | collective-permute-start | bytes 393224 | tf_op jit(solution)/shard_map/ppermute | solution.py:605
  163.9 8.6 %collective-permute-start.21 = (bf16[1,2,128,128]{3,2,1,0:T(8,128)(2,1)S(1)}, bf16[1,2,128,128]{3,2,1,0:T(8,128)(2,1)S(1)}, u32[]{:S(2)}, u32[]{:S(2)}) collective-permute-start(bf16[1,2,128,128]{3,2,1,0:T(8,128)(2,1)S(1)} %dynamic-slice_convert_fusion.5), channel_id=1, source_target_pairs={{0,16},{1,17},{2,18},{3,19},{4,20},{5,21},{6,22},{7,23},{8,24},{9,... | collective-permute-start | bytes 196616 | tf_op jit(solution)/shard_map/ppermute | solution.py:605
  169.9 5.6 %collective-permute-start.22 = (bf16[4,2,56,128]{3,2,1,0:T(8,128)(2,1)S(1)}, bf16[4,2,56,128]{3,2,1,0:T(8,128)(2,1)S(1)}, u32[]{:S(2)}, u32[]{:S(2)}) collective-permute-start(bf16[4,2,56,128]{3,2,1,0:T(8,128)(2,1)S(1)} %fusion.6), channel_id=1, source_target_pairs={{0,4},{1,5},{2,6},{3,7},{4,0},{5,1},{6,2},{7,3},{8,12},{9,13},{10,... | collective-permute-start | bytes 344072 | tf_op jit(solution)/shard_map/ppermute | solution.py:605
  175.6 4.2 %collective-permute-start.24 = (bf16[2,2,56,128]{3,2,1,0:T(8,128)(2,1)S(1)}, bf16[2,2,56,128]{3,2,1,0:T(8,128)(2,1)S(1)}, u32[]{:S(2)}, u32[]{:S(2)}) collective-permute-start(bf16[2,2,56,128]{3,2,1,0:T(8,128)(2,1)S(1)} %fusion.9), channel_id=1, source_target_pairs={{0,8},{1,9},{2,10},{3,11},{4,12},{5,13},{6,14},{7,15},{8,0},{9,1},... | collective-permute-start | bytes 172040 | tf_op jit(solution)/shard_map/ppermute | solution.py:605
  179.9 4.8 %collective-permute-start.26 = (bf16[1,2,56,128]{3,2,1,0:T(8,128)(2,1)S(1)}, bf16[1,2,56,128]{3,2,1,0:T(8,128)(2,1)S(1)}, u32[]{:S(2)}, u32[]{:S(2)}) collective-permute-start(bf16[1,2,56,128]{3,2,1,0:T(8,128)(2,1)S(1)} %dynamic-slice_convert_fusion.7), channel_id=1, source_target_pairs={{0,16},{1,17},{2,18},{3,19},{4,20},{5,21},{6,22},{7,23},{8,24},{9,... | collective-permute-start | bytes 86024 | tf_op jit(solution)/shard_map/ppermute | solution.py:605
  188.7 4.8 %collective-permute-start.28 = (f32[8,800]{1,0:T(8,128)S(1)}, f32[8,800]{1,0:T(8,128)S(1)}, u32[]{:S(2)}, u32[]{:S(2)}) collective-permute-start(f32[8,800]{1,0:T(8,128)S(1)} %add.130), channel_id=1, source_target_pairs={{0,16},{1,17},{2,18},{3,19},{4,20},{5,21},{6,22},{7,23},{8,24},{9,... | collective-permute-start | bytes 76808 | tf_op jit(solution)/shard_map/ppermute | solution.py:605
  (13 other events, 87.9 us)

commit v4 on v3

--- a/solution.py
+++ b/solution.py
@@ -724,13 +724,14 @@
 
     rest_bits, in_bits = bits[2 + halves:], bits[halves:]
     flat = {}
+    order = in_bits + bits[:halves][::-1]
     for j in range(len(bits)):
         if j == len(in_bits) + 1:
             small, flat["in"], flat["conv"] = together(small, owned(into[0], 0, D, F), owned(rest[0], 0, 3 * F, F))
-        got = swap(small, bits[j], n)
-        if j < len(rest_bits):
-            keep_r, send_r = split_for(rest, rest_bits[j], me)
-            rest = keep_r + swap(send_r, rest_bits[j], n).astype(F32)
+        got = swap(small, order[j], n)
+        if order[j] in rest_bits:
+            keep_r, send_r = split_for(rest, order[j], me)
+            rest = keep_r + swap(send_r, order[j], n).astype(F32)
         if j < len(in_bits):
             keep_i, send_i = split_for(into, in_bits[j], me)
             into = keep_i + swap(send_i, in_bits[j], n).astype(F32)

time: 197 us -> 195 us (0.990)
  waiting for transfers between devices: 21.5 us -> 18.9 us
    ppermute x25, waiting for transfers between devices: 17.7 us -> 15.1 us  [swap(): return lax.ppermute(v, 'ctx', [(i, i ^ bit) for i in range(n)])]
  transfers between devices with their start and end apart: 29 -> 29, of which waited for: 13 -> 10; matrix products, arithmetic and copies ran while one was open for 3% -> 3% of each run, Pallas kernels for 45% -> 45%
where the time goes in v4:
time: 195 us; the launch traced here: 194 us
  Pallas kernels  124 us (64%)
  starting transfers between devices  34.3 us (18%)
  waiting for transfers between devices  18.9 us (10%)
  local copies, waits for them, and re-layouts  9.67 us (5%)
  other arithmetic  4.92 us (3%)
  between operations  2.51 us (1%)
    pallas_call x1, Pallas kernels, middle(): pl.pallas_call(functools.partial(middle_kernel, n, Q, G // 2), grid=(G,),...  36.3 us
    pallas_call x4, Pallas kernels, wide_fwd(): pl.pallas_call(functools.partial(wide_fwd_kernel, Q, start), grid=(steps,...  28.6 us
    ppermute x25, starting transfers between devices, swap(): return lax.ppermute(v, 'ctx', [(i, i ^ bit) for i in range(n)])  24.1 us
    pallas_call x2, Pallas kernels, wide_bwd(): pl.pallas_call(functools.partial(wide_bwd_kernel, Q), grid=(steps,), in_s...  23.2 us
    pallas_call x1, Pallas kernels, back(): pl.pallas_call(functools.partial(back_kernel, n, Q, G // 2), grid=(G,), i...  18.1 us
    ppermute x25, waiting for transfers between devices, swap(): return lax.ppermute(v, 'ctx', [(i, i ^ bit) for i in range(n)])  15.1 us
    pallas_call x1, Pallas kernels, front(): pl.pallas_call(functools.partial(front_kernel, Q, G // 2), grid=(G,), in_...  12.6 us
    ppermute x1, starting transfers between devices, on_device(): above = lax.ppermute(heads[0], 'ctx', down)  4.83 us
  transfers between devices with their start and end apart: 29, of which 10 were waited for; matrix products, arithmetic and copies ran while one was open for 3% of the time, Pallas kernels for 45%

profile of v4, /device:TPU:0, one launch (start us, length us, event | category | flops | bytes accessed | tf_op | source)
XLA Modules:
  0.0 194.2 jit_solution(14791276781713364213)
XLA Ops:
  2.6 4.1 %collective-permute-start.1 = (bf16[1,2,128,128]{3,2,1,0:T(8,128)(2,1)S(1)}, bf16[1,2,128,128]{3,2,1,0:T(8,128)(2,1)S(1)}, u32[]{:S(2)}, u32[]{:S(2)}) collective-permute-start(bf16[1,2,128,128]{3,2,1,0:T(8,128)(2,1)S(1)} %fusion.8), channel_id=1, source_target_pairs={{0,16},{1,17},{2,18},{3,19},{4,20},{5,21},{6,22},{7,23},{8,24},{9,... | collective-permute-start | bytes 196616 | tf_op jit(solution)/shard_map/ppermute | solution.py:605
  9.1 7.1 %wide_fwd.4 = (bf16[4,816,1152]{2,1,0:T(8,128)(2,1)}, bf16[8,800,576]{2,1,0:T(8,128)(2,1)}, bf16[8,800,576]{2,1,0:T(8,128)(2,1)}, f32[8,1,576]{2,1,0:T(1,128)S(1)}, f32[8,128]{1,0:T(8,128)S(1)}) custom-call(bf16[8,800,576]{2,1,0:T(8,128)(2,1)} %bitcast.106, f32[800]{0:T(1024)S(1)} %copy-done, f32[2,800]{1,0:T(2,128)S(1)} %copy-done.2), custom_call_target="tpu_custom_call" | custom-call | flops 2000000000 | bytes 11000000 | tf_op jit(solution)/shard_map/wide_fwd/pallas_call | solution.py:290
  16.3 2.0 %collective-permute-start.3 = (bf16[2,2,128,128]{3,2,1,0:T(8,128)(2,1)S(1)}, bf16[2,2,128,128]{3,2,1,0:T(8,128)(2,1)S(1)}, u32[]{:S(2)}, u32[]{:S(2)}) collective-permute-start(bf16[2,2,128,128]{3,2,1,0:T(8,128)(2,1)S(1)} %pad_maximum_fusion.5), channel_id=1, source_target_pairs={{0,8},{1,9},{2,10},{3,11},{4,12},{5,13},{6,14},{7,15},{8,0},{9,1},... | collective-permute-start | bytes 393224 | tf_op jit(solution)/shard_map/ppermute | solution.py:605
  18.4 7.1 %wide_fwd.5 = (bf16[4,816,1152]{2,1,0:T(8,128)(2,1)}, bf16[8,800,576]{2,1,0:T(8,128)(2,1)}, bf16[8,800,576]{2,1,0:T(8,128)(2,1)}, f32[8,1,576]{2,1,0:T(1,128)S(1)}, f32[8,128]{1,0:T(8,128)S(1)}) custom-call(bf16[8,800,576]{2,1,0:T(8,128)(2,1)} %bitcast.107, ...), custom_call_target="tpu_custom_call", output_to_operand_aliasing={{0}: (3, {}), {1}: (4, {}), {2}: (5, {}), {3}: (6, {})} | custom-call | flops 2000000000 | bytes 11000000 | tf_op jit(solution)/shard_map/wide_fwd/pallas_call | solution.py:290
  25.6 1.9 collective-permute-start.5
  27.7 7.1 %wide_fwd.6 = (bf16[4,816,1152]{2,1,0:T(8,128)(2,1)}, bf16[8,800,576]{2,1,0:T(8,128)(2,1)}, bf16[8,800,576]{2,1,0:T(8,128)(2,1)}, f32[8,1,576]{2,1,0:T(1,128)S(1)}, f32[8,128]{1,0:T(8,128)S(1)}) custom-call(bf16[8,800,576]{2,1,0:T(8,128)(2,1)} %bitcast.108, ...), custom_call_target="tpu_custom_call", output_to_operand_aliasing={{0}: (3, {}), {1}: (4, {}), {2}: (5, {}), {3}: (6, {})} | custom-call | flops 2000000000 | bytes 11000000 | tf_op jit(solution)/shard_map/wide_fwd/pallas_call | solution.py:290
  37.0 7.2 %wide_fwd.7 = (bf16[4,816,1152]{2,1,0:T(8,128)(2,1)}, bf16[8,800,576]{2,1,0:T(8,128)(2,1)}, bf16[8,800,576]{2,1,0:T(8,128)(2,1)}, f32[8,1,576]{2,1,0:T(1,128)S(1)}, f32[8,128]{1,0:T(8,128)S(1)}) custom-call(bf16[8,800,576]{2,1,0:T(8,128)(2,1)} %bitcast.109, ...), custom_call_target="tpu_custom_call", output_to_operand_aliasing={{0}: (3, {}), {1}: (4, {}), {2}: (5, {}), {3}: (6, {})} | custom-call | flops 2000000000 | bytes 11000000 | tf_op jit(solution)/shard_map/wide_fwd/pallas_call | solution.py:290
  47.8 12.6 %front.1 = (bf16[4,400,1152]{2,1,0:T(8,128)(2,1)}, bf16[4,400,1152]{2,1,0:T(8,128)(2,1)}, bf16[4,400,1152]{2,1,0:T(8,128)(2,1)}, f32[4,1,1152]{2,1,0:T(1,128)S(1)}, bf16[2,400,128]{2,1,0:T(8,128)(2,1)S(1)}) custom-call(bf16[4,816,1152]{2,1,0:T(8,128)(2,1)} %get-tuple-element.128.r1_ref, bf16[400,816]{1,0:T(8,128)(2,1)S(1)} %get-tuple-element.137.w1t_ref, ...), custom_call_target="tpu_custom_call" | custom-call | flops 4000000000 | bytes 19000000 | tf_op jit(solution)/shard_map/front/pallas_call | solution.py:339
  62.7 4.5 %collective-permute-start.10 = (bf16[400,128]{1,0:T(8,128)(2,1)S(1)}, bf16[400,128]{1,0:T(8,128)(2,1)S(1)}, u32[]{:S(2)}, u32[]{:S(2)}) collective-permute-start(bf16[400,128]{1,0:T(8,128)(2,1)S(1)} %get-tuple-element.196), channel_id=1, source_target_pairs={{1,0},{2,1},{3,2},{4,3},{5,4},{6,5},{7,6},{8,7},{9,8},{10,9},{11,1... | collective-permute-start | bytes 307208 | tf_op jit(solution)/shard_map/ppermute | solution.py:695
  67.3 3.6 %unpack_rest.1 = (bf16[400,1200]{1,0:T(8,128)(2,1)S(1)}, bf16[400,1216]{1,0:T(8,128)(2,1)S(1)}, bf16[400,800]{1,0:T(8,128)(2,1)S(1)}, bf16[800,416]{1,0:T(8,128)(2,1)S(1)}) custom-call(s32[33]{0:T(128)S(1)} %pad_add_fusion.slots_ref, bf16[16,2,128,128]{3,2,1,0:T(8,128)(2,1)S(1)} %pad_maximum_fusion.a_ref, ...), custom_call_target="tpu_custom_call" | custom-call | flops 2000000000 | bytes 14000000 | tf_op jit(solution)/shard_map/unpack_rest/pallas_call | solution.py:221
  71.9 3.1 %collective-permute-done.9.below_ref = bf16[400,128]{1,0:T(8,128)(2,1)S(1)} collective-permute-done((bf16[400,128]{1,0:T(8,128)(2,1)S(1)}, bf16[400,128]{1,0:T(8,128)(2,1)S(1)}, u32[]{:S(2)}, u32[]{:S(2)}) %collective-permute-start.9) | collective-permute-done | bytes 102432 | tf_op jit(solution)/shard_map/ppermute | solution.py:694
  75.0 36.3 %middle.1 = (bf16[4,400,1152]{2,1,0:T(8,128)(2,1)}, bf16[8,800,576]{2,1,0:T(8,128)(2,1)}, bf16[32,2,128,128]{3,2,1,0:T(8,128)(2,1)S(1)}, f32[8,800]{1,0:T(8,128)S(1)}, bf16[2,400,128]{2,1,0:T(8,128)(2,1)S(1)}) custom-call(s32[2]{0:T(128)S(1)} %add_convert_fusion.flags_ref, bf16[4,400,1152]{2,1,0:T(8,128)(2,1)} %get-tuple-element.138.u_ref, ...), custom_call_target="tpu_custom_call" | custom-call | flops 17999998976 | bytes 36000000 | tf_op jit(solution)/shard_map/middle/pallas_call | solution.py:454
  113.2 4.8 %collective-permute-start.13 = (bf16[400,128]{1,0:T(8,128)(2,1)S(1)}, bf16[400,128]{1,0:T(8,128)(2,1)S(1)}, u32[]{:S(2)}, u32[]{:S(2)}) collective-permute-start(bf16[400,128]{1,0:T(8,128)(2,1)S(1)} %get-tuple-element.194), channel_id=1, source_target_pairs={{1,0},{2,1},{3,2},{4,3},{5,4},{6,5},{7,6},{8,7},{9,8},{10,9},{11,1... | collective-permute-start | bytes 307208 | tf_op jit(solution)/shard_map/ppermute | solution.py:703
  120.4 18.1 %back.1 = (bf16[8,400,576]{2,1,0:T(8,128)(2,1)}, bf16[32,2,56,128]{3,2,1,0:T(8,128)(2,1)S(1)}, f32[8,800]{1,0:T(8,128)S(1)}) custom-call(s32[2]{0:T(128)S(1)} %add_convert_fusion.flags_ref, bf16[4,400,1152]{2,1,0:T(8,128)(2,1)} %get-tuple-element.147.e_ref, bf16[400,128]{1,0:T(8,128)(2,1)S(1)} %collective-permute-done.12.below_ref, ...), custom_call_target="tpu_custom_call" | custom-call | flops 8000000000 | bytes 25000000 | tf_op jit(solution)/shard_map/back/pallas_call | solution.py:515
  138.9 11.6 %wide_bwd.2 = (bf16[8,800,576]{2,1,0:T(8,128)(2,1)}, f32[8,800]{1,0:T(8,128)S(1)}) custom-call(bf16[8,400,576]{2,1,0:T(8,128)(2,1)} %get-tuple-element.156.e_ref, bf16[800,400]{1,0:T(8,128)(2,1)S(1)} %get-tuple-element.157.w1_ref, bf16[8,800,576]{2,1,0:T(8,128)(2,1)} %get-tuple-element.158.n_ref, bf16[8,800,576]{2,1,0:T(8,128)(2,1)} %get-tuple-element.159.s_ref, ...), custom_call_target="tpu_custom_call" | custom-call | flops 4000000000 | bytes 16800000 | tf_op jit(solution)/shard_map/wide_bwd/pallas_call | solution.py:592
  152.2 11.6 %wide_bwd.3 = (bf16[8,800,576]{2,1,0:T(8,128)(2,1)}, f32[8,800]{1,0:T(8,128)S(1)}) custom-call(bf16[8,400,576]{2,1,0:T(8,128)(2,1)} %get-tuple-element.156.e_ref, bf16[800,400]{1,0:T(8,128)(2,1)S(1)} %get-tuple-element.157.w1_ref, bf16[8,800,576]{2,1,0:T(8,128)(2,1)} %get-tuple-element.158.n_ref, ...), custom_call_target="tpu_custom_call", output_to_operand_aliasing={{0}: (8, {})} | custom-call | flops 4000000000 | bytes 16800000 | tf_op jit(solution)/shard_map/wide_bwd/pallas_call | solution.py:592
  163.9 2.1 %collective-permute-start.21 = (bf16[4,2,56,128]{3,2,1,0:T(8,128)(2,1)S(1)}, bf16[4,2,56,128]{3,2,1,0:T(8,128)(2,1)S(1)}, u32[]{:S(2)}, u32[]{:S(2)}) collective-permute-start(bf16[4,2,56,128]{3,2,1,0:T(8,128)(2,1)S(1)} %fusion.6), channel_id=1, source_target_pairs={{0,4},{1,5},{2,6},{3,7},{4,0},{5,1},{6,2},{7,3},{8,12},{9,13},{10,... | collective-permute-start | bytes 344072 | tf_op jit(solution)/shard_map/ppermute | solution.py:605
  166.0 3.8 %collective-permute-done.20 = f32[8,800]{1,0:T(8,128)S(1)} collective-permute-done((f32[8,800]{1,0:T(8,128)S(1)}, f32[8,800]{1,0:T(8,128)S(1)}, u32[]{:S(2)}, u32[]{:S(2)}) %collective-permute-start.20) | collective-permute-done | bytes 25632 | tf_op jit(solution)/shard_map/ppermute | solution.py:605
  169.9 2.1 %collective-permute-start.23 = (bf16[2,2,56,128]{3,2,1,0:T(8,128)(2,1)S(1)}, bf16[2,2,56,128]{3,2,1,0:T(8,128)(2,1)S(1)}, u32[]{:S(2)}, u32[]{:S(2)}) collective-permute-start(bf16[2,2,56,128]{3,2,1,0:T(8,128)(2,1)S(1)} %fusion.9), channel_id=1, source_target_pairs={{0,8},{1,9},{2,10},{3,11},{4,12},{5,13},{6,14},{7,15},{8,0},{9,1},... | collective-permute-start | bytes 172040 | tf_op jit(solution)/shard_map/ppermute | solution.py:605
  172.1 3.8 %collective-permute-done.22 = f32[8,800]{1,0:T(8,128)S(1)} collective-permute-done((f32[8,800]{1,0:T(8,128)S(1)}, f32[8,800]{1,0:T(8,128)S(1)}, u32[]{:S(2)}, u32[]{:S(2)}) %collective-permute-start.22) | collective-permute-done | bytes 25632 | tf_op jit(solution)/shard_map/ppermute | solution.py:605
  175.9 4.1 %collective-permute-start.26 = (bf16[1,2,56,128]{3,2,1,0:T(8,128)(2,1)S(1)}, bf16[1,2,56,128]{3,2,1,0:T(8,128)(2,1)S(1)}, u32[]{:S(2)}, u32[]{:S(2)}) collective-permute-start(bf16[1,2,56,128]{3,2,1,0:T(8,128)(2,1)S(1)} %dynamic-slice_convert_fusion.7), channel_id=1, source_target_pairs={{0,16},{1,17},{2,18},{3,19},{4,20},{5,21},{6,22},{7,23},{8,24},{9,... | collective-permute-start | bytes 86024 | tf_op jit(solution)/shard_map/ppermute | solution.py:605
  180.1 2.9 %collective-permute-start.25 = (bf16[1,2,128,128]{3,2,1,0:T(8,128)(2,1)S(1)}, bf16[1,2,128,128]{3,2,1,0:T(8,128)(2,1)S(1)}, u32[]{:S(2)}, u32[]{:S(2)}) collective-permute-start(bf16[1,2,128,128]{3,2,1,0:T(8,128)(2,1)S(1)} %dynamic-slice_convert_fusion.5), channel_id=1, source_target_pairs={{0,16},{1,17},{2,18},{3,19},{4,20},{5,21},{6,22},{7,23},{8,24},{9,... | collective-permute-start | bytes 196616 | tf_op jit(solution)/shard_map/ppermute | solution.py:605
  183.1 1.8 collective-permute-done.24
  188.5 2.0 %collective-permute-done.27 = f32[8,800]{1,0:T(8,128)S(1)} collective-permute-done((f32[8,800]{1,0:T(8,128)S(1)}, f32[8,800]{1,0:T(8,128)S(1)}, u32[]{:S(2)}, u32[]{:S(2)}) %collective-permute-start.27) | collective-permute-done | bytes 25632 | tf_op jit(solution)/shard_map/ppermute | solution.py:605
  (134 shorter events, 26.4 us)
Async XLA Ops:
  2.6 13.7 %collective-permute-start.1 = (bf16[1,2,128,128]{3,2,1,0:T(8,128)(2,1)S(1)}, bf16[1,2,128,128]{3,2,1,0:T(8,128)(2,1)S(1)}, u32[]{:S(2)}, u32[]{:S(2)}) collective-permute-start(bf16[1,2,128,128]{3,2,1,0:T(8,128)(2,1)S(1)} %fusion.8), channel_id=1, source_target_pairs={{0,16},{1,17},{2,18},{3,19},{4,20},{5,21},{6,22},{7,23},{8,24},{9,... | collective-permute-start | bytes 196616 | tf_op jit(solution)/shard_map/ppermute | solution.py:605
  7.6 8.6 %collective-permute-start = (bf16[1,2,56,128]{3,2,1,0:T(8,128)(2,1)S(1)}, bf16[1,2,56,128]{3,2,1,0:T(8,128)(2,1)S(1)}, u32[]{:S(2)}, u32[]{:S(2)}) collective-permute-start(bf16[1,2,56,128]{3,2,1,0:T(8,128)(2,1)S(1)} %pad_bitcast_fusion), channel_id=1, source_target_pairs={{0,16},{1,17},{2,18},{3,19},{4,20},{5,21},{6,22},{7,23},{8,24},{9,... | collective-permute-start | bytes 86024 | tf_op jit(solution)/shard_map/ppermute | solution.py:605
  16.3 9.3 %collective-permute-start.3 = (bf16[2,2,128,128]{3,2,1,0:T(8,128)(2,1)S(1)}, bf16[2,2,128,128]{3,2,1,0:T(8,128)(2,1)S(1)}, u32[]{:S(2)}, u32[]{:S(2)}) collective-permute-start(bf16[2,2,128,128]{3,2,1,0:T(8,128)(2,1)S(1)} %pad_maximum_fusion.5), channel_id=1, source_target_pairs={{0,8},{1,9},{2,10},{3,11},{4,12},{5,13},{6,14},{7,15},{8,0},{9,1},... | collective-permute-start | bytes 393224 | tf_op jit(solution)/shard_map/ppermute | solution.py:605
  18.3 7.3 %collective-permute-start.2 = (bf16[2,2,56,128]{3,2,1,0:T(8,128)(2,1)S(1)}, bf16[2,2,56,128]{3,2,1,0:T(8,128)(2,1)S(1)}, u32[]{:S(2)}, u32[]{:S(2)}) collective-permute-start(bf16[2,2,56,128]{3,2,1,0:T(8,128)(2,1)S(1)} %pad_maximum_fusion.7), channel_id=1, source_target_pairs={{0,8},{1,9},{2,10},{3,11},{4,12},{5,13},{6,14},{7,15},{8,0},{9,1},... | collective-permute-start | bytes 172040 | tf_op jit(solution)/shard_map/ppermute | solution.py:605
  25.6 9.8 %collective-permute-start.5 = (bf16[4,2,128,128]{3,2,1,0:T(8,128)(2,1)S(1)}, bf16[4,2,128,128]{3,2,1,0:T(8,128)(2,1)S(1)}, u32[]{:S(2)}, u32[]{:S(2)}) collective-permute-start(bf16[4,2,128,128]{3,2,1,0:T(8,128)(2,1)S(1)} %pad_maximum_fusion.3), channel_id=1, source_target_pairs={{0,4},{1,5},{2,6},{3,7},{4,0},{5,1},{6,2},{7,3},{8,12},{9,13},{10,... | collective-permute-start | bytes 786440 | tf_op jit(solution)/shard_map/ppermute | solution.py:605
  27.5 7.8 %collective-permute-start.4 = (bf16[4,2,56,128]{3,2,1,0:T(8,128)(2,1)S(1)}, bf16[4,2,56,128]{3,2,1,0:T(8,128)(2,1)S(1)}, u32[]{:S(2)}, u32[]{:S(2)}) collective-permute-start(bf16[4,2,56,128]{3,2,1,0:T(8,128)(2,1)S(1)} %pad_maximum_fusion.6), channel_id=1, source_target_pairs={{0,4},{1,5},{2,6},{3,7},{4,0},{5,1},{6,2},{7,3},{8,12},{9,13},{10,... | collective-permute-start | bytes 344072 | tf_op jit(solution)/shard_map/ppermute | solution.py:605
  35.4 8.8 %collective-permute-start.6 = (bf16[8,2,56,128]{3,2,1,0:T(8,128)(2,1)S(1)}, bf16[8,2,56,128]{3,2,1,0:T(8,128)(2,1)S(1)}, u32[]{:S(2)}, u32[]{:S(2)}) collective-permute-start(bf16[8,2,56,128]{3,2,1,0:T(8,128)(2,1)S(1)} %pad_maximum_fusion.4), channel_id=1, source_target_pairs={{0,2},{1,3},{2,0},{3,1},{4,6},{5,7},{6,4},{7,5},{8,10},{9,11},{10,... | collective-permute-start | bytes 688136 | tf_op jit(solution)/shard_map/ppermute | solution.py:605
  44.3 16.1 %collective-permute-start.8 = (bf16[8,2,128,128]{3,2,1,0:T(8,128)(2,1)S(1)}, bf16[8,2,128,128]{3,2,1,0:T(8,128)(2,1)S(1)}, u32[]{:S(2)}, u32[]{:S(2)}) collective-permute-start(bf16[8,2,128,128]{3,2,1,0:T(8,128)(2,1)S(1)} %pad_maximum_fusion.1), channel_id=1, source_target_pairs={{0,2},{1,3},{2,0},{3,1},{4,6},{5,7},{6,4},{7,5},{8,10},{9,11},{10,... | collective-permute-start | bytes 1572872 | tf_op jit(solution)/shard_map/ppermute | solution.py:605
  60.5 6.8 %collective-permute-start.11 = (bf16[16,2,128,128]{3,2,1,0:T(8,128)(2,1)S(1)}, bf16[16,2,128,128]{3,2,1,0:T(8,128)(2,1)S(1)}, u32[]{:S(2)}, u32[]{:S(2)}) collective-permute-start(bf16[16,2,128,128]{3,2,1,0:T(8,128)(2,1)S(1)} %pad_maximum_fusion.a_ref), channel_id=1, source_target_pairs={{0,1},{1,0},{2,3},{3,2},{4,5},{5,4},{6,7},{7,6},{8,9},{9,8},{10,11... | collective-permute-start | bytes 3145736 | tf_op jit(solution)/shard_map/ppermute | solution.py:605
  62.7 9.2 %collective-permute-start.10 = (bf16[400,128]{1,0:T(8,128)(2,1)S(1)}, bf16[400,128]{1,0:T(8,128)(2,1)S(1)}, u32[]{:S(2)}, u32[]{:S(2)}) collective-permute-start(bf16[400,128]{1,0:T(8,128)(2,1)S(1)} %get-tuple-element.196), channel_id=1, source_target_pairs={{1,0},{2,1},{3,2},{4,3},{5,4},{6,5},{7,6},{8,7},{9,8},{10,9},{11,1... | collective-permute-start | bytes 307208 | tf_op jit(solution)/shard_map/ppermute | solution.py:695
  67.3 7.7 %collective-permute-start.9 = (bf16[400,128]{1,0:T(8,128)(2,1)S(1)}, bf16[400,128]{1,0:T(8,128)(2,1)S(1)}, u32[]{:S(2)}, u32[]{:S(2)}) collective-permute-start(bf16[400,128]{1,0:T(8,128)(2,1)S(1)} %get-tuple-element.197), channel_id=1, source_target_pairs={{0,1},{1,2},{2,3},{3,4},{4,5},{5,6},{6,7},{7,8},{8,9},{9,10},{10,1... | collective-permute-start | bytes 307208 | tf_op jit(solution)/shard_map/ppermute | solution.py:694
  112.4 5.6 %collective-permute-start.14 = (bf16[16,2,128,128]{3,2,1,0:T(8,128)(2,1)}, bf16[16,2,128,128]{3,2,1,0:T(8,128)(2,1)}, u32[]{:S(2)}, u32[]{:S(2)}) collective-permute-start(bf16[16,2,128,128]{3,2,1,0:T(8,128)(2,1)} %dynamic-slice_bitcast_fusion), channel_id=1, source_target_pairs={{0,1},{1,0},{2,3},{3,2},{4,5},{5,4},{6,7},{7,6},{8,9},{9,8},{10,11... | collective-permute-start | bytes 3145736 | tf_op jit(solution)/shard_map/ppermute | solution.py:605
  112.4 8.1 %collective-permute-start.12 = (bf16[400,128]{1,0:T(8,128)(2,1)S(1)}, bf16[400,128]{1,0:T(8,128)(2,1)S(1)}, u32[]{:S(2)}, u32[]{:S(2)}) collective-permute-start(bf16[400,128]{1,0:T(8,128)(2,1)S(1)} %get-tuple-element.195), channel_id=1, source_target_pairs={{0,1},{1,2},{2,3},{3,4},{4,5},{5,6},{6,7},{7,8},{8,9},{9,10},{10,1... | collective-permute-start | bytes 307208 | tf_op jit(solution)/shard_map/ppermute | solution.py:704
  113.2 7.3 %collective-permute-start.13 = (bf16[400,128]{1,0:T(8,128)(2,1)S(1)}, bf16[400,128]{1,0:T(8,128)(2,1)S(1)}, u32[]{:S(2)}, u32[]{:S(2)}) collective-permute-start(bf16[400,128]{1,0:T(8,128)(2,1)S(1)} %get-tuple-element.194), channel_id=1, source_target_pairs={{1,0},{2,1},{3,2},{4,3},{5,4},{6,5},{7,6},{8,7},{9,8},{10,9},{11,1... | collective-permute-start | bytes 307208 | tf_op jit(solution)/shard_map/ppermute | solution.py:703
  119.7 18.9 %collective-permute-start.15 = (bf16[8,2,128,128]{3,2,1,0:T(8,128)(2,1)S(1)}, bf16[8,2,128,128]{3,2,1,0:T(8,128)(2,1)S(1)}, u32[]{:S(2)}, u32[]{:S(2)}) collective-permute-start(bf16[8,2,128,128]{3,2,1,0:T(8,128)(2,1)S(1)} %fusion), channel_id=1, source_target_pairs={{0,2},{1,3},{2,0},{3,1},{4,6},{5,7},{6,4},{7,5},{8,10},{9,11},{10,... | collective-permute-start | bytes 1572872 | tf_op jit(solution)/shard_map/ppermute | solution.py:605
  138.7 11.8 %collective-permute-start.17 = (bf16[16,2,56,128]{3,2,1,0:T(8,128)(2,1)S(1)}, bf16[16,2,56,128]{3,2,1,0:T(8,128)(2,1)S(1)}, u32[]{:S(2)}, u32[]{:S(2)}) collective-permute-start(bf16[16,2,56,128]{3,2,1,0:T(8,128)(2,1)S(1)} %dynamic-slice_bitcast_fusion.1), channel_id=1, source_target_pairs={{0,1},{1,0},{2,3},{3,2},{4,5},{5,4},{6,7},{7,6},{8,9},{9,8},{10,11... | collective-permute-start | bytes 1376264 | tf_op jit(solution)/shard_map/ppermute | solution.py:605
  138.8 11.7 %collective-permute-start.16 = (bf16[4,2,128,128]{3,2,1,0:T(8,128)(2,1)S(1)}, bf16[4,2,128,128]{3,2,1,0:T(8,128)(2,1)S(1)}, u32[]{:S(2)}, u32[]{:S(2)}) collective-permute-start(bf16[4,2,128,128]{3,2,1,0:T(8,128)(2,1)S(1)} %fusion.1), channel_id=1, source_target_pairs={{0,4},{1,5},{2,6},{3,7},{4,0},{5,1},{6,2},{7,3},{8,12},{9,13},{10,... | collective-permute-start | bytes 786440 | tf_op jit(solution)/shard_map/ppermute | solution.py:605
  150.8 13.0 %collective-permute-start.19 = (bf16[8,2,56,128]{3,2,1,0:T(8,128)(2,1)S(1)}, bf16[8,2,56,128]{3,2,1,0:T(8,128)(2,1)S(1)}, u32[]{:S(2)}, u32[]{:S(2)}) collective-permute-start(bf16[8,2,56,128]{3,2,1,0:T(8,128)(2,1)S(1)} %fusion.2), channel_id=1, source_target_pairs={{0,2},{1,3},{2,0},{3,1},{4,6},{5,7},{6,4},{7,5},{8,10},{9,11},{10,... | collective-permute-start | bytes 688136 | tf_op jit(solution)/shard_map/ppermute | solution.py:605
  152.2 11.6 %collective-permute-start.18 = (bf16[2,2,128,128]{3,2,1,0:T(8,128)(2,1)S(1)}, bf16[2,2,128,128]{3,2,1,0:T(8,128)(2,1)S(1)}, u32[]{:S(2)}, u32[]{:S(2)}) collective-permute-start(bf16[2,2,128,128]{3,2,1,0:T(8,128)(2,1)S(1)} %fusion.3), channel_id=1, source_target_pairs={{0,8},{1,9},{2,10},{3,11},{4,12},{5,13},{6,14},{7,15},{8,0},{9,1},... | collective-permute-start | bytes 393224 | tf_op jit(solution)/shard_map/ppermute | solution.py:605
  163.9 5.9 %collective-permute-start.21 = (bf16[4,2,56,128]{3,2,1,0:T(8,128)(2,1)S(1)}, bf16[4,2,56,128]{3,2,1,0:T(8,128)(2,1)S(1)}, u32[]{:S(2)}, u32[]{:S(2)}) collective-permute-start(bf16[4,2,56,128]{3,2,1,0:T(8,128)(2,1)S(1)} %fusion.6), channel_id=1, source_target_pairs={{0,4},{1,5},{2,6},{3,7},{4,0},{5,1},{6,2},{7,3},{8,12},{9,13},{10,... | collective-permute-start | bytes 344072 | tf_op jit(solution)/shard_map/ppermute | solution.py:605
  169.9 6.0 %collective-permute-start.23 = (bf16[2,2,56,128]{3,2,1,0:T(8,128)(2,1)S(1)}, bf16[2,2,56,128]{3,2,1,0:T(8,128)(2,1)S(1)}, u32[]{:S(2)}, u32[]{:S(2)}) collective-permute-start(bf16[2,2,56,128]{3,2,1,0:T(8,128)(2,1)S(1)} %fusion.9), channel_id=1, source_target_pairs={{0,8},{1,9},{2,10},{3,11},{4,12},{5,13},{6,14},{7,15},{8,0},{9,1},... | collective-permute-start | bytes 172040 | tf_op jit(solution)/shard_map/ppermute | solution.py:605
  175.9 8.9 %collective-permute-start.26 = (bf16[1,2,56,128]{3,2,1,0:T(8,128)(2,1)S(1)}, bf16[1,2,56,128]{3,2,1,0:T(8,128)(2,1)S(1)}, u32[]{:S(2)}, u32[]{:S(2)}) collective-permute-start(bf16[1,2,56,128]{3,2,1,0:T(8,128)(2,1)S(1)} %dynamic-slice_convert_fusion.7), channel_id=1, source_target_pairs={{0,16},{1,17},{2,18},{3,19},{4,20},{5,21},{6,22},{7,23},{8,24},{9,... | collective-permute-start | bytes 86024 | tf_op jit(solution)/shard_map/ppermute | solution.py:605
  180.1 4.8 %collective-permute-start.24 = (f32[8,800]{1,0:T(8,128)S(1)}, f32[8,800]{1,0:T(8,128)S(1)}, u32[]{:S(2)}, u32[]{:S(2)}) collective-permute-start(f32[8,800]{1,0:T(8,128)S(1)} %add.124), channel_id=1, source_target_pairs={{0,16},{1,17},{2,18},{3,19},{4,20},{5,21},{6,22},{7,23},{8,24},{9,... | collective-permute-start | bytes 76808 | tf_op jit(solution)/shard_map/ppermute | solution.py:605
  180.1 6.4 %collective-permute-start.25 = (bf16[1,2,128,128]{3,2,1,0:T(8,128)(2,1)S(1)}, bf16[1,2,128,128]{3,2,1,0:T(8,128)(2,1)S(1)}, u32[]{:S(2)}, u32[]{:S(2)}) collective-permute-start(bf16[1,2,128,128]{3,2,1,0:T(8,128)(2,1)S(1)} %dynamic-slice_convert_fusion.5), channel_id=1, source_target_pairs={{0,16},{1,17},{2,18},{3,19},{4,20},{5,21},{6,22},{7,23},{8,24},{9,... | collective-permute-start | bytes 196616 | tf_op jit(solution)/shard_map/ppermute | solution.py:605
  (13 other events, 87.9 us)
